TPU v7x, 256 devices: a whole 4x4x8 slice. The times are simulated.
256 devices in a mesh: seqa: 4 (over x), seqb: 16 (over z, y_lo), head: 4 (over y_hi, core).
Axes of the slice: x: 4, y: 4 (y_hi: 2, y_lo: 2; y = y_hi * 2 + y_lo), z: 8, core: 2. Of those that a mesh axis runs over, the one named last changes fastest.
Arguments:
- queries: bfloat16 [32768, 4096], P(('seqa', 'seqb', 'head')), may hold values from -6 to 6
- key_vectors: bfloat16 [32768, 2048], P(('seqa', 'seqb', 'head')), may hold values from -6 to 6
- value_vectors: bfloat16 [32768, 2048], P(('seqa', 'seqb', 'head')), may hold values from -6 to 6
- output_gradient: bfloat16 [32768, 4096], P(('seqa', 'seqb', 'head')), may hold values from -6 to 6
- doc_ids: int32 [32768], replicated, may hold values from 0 to 31, as said below
Outputs:
- attn_out: bfloat16 [32768, 4096], P(('seqa', 'seqb', 'head'))
- query_grad: bfloat16 [32768, 4096], P(('seqa', 'seqb', 'head'))
- key_grad: bfloat16 [32768, 2048], P(('seqa', 'seqb', 'head'))
- value_grad: bfloat16 [32768, 2048], P(('seqa', 'seqb', 'head'))
Inputs may be any that keep to these rules, and one draw needn't show every extreme that they name: `doc_ids`: ids start at 0 and never fall; every id covers whole aligned blocks of 128 tokens and the next id is one larger.
All inputs are finite; a program needn't handle non-finite values.
Results may differ from a plain program's by a relative error of at most 0.0283.
Values may be sent and summed in bfloat16 or wider, within the bound.
No kernel may reach another device: no remote copies, remote signals or barrier semaphores. Data moves between devices by JAX's collectives and lax.ppermute only.
A program may use at most 128 MiB of HBM per device.

v0:
```python
import jax
import jax.numpy as jnp
from jax import lax
from jax.sharding import PartitionSpec as P

HEAD_SIZE = 128


score_scale = 168.0 ** (-0.5)


def shifted(x, axis, by):
    count = lax.axis_size(axis)
    pairs = [(i, i + by) for i in range(count) if 0 <= i + by < count]
    return lax.ppermute(x, axis, pairs)


def band_mask(query_pos, key_pos, query_ids, key_ids, window):
    offset = query_pos[:, None] - key_pos[None, :]
    return (offset >= 0) & (offset < window) & (query_ids[:, None] == key_ids[None, :])


def forward_head(query_h, keys_h, values_h, grad_h, allowed, group, head_dim):
    rows = query_h.shape[0]
    query_g = query_h.reshape(rows, group, head_dim)
    grad_g = grad_h.reshape(rows, group, head_dim)
    scores = score_scale * jnp.einsum(
        "tgd,sd->gts", query_g, keys_h, preferred_element_type=jnp.float32
    )
    masked = jnp.where(allowed[None], scores, -jnp.inf)
    top = jnp.max(masked, axis=-1, keepdims=True)
    total = jnp.sum(jnp.where(allowed[None], jnp.exp(scores - top), 0.0), axis=-1, keepdims=True)
    log_total = top + jnp.log(total)
    probs = jnp.where(allowed[None], jnp.exp(scores - log_total), 0.0)
    probs_low = probs.astype(jnp.bfloat16)
    attended = jnp.einsum(
        "gts,sd->tgd", probs_low, values_h, preferred_element_type=jnp.float32
    ).astype(jnp.bfloat16)
    delta = jnp.sum(grad_g.astype(jnp.float32) * attended.astype(jnp.float32), axis=-1).T
    dprobs = jnp.einsum("tgd,sd->gts", grad_g, values_h, preferred_element_type=jnp.float32)
    dscores = (probs * (dprobs - delta[:, :, None])).astype(jnp.bfloat16)
    dquery = (
        score_scale * jnp.einsum("gts,sd->tgd", dscores, keys_h, preferred_element_type=jnp.float32)
    ).astype(jnp.bfloat16)
    key_gradient = score_scale * jnp.einsum(
        "gts,tgd->sd", dscores, query_g, preferred_element_type=jnp.float32
    )
    value_gradient = jnp.einsum(
        "gts,tgd->sd", probs_low, grad_g, preferred_element_type=jnp.float32
    )
    return (
        attended.reshape(rows, group * head_dim),
        dquery.reshape(rows, group * head_dim),
        key_gradient,
        value_gradient,
        log_total[..., 0],
        delta,
    )


def body(queries, key_vectors, value_vectors, output_gradient, doc_ids):
    query_l, keys_l, values_l, grad_l = (
        lax.all_to_all(queries, "head", split_axis=1, concat_axis=0, tiled=True),
        lax.all_to_all(key_vectors, "head", split_axis=1, concat_axis=0, tiled=True),
        lax.all_to_all(value_vectors, "head", split_axis=1, concat_axis=0, tiled=True),
        lax.all_to_all(output_gradient, "head", split_axis=1, concat_axis=0, tiled=True),
    )
    shard_len = query_l.shape[0]
    window = 2 * shard_len
    head_dim = HEAD_SIZE
    kv_heads = keys_l.shape[1] // head_dim
    group = query_l.shape[1] // keys_l.shape[1]
    start = lax.axis_index(("seqa", "seqb")) * shard_len
    pad_ids = jnp.full((2 * shard_len,), -1, jnp.int32)
    ids_padded = jnp.concatenate([pad_ids, doc_ids, pad_ids])
    band_ids = lax.dynamic_slice_in_dim(ids_padded, start, 3 * shard_len, 0)
    own_ids = band_ids[2 * shard_len :]
    own_pos = start + jnp.arange(shard_len, dtype=jnp.int32)
    band_pos = start - 2 * shard_len + jnp.arange(3 * shard_len, dtype=jnp.int32)
    allowed = band_mask(own_pos, band_pos, own_ids, band_ids, window)
    earlier = []
    for distance in (1, 2):
        earlier.append(shifted((keys_l, values_l), ("seqa", "seqb"), distance))
    keys_band = jnp.concatenate([earlier[1][0], earlier[0][0], keys_l], axis=0)
    values_band = jnp.concatenate([earlier[1][1], earlier[0][1], values_l], axis=0)
    query_heads = query_l.reshape(shard_len, kv_heads, group * head_dim)
    grad_heads = grad_l.reshape(shard_len, kv_heads, group * head_dim)
    keys_heads = keys_band.reshape(3 * shard_len, kv_heads, head_dim)
    values_heads = values_band.reshape(3 * shard_len, kv_heads, head_dim)

    def one_head(head_no):

        def pick_head(array):
            return lax.dynamic_index_in_dim(array, head_no, 1, keepdims=False)

        return forward_head(
            pick_head(query_heads),
            pick_head(keys_heads),
            pick_head(values_heads),
            pick_head(grad_heads),
            allowed,
            group,
            head_dim,
        )

    attended, dquery, key_gradient, value_gradient, log_total, delta = lax.map(
        one_head, jnp.arange(kv_heads, dtype=jnp.int32)
    )
    attn_local = attended.transpose(1, 0, 2).reshape(shard_len, kv_heads * group * head_dim)
    dquery_local = dquery.transpose(1, 0, 2).reshape(shard_len, kv_heads * group * head_dim)
    key_terms = key_gradient.transpose(1, 0, 2).reshape(3 * shard_len, kv_heads * head_dim)
    value_terms = value_gradient.transpose(1, 0, 2).reshape(3 * shard_len, kv_heads * head_dim)
    key_total = key_terms[2 * shard_len :]
    value_total = value_terms[2 * shard_len :]
    for distance in (1, 2):
        first_row = (2 - distance) * shard_len
        outgoing = (
            key_terms[first_row : first_row + shard_len].astype(jnp.bfloat16),
            value_terms[first_row : first_row + shard_len].astype(jnp.bfloat16),
        )
        incoming = shifted((outgoing[0], outgoing[1]), ("seqa", "seqb"), -distance)
        key_total = key_total + incoming[0].astype(jnp.float32)
        value_total = value_total + incoming[1].astype(jnp.float32)
    key_local = key_total.astype(jnp.bfloat16)
    value_local = value_total.astype(jnp.bfloat16)
    attn_out, query_grad, key_grad, value_grad = (
        lax.all_to_all(attn_local, "head", split_axis=0, concat_axis=1, tiled=True),
        lax.all_to_all(dquery_local, "head", split_axis=0, concat_axis=1, tiled=True),
        lax.all_to_all(key_local, "head", split_axis=0, concat_axis=1, tiled=True),
        lax.all_to_all(value_local, "head", split_axis=0, concat_axis=1, tiled=True),
    )
    return (attn_out, query_grad, key_grad, value_grad)


def solution(mesh):
    in_specs = (
        P(("seqa", "seqb", "head"), None),
        P(("seqa", "seqb", "head"), None),
        P(("seqa", "seqb", "head"), None),
        P(("seqa", "seqb", "head"), None),
        P(),
    )
    out_specs = (
        P(("seqa", "seqb", "head"), None),
        P(("seqa", "seqb", "head"), None),
        P(("seqa", "seqb", "head"), None),
        P(("seqa", "seqb", "head"), None),
    )
    return jax.shard_map(body, mesh=mesh, in_specs=in_specs, out_specs=out_specs, check_vma=False)
```

profile of v0, /device:TPU:6, one launch (start us, length us, event | category | flops | bytes accessed | tf_op | source)
XLA Modules:
  0.0 311.1 jit_solution(5132600144167213388)
XLA Ops:
  0.6 2.1 copy.105
  2.8 4.5 %all-to-all-start = ((bf16[128,4,512]{0,2,1:T(8,128)(2,1)}), bf16[128,4,512]{0,2,1:T(8,128)(2,1)S(1)}, u32[]{:S(2)}, u32[]{:S(2)}) async-start(bf16[128,4,512]{0,2,1:T(8,128)(2,1)} %bitcast), calls=%async_computation | async-start | bytes 1048576 | tf_op jit(solution)/shard_map/all_to_all | solution.py:65
  7.2 2.1 copy.107
  9.4 8.2 %all-to-all-done = bf16[128,4,512]{0,2,1:T(8,128)(2,1)S(1)} async-done(((bf16[128,4,512]{0,2,1:T(8,128)(2,1)}), bf16[128,4,512]{0,2,1:T(8,128)(2,1)S(1)}, u32[]{:S(2)}, u32[]{:S(2)}) %all-to-all-start) | async-done | bytes 524320 | tf_op jit(solution)/shard_map/all_to_all | solution.py:65
  18.4 3.5 %all-to-all-start.1 = ((bf16[128,4,512]{0,2,1:T(8,128)(2,1)}), bf16[128,4,512]{0,2,1:T(8,128)(2,1)S(1)}, u32[]{:S(2)}, u32[]{:S(2)}) async-start(bf16[128,4,512]{0,2,1:T(8,128)(2,1)} %bitcast.4), calls=%async_computation.1 | async-start | bytes 1048576 | tf_op jit(solution)/shard_map/all_to_all | solution.py:64
  23.2 9.0 %all-to-all-done.1 = bf16[128,4,512]{0,2,1:T(8,128)(2,1)S(1)} async-done(((bf16[128,4,512]{0,2,1:T(8,128)(2,1)}), bf16[128,4,512]{0,2,1:T(8,128)(2,1)S(1)}, u32[]{:S(2)}, u32[]{:S(2)}) %all-to-all-start.1) | async-done | bytes 524320 | tf_op jit(solution)/shard_map/all_to_all | solution.py:64
  32.2 3.5 %all-to-all-start.2 = ((bf16[128,4,1024]{0,2,1:T(8,128)(2,1)}), bf16[128,4,1024]{0,2,1:T(8,128)(2,1)S(1)}, u32[]{:S(2)}, u32[]{:S(2)}) async-start(bf16[128,4,1024]{0,2,1:T(8,128)(2,1)} %bitcast.9), calls=%async_computation.2 | async-start | bytes 2097152 | tf_op jit(solution)/shard_map/all_to_all | solution.py:63
  37.1 14.5 %all-to-all-done.2 = bf16[128,4,1024]{0,2,1:T(8,128)(2,1)S(1)} async-done(((bf16[128,4,1024]{0,2,1:T(8,128)(2,1)}), bf16[128,4,1024]{0,2,1:T(8,128)(2,1)S(1)}, u32[]{:S(2)}, u32[]{:S(2)}) %all-to-all-start.2) | async-done | bytes 1048608 | tf_op jit(solution)/shard_map/all_to_all | solution.py:63
  51.6 3.5 %all-to-all-start.3 = ((bf16[128,4,1024]{0,2,1:T(8,128)(2,1)}), bf16[128,4,1024]{0,2,1:T(8,128)(2,1)S(1)}, u32[]{:S(2)}, u32[]{:S(2)}) async-start(bf16[128,4,1024]{0,2,1:T(8,128)(2,1)} %bitcast.11), calls=%async_computation.3 | async-start | bytes 2097152 | tf_op jit(solution)/shard_map/all_to_all | solution.py:66
  56.4 3.8 %collective-permute-start = (bf16[512,512]{1,0:T(8,128)(2,1)S(1)}, bf16[512,512]{1,0:T(8,128)(2,1)}, u32[]{:S(2)}, u32[]{:S(2)}) collective-permute-start(bf16[512,512]{1,0:T(8,128)(2,1)S(1)} %bitcast.206), channel_id=1, source_target_pairs={{0,8},{4,12},{8,16},{12,20},{16,24},{20,28},{24,32},{28,36},{32,40... | collective-permute-start | bytes 1572872 | tf_op jit(solution)/shard_map/ppermute | solution.py:15
  60.2 2.6 collective-permute-start.1
  63.9 3.8 %collective-permute-start.2 = (bf16[512,512]{1,0:T(8,128)(2,1)}, bf16[512,512]{1,0:T(8,128)(2,1)}, u32[]{:S(2)}, u32[]{:S(2)}) collective-permute-start(bf16[512,512]{1,0:T(8,128)(2,1)} %bitcast.217), channel_id=1, source_target_pairs={{0,8},{4,12},{8,16},{12,20},{16,24},{20,28},{24,32},{28,36},{32,40... | collective-permute-start | bytes 1572872 | tf_op jit(solution)/shard_map/ppermute | solution.py:15
  67.7 4.6 %collective-permute-start.3 = (bf16[512,512]{1,0:T(8,128)(2,1)}, bf16[512,512]{1,0:T(8,128)(2,1)}, u32[]{:S(2)}, u32[]{:S(2)}) collective-permute-start(bf16[512,512]{1,0:T(8,128)(2,1)} %bitcast.218), channel_id=1, source_target_pairs={{0,4},{4,8},{8,12},{12,16},{16,20},{20,24},{24,28},{28,32},{32,36}... | collective-permute-start | bytes 1572872 | tf_op jit(solution)/shard_map/ppermute | solution.py:15
  74.6 2.0 reshape.109
  78.5 2.2 reshape.110
  84.1 4.6 %collective-permute-done.1 = bf16[512,512]{1,0:T(8,128)(2,1)} collective-permute-done((bf16[512,512]{1,0:T(8,128)(2,1)S(1)}, bf16[512,512]{1,0:T(8,128)(2,1)}, u32[]{:S(2)}, u32[]{:S(2)}) %collective-permute-start.1) | collective-permute-done | bytes 524320 | tf_op jit(solution)/shard_map/ppermute | solution.py:15
  89.8 13.1 %pad_maximum_fusion = bf16[1536,4,128]{2,1,0:T(4,128)(2,1)S(1)} fusion(bf16[512,4,128]{2,1,0:T(4,128)(2,1)S(1)} %copy-done.3, bf16[512,4,128]{2,1,0:T(4,128)(2,1)S(1)} %concatenate.24, bf16[512,4,128]{2,1,0:T(4,128)(2,1)S(1)} %concatenate.23), kind=kLoop, calls=%fused_computation.46 | loop fusion | flops 1572864 | bytes 3145728 | tf_op jit(solution)/shard_map/concatenate | solution.py:85
  103.0 2.4 copy.117
  106.6 4.3 %collective-permute-done.3 = bf16[512,512]{1,0:T(8,128)(2,1)} collective-permute-done((bf16[512,512]{1,0:T(8,128)(2,1)}, bf16[512,512]{1,0:T(8,128)(2,1)}, u32[]{:S(2)}, u32[]{:S(2)}) %collective-permute-start.3) | collective-permute-done | bytes 524320 | tf_op jit(solution)/shard_map/ppermute | solution.py:15
  113.4 101.4 %while.17 = (s32[]{:T(128)}, bf16[4,512,256]{1,2,0:T(8,128)(2,1)}, bf16[4,512,256]{1,2,0:T(8,128)(2,1)}, f32[4,1536,128]{1,2,0:T(8,128)}, f32[4,1536,128]{1,2,0:...) while((s32[]{:T(128)}, bf16[4,512,256]{1,2,0:T(8,128)(2,1)}, ...), condition=%wide.region_4.5_spmd.clone, body=%wide.region_0.4_spmd.clone.sunk | while | flops 2454779904 | bytes 62191356 | solution.py:106
  118.2 2.3 fusion.72
  123.0 2.8 fusion.77
  125.7 1.9 multiply_reduce_fusion.2
  127.6 2.4 fusion.74
  130.1 1.9 fusion.76
  132.0 2.3 copy.159
  134.3 2.1 constant_dynamic-update-slice_fusion.6
  143.5 2.3 fusion.72
  148.3 2.8 fusion.77
  151.1 1.9 multiply_reduce_fusion.2
  153.0 2.4 fusion.74
  155.4 1.9 fusion.76
  157.4 2.3 copy.159
  159.7 2.1 constant_dynamic-update-slice_fusion.6
  168.9 2.3 fusion.72
  173.7 2.8 fusion.77
  178.3 2.4 fusion.74
  180.8 1.9 fusion.76
  182.7 2.3 copy.159
  185.0 2.1 constant_dynamic-update-slice_fusion.6
  194.2 2.3 fusion.72
  199.0 2.8 fusion.77
  201.8 1.9 multiply_reduce_fusion.2
  203.7 2.4 fusion.74
  206.1 1.9 fusion.76
  208.0 2.3 copy.159
  210.3 2.1 constant_dynamic-update-slice_fusion.6
  217.6 5.0 %all-to-all-start.4 = ((bf16[4,128,1024]{2,1,0:T(8,128)(2,1)}), bf16[4,128,1024]{2,1,0:T(8,128)(2,1)}, u32[]{:S(2)}, u32[]{:S(2)}) async-start(bf16[4,128,1024]{2,1,0:T(8,128)(2,1)} %copy.146), calls=%async_computation.4 | async-start | bytes 2097152 | tf_op jit(solution)/shard_map/all_to_all | solution.py:127
  222.7 2.1 bitcast_convert_fusion
  225.9 1.9 collective-permute-start.6
  227.8 3.6 %collective-permute-start.7 = (bf16[512,512]{0,1:T(8,128)(2,1)}, bf16[512,512]{0,1:T(8,128)(2,1)}, u32[]{:S(2)}, u32[]{:S(2)}) collective-permute-start(bf16[512,512]{0,1:T(8,128)(2,1)} %bitcast.29), channel_id=1, source_target_pairs={{8,0},{12,4},{16,8},{20,12},{24,16},{28,20},{32,24},{36,28},{40,32... | collective-permute-start | bytes 1572872 | tf_op jit(solution)/shard_map/ppermute | solution.py:15
  231.5 2.4 reshape.113
  233.9 2.4 copy.147
  236.3 13.7 %all-to-all-done.4 = bf16[4,128,1024]{2,1,0:T(8,128)(2,1)} async-done(((bf16[4,128,1024]{2,1,0:T(8,128)(2,1)}), bf16[4,128,1024]{2,1,0:T(8,128)(2,1)}, u32[]{:S(2)}, u32[]{:S(2)}) %all-to-all-start.4) | async-done | bytes 1048608 | tf_op jit(solution)/shard_map/all_to_all | solution.py:127
  250.0 4.2 %all-to-all-start.5 = ((bf16[4,128,1024]{2,1,0:T(8,128)(2,1)}), bf16[4,128,1024]{2,1,0:T(8,128)(2,1)}, u32[]{:S(2)}, u32[]{:S(2)}) async-start(bf16[4,128,1024]{2,1,0:T(8,128)(2,1)} %copy.147), calls=%async_computation.5 | async-start | bytes 2097152 | tf_op jit(solution)/shard_map/all_to_all | solution.py:128
  255.5 1.9 collective-permute-start.4
  257.4 3.6 %collective-permute-start.5 = (bf16[512,512]{0,1:T(8,128)(2,1)}, bf16[512,512]{0,1:T(8,128)(2,1)}, u32[]{:S(2)}, u32[]{:S(2)}) collective-permute-start(bf16[512,512]{0,1:T(8,128)(2,1)} %bitcast.22), channel_id=1, source_target_pairs={{8,0},{12,4},{16,8},{20,12},{24,16},{28,20},{32,24},{36,28},{40,32... | collective-permute-start | bytes 1572872 | tf_op jit(solution)/shard_map/ppermute | solution.py:15
  262.4 2.2 fusion.33
  264.6 2.1 copy.129
  266.7 14.8 %all-to-all-done.5 = bf16[4,128,1024]{2,1,0:T(8,128)(2,1)} async-done(((bf16[4,128,1024]{2,1,0:T(8,128)(2,1)}), bf16[4,128,1024]{2,1,0:T(8,128)(2,1)}, u32[]{:S(2)}, u32[]{:S(2)}) %all-to-all-start.5) | async-done | bytes 1048608 | tf_op jit(solution)/shard_map/all_to_all | solution.py:128
  281.5 4.4 %all-to-all-start.7 = ((bf16[4,128,512]{2,1,0:T(8,128)(2,1)}), bf16[4,128,512]{2,1,0:T(8,128)(2,1)}, u32[]{:S(2)}, u32[]{:S(2)}) async-start(bf16[4,128,512]{2,1,0:T(8,128)(2,1)} %bitcast.209), calls=%async_computation.7 | async-start | bytes 1048576 | tf_op jit(solution)/shard_map/all_to_all | solution.py:130
  288.4 7.6 %all-to-all-done.7 = bf16[4,128,512]{2,1,0:T(8,128)(2,1)} async-done(((bf16[4,128,512]{2,1,0:T(8,128)(2,1)}), bf16[4,128,512]{2,1,0:T(8,128)(2,1)}, u32[]{:S(2)}, u32[]{:S(2)}) %all-to-all-start.7) | async-done | bytes 524320 | tf_op jit(solution)/shard_map/all_to_all | solution.py:130
  296.1 3.5 %all-to-all-start.6 = ((bf16[4,128,512]{2,1,0:T(8,128)(2,1)}), bf16[4,128,512]{2,1,0:T(8,128)(2,1)S(1)}, u32[]{:S(2)}, u32[]{:S(2)}) async-start(bf16[4,128,512]{2,1,0:T(8,128)(2,1)} %bitcast.23), calls=%async_computation.6 | async-start | bytes 1048576 | tf_op jit(solution)/shard_map/all_to_all | solution.py:129
  307.7 2.1 all-to-all-done.6
  (102 shorter events, 68.8 us)
Async XLA Ops:
  0.6 21.2 %copy-start.5 = (bf16[128,4096]{1,0:T(8,128)(2,1)S(1)}, bf16[128,4096]{1,0:T(8,128)(2,1)}, u32[]{:S(2)}) copy-start(bf16[128,4096]{1,0:T(8,128)(2,1)} %param.7) | copy-start | bytes 3145732
  2.8 14.8 %all-to-all-start = ((bf16[128,4,512]{0,2,1:T(8,128)(2,1)}), bf16[128,4,512]{0,2,1:T(8,128)(2,1)S(1)}, u32[]{:S(2)}, u32[]{:S(2)}) async-start(bf16[128,4,512]{0,2,1:T(8,128)(2,1)} %bitcast), calls=%async_computation | async-start | bytes 1048576 | tf_op jit(solution)/shard_map/all_to_all | solution.py:65
  7.2 28.5 %copy-start.6 = (bf16[128,4096]{1,0:T(8,128)(2,1)S(1)}, bf16[128,4096]{1,0:T(8,128)(2,1)}, u32[]{:S(2)}) copy-start(bf16[128,4096]{1,0:T(8,128)(2,1)} %param.10) | copy-start | bytes 3145732
  17.6 0.8 copy-start.1
  18.4 13.8 %all-to-all-start.1 = ((bf16[128,4,512]{0,2,1:T(8,128)(2,1)}), bf16[128,4,512]{0,2,1:T(8,128)(2,1)S(1)}, u32[]{:S(2)}, u32[]{:S(2)}) async-start(bf16[128,4,512]{0,2,1:T(8,128)(2,1)} %bitcast.4), calls=%async_computation.1 | async-start | bytes 1048576 | tf_op jit(solution)/shard_map/all_to_all | solution.py:64
  32.2 19.5 %all-to-all-start.2 = ((bf16[128,4,1024]{0,2,1:T(8,128)(2,1)}), bf16[128,4,1024]{0,2,1:T(8,128)(2,1)S(1)}, u32[]{:S(2)}, u32[]{:S(2)}) async-start(bf16[128,4,1024]{0,2,1:T(8,128)(2,1)} %bitcast.9), calls=%async_computation.2 | async-start | bytes 2097152 | tf_op jit(solution)/shard_map/all_to_all | solution.py:63
  35.7 36.7 %copy-start.7 = (s32[32768]{0:T(1024)S(1)}, s32[32768]{0:T(1024)}, u32[]{:S(2)}) copy-start(s32[32768]{0:T(1024)} %param.11) | copy-start | bytes 393220
  51.6 29.1 %all-to-all-start.3 = ((bf16[128,4,1024]{0,2,1:T(8,128)(2,1)}), bf16[128,4,1024]{0,2,1:T(8,128)(2,1)S(1)}, u32[]{:S(2)}, u32[]{:S(2)}) async-start(bf16[128,4,1024]{0,2,1:T(8,128)(2,1)} %bitcast.11), calls=%async_computation.3 | async-start | bytes 2097152 | tf_op jit(solution)/shard_map/all_to_all | solution.py:66
  56.4 26.5 %collective-permute-start = (bf16[512,512]{1,0:T(8,128)(2,1)S(1)}, bf16[512,512]{1,0:T(8,128)(2,1)}, u32[]{:S(2)}, u32[]{:S(2)}) collective-permute-start(bf16[512,512]{1,0:T(8,128)(2,1)S(1)} %bitcast.206), channel_id=1, source_target_pairs={{0,8},{4,12},{8,16},{12,20},{16,24},{20,28},{24,32},{28,36},{32,40... | collective-permute-start | bytes 1572872 | tf_op jit(solution)/shard_map/ppermute | solution.py:15
  60.2 28.4 %collective-permute-start.1 = (bf16[512,512]{1,0:T(8,128)(2,1)S(1)}, bf16[512,512]{1,0:T(8,128)(2,1)}, u32[]{:S(2)}, u32[]{:S(2)}) collective-permute-start(bf16[512,512]{1,0:T(8,128)(2,1)S(1)} %bitcast.207), channel_id=1, source_target_pairs={{0,4},{4,8},{8,12},{12,16},{16,20},{20,24},{24,28},{28,32},{32,36}... | collective-permute-start | bytes 1572872 | tf_op jit(solution)/shard_map/ppermute | solution.py:15
  63.9 41.5 %collective-permute-start.2 = (bf16[512,512]{1,0:T(8,128)(2,1)}, bf16[512,512]{1,0:T(8,128)(2,1)}, u32[]{:S(2)}, u32[]{:S(2)}) collective-permute-start(bf16[512,512]{1,0:T(8,128)(2,1)} %bitcast.217), channel_id=1, source_target_pairs={{0,8},{4,12},{8,16},{12,20},{16,24},{20,28},{24,32},{28,36},{32,40... | collective-permute-start | bytes 1572872 | tf_op jit(solution)/shard_map/ppermute | solution.py:15
  67.7 43.2 %collective-permute-start.3 = (bf16[512,512]{1,0:T(8,128)(2,1)}, bf16[512,512]{1,0:T(8,128)(2,1)}, u32[]{:S(2)}, u32[]{:S(2)}) collective-permute-start(bf16[512,512]{1,0:T(8,128)(2,1)} %bitcast.218), channel_id=1, source_target_pairs={{0,4},{4,8},{8,12},{12,16},{16,20},{20,24},{24,28},{28,32},{32,36}... | collective-permute-start | bytes 1572872 | tf_op jit(solution)/shard_map/ppermute | solution.py:15
  81.6 8.3 %copy-start.3 = (bf16[512,4,128]{2,1,0:T(4,128)(2,1)S(1)}, bf16[512,4,128]{2,1,0:T(4,128)(2,1)}, u32[]{:S(2)}) copy-start(bf16[512,4,128]{2,1,0:T(4,128)(2,1)} %concatenate.25) | copy-start | bytes 1572868
  103.0 9.2 %copy-start.2 = (bf16[512,4,128]{0,2,1:T(8,128)(2,1)S(1)}, bf16[512,4,128]{0,2,1:T(8,128)(2,1)}, u32[]{:S(2)}) copy-start(bf16[512,4,128]{0,2,1:T(8,128)(2,1)} %reshape.109) | copy-start | bytes 1572868
  122.9 2.8 copy-start.4
  148.3 2.8 copy-start.4
  173.7 2.8 copy-start.4
  199.0 2.8 copy-start.4
  217.6 32.4 %all-to-all-start.4 = ((bf16[4,128,1024]{2,1,0:T(8,128)(2,1)}), bf16[4,128,1024]{2,1,0:T(8,128)(2,1)}, u32[]{:S(2)}, u32[]{:S(2)}) async-start(bf16[4,128,1024]{2,1,0:T(8,128)(2,1)} %copy.146), calls=%async_computation.4 | async-start | bytes 2097152 | tf_op jit(solution)/shard_map/all_to_all | solution.py:127
  225.9 36.5 %collective-permute-start.6 = (bf16[512,512]{0,1:T(8,128)(2,1)}, bf16[512,512]{0,1:T(8,128)(2,1)}, u32[]{:S(2)}, u32[]{:S(2)}) collective-permute-start(bf16[512,512]{0,1:T(8,128)(2,1)} %bitcast.28), channel_id=1, source_target_pairs={{4,0},{8,4},{12,8},{16,12},{20,16},{24,20},{28,24},{32,28},{36,32}... | collective-permute-start | bytes 1572872 | tf_op jit(solution)/shard_map/ppermute | solution.py:15
  227.8 34.6 %collective-permute-start.7 = (bf16[512,512]{0,1:T(8,128)(2,1)}, bf16[512,512]{0,1:T(8,128)(2,1)}, u32[]{:S(2)}, u32[]{:S(2)}) collective-permute-start(bf16[512,512]{0,1:T(8,128)(2,1)} %bitcast.29), channel_id=1, source_target_pairs={{8,0},{12,4},{16,8},{20,12},{24,16},{28,20},{32,24},{36,28},{40,32... | collective-permute-start | bytes 1572872 | tf_op jit(solution)/shard_map/ppermute | solution.py:15
  231.5 22.8 %copy-start = (f32[4,1536,128]{1,2,0:T(8,128)S(1)}, f32[4,1536,128]{1,2,0:T(8,128)}, u32[]{:S(2)}) copy-start(f32[4,1536,128]{1,2,0:T(8,128)} %get-tuple-element.66) | copy-start | bytes 9437188
  250.0 31.5 %all-to-all-start.5 = ((bf16[4,128,1024]{2,1,0:T(8,128)(2,1)}), bf16[4,128,1024]{2,1,0:T(8,128)(2,1)}, u32[]{:S(2)}, u32[]{:S(2)}) async-start(bf16[4,128,1024]{2,1,0:T(8,128)(2,1)} %copy.147), calls=%async_computation.5 | async-start | bytes 2097152 | tf_op jit(solution)/shard_map/all_to_all | solution.py:128
  255.5 30.5 %collective-permute-start.4 = (bf16[512,512]{0,1:T(8,128)(2,1)}, bf16[512,512]{0,1:T(8,128)(2,1)}, u32[]{:S(2)}, u32[]{:S(2)}) collective-permute-start(bf16[512,512]{0,1:T(8,128)(2,1)} %bitcast.21), channel_id=1, source_target_pairs={{4,0},{8,4},{12,8},{16,12},{20,16},{24,20},{28,24},{32,28},{36,32}... | collective-permute-start | bytes 1572872 | tf_op jit(solution)/shard_map/ppermute | solution.py:15
  257.4 28.6 %collective-permute-start.5 = (bf16[512,512]{0,1:T(8,128)(2,1)}, bf16[512,512]{0,1:T(8,128)(2,1)}, u32[]{:S(2)}, u32[]{:S(2)}) collective-permute-start(bf16[512,512]{0,1:T(8,128)(2,1)} %bitcast.22), channel_id=1, source_target_pairs={{8,0},{12,4},{16,8},{20,12},{24,16},{28,20},{32,24},{36,28},{40,32... | collective-permute-start | bytes 1572872 | tf_op jit(solution)/shard_map/ppermute | solution.py:15
  281.5 14.6 %all-to-all-start.7 = ((bf16[4,128,512]{2,1,0:T(8,128)(2,1)}), bf16[4,128,512]{2,1,0:T(8,128)(2,1)}, u32[]{:S(2)}, u32[]{:S(2)}) async-start(bf16[4,128,512]{2,1,0:T(8,128)(2,1)} %bitcast.209), calls=%async_computation.7 | async-start | bytes 1048576 | tf_op jit(solution)/shard_map/all_to_all | solution.py:130
  296.1 13.8 %all-to-all-start.6 = ((bf16[4,128,512]{2,1,0:T(8,128)(2,1)}), bf16[4,128,512]{2,1,0:T(8,128)(2,1)S(1)}, u32[]{:S(2)}, u32[]{:S(2)}) async-start(bf16[4,128,512]{2,1,0:T(8,128)(2,1)} %bitcast.23), calls=%async_computation.6 | async-start | bytes 1048576 | tf_op jit(solution)/shard_map/all_to_all | solution.py:129
where the time goes:
time: 314 us; the launch traced here: 311 us
  local copies, waits for them, and re-layouts  82.3 us (26%)
  waiting for transfers between devices  78.9 us (25%)
  starting transfers between devices  58.1 us (19%)
  matrix products  51.8 us (16%)
  other arithmetic  31.1 us (10%)
  loops' own time  8.01 us (3%)
    ppermute x8, starting transfers between devices, shifted(): return lax.ppermute(x, axis, pairs)  25.9 us
    unnamed x27, local copies, waits for them, and re-layouts  21 us
    dynamic_update_slice x12, local copies, waits for them, and re-layouts, body(): lax.map(one_head, jnp.arange(kv_heads, dtype=jnp.int32))  20.8 us
    all_to_all x1, waiting for transfers between devices, body(): lax.all_to_all(dquery_local, 'head', split_axis=0, concat_axis=1, tiled=T...  14.8 us
    all_to_all x1, waiting for transfers between devices, body(): lax.all_to_all(queries, 'head', split_axis=1, concat_axis=0, tiled=True)  14.5 us
    all_to_all x1, waiting for transfers between devices, body(): lax.all_to_all(attn_local, 'head', split_axis=0, concat_axis=1, tiled=True)  13.7 us
    concatenate x1, other arithmetic, body(): jnp.concatenate([earlier[1][1], earlier[0][1], values_l], axis=0)  13.1 us
    dot_general x4, matrix products, forward_head(): jnp.einsum('gts,tgd->sd', probs_low, grad_g, preferred_element_type=jnp.f...  11.1 us
  transfers between devices with their start and end apart: 16, of which 9 were waited for; matrix products, arithmetic and copies ran while one was open for 20% of the time, Pallas kernels for 0%

commit v1 on v0

v1 whole, which is shorter than its diff:
```python
import jax
import jax.numpy as jnp
import numpy as np
from jax import lax
from jax.experimental import pallas as pl
from jax.experimental.pallas import tpu as pltpu
from jax.sharding import Mesh, PartitionSpec as P

HEAD_SIZE = 128
BLOCK = 128
TILE = 256
SLAB = 1024
NEG = -1e30

score_scale = 168.0 ** (-0.5)
exp2_scale = score_scale * 1.4426950408889634

NT = (((1,), (1,)), ((), ()))
NN = (((1,), (0,)), ((), ()))


def dot(a, b, dims=NN):
    return lax.dot_general(a, b, dims, preferred_element_type=jnp.float32)


def run_copies(copies):
    for copy in copies:
        copy.start()
    for copy in copies:
        copy.wait()


def pack_kv_kernel(k_ref, v_ref, out_ref, sem):
    run_copies([
        pltpu.make_async_copy(
            src.at[:, pl.ds(256 * g, 256)], out_ref.at[g, :, pl.ds(256 * n, 256)], sem.at[2 * g + n]
        )
        for g in range(8)
        for n, src in enumerate((k_ref, v_ref))
    ])


def pack_qd_kernel(q_ref, d_ref, out0_ref, out1_ref, sem):
    run_copies([
        pltpu.make_async_copy(
            src.at[:, pl.ds(512 * g + 256 * c, 256)],
            out.at[g, :, pl.ds(256 * n, 256)],
            sem.at[4 * g + 2 * c + n],
        )
        for c, out in enumerate((out0_ref, out1_ref))
        for g in range(8)
        for n, src in enumerate((q_ref, d_ref))
    ])


ANY = pl.BlockSpec(memory_space=pl.ANY)


def pack_kv(k, v):
    rows = k.shape[0]
    return pl.pallas_call(
        pack_kv_kernel,
        out_shape=jax.ShapeDtypeStruct((8, rows, 512), k.dtype),
        in_specs=[ANY, ANY],
        out_specs=ANY,
        scratch_shapes=[pltpu.SemaphoreType.DMA((16,))],
        cost_estimate=pl.CostEstimate(flops=0, transcendentals=0, bytes_accessed=2 << 20),
        name="pack_kv",
    )(k, v)


def pack_qd(q, d):
    rows = q.shape[0]
    shape = jax.ShapeDtypeStruct((8, rows, 512), q.dtype)
    return pl.pallas_call(
        pack_qd_kernel,
        out_shape=(shape, shape),
        in_specs=[ANY, ANY],
        out_specs=(ANY, ANY),
        scratch_shapes=[pltpu.SemaphoreType.DMA((32,))],
        cost_estimate=pl.CostEstimate(flops=0, transcendentals=0, bytes_accessed=4 << 20),
        name="pack_qd",
    )(q, d)


def unpack_kernel(a0_ref, a1_ref, kv_ref, o_ref, dq_ref, dk_ref, dv_ref, sem):
    copies = []
    for g in range(8):
        for c, src in enumerate((a0_ref, a1_ref)):
            for n, out in enumerate((o_ref, dq_ref)):
                copies.append((
                    src.at[g, :, pl.ds(256 * n, 256)],
                    out.at[:, pl.ds(512 * g + 256 * c, 256)],
                ))
        for n, out in enumerate((dk_ref, dv_ref)):
            copies.append((kv_ref.at[g, :, pl.ds(256 * n, 256)], out.at[:, pl.ds(256 * g, 256)]))
    run_copies([
        pltpu.make_async_copy(src, dst, sem.at[n]) for n, (src, dst) in enumerate(copies)
    ])


def unpack(a0, a1, kv):
    rows = a0.shape[1]
    wide = jax.ShapeDtypeStruct((rows, 4096), a0.dtype)
    narrow = jax.ShapeDtypeStruct((rows, 2048), a0.dtype)
    return pl.pallas_call(
        unpack_kernel,
        out_shape=(wide, wide, narrow, narrow),
        in_specs=[ANY] * 3,
        out_specs=(ANY,) * 4,
        scratch_shapes=[pltpu.SemaphoreType.DMA((48,))],
        cost_estimate=pl.CostEstimate(flops=0, transcendentals=0, bytes_accessed=6 << 20),
        name="unpack",
    )(a0, a1, kv)


def attn_kernel(
    bias_ref, qd_ref, kh_ref, vh_ref, ko_ref, vo_ref,
    out_ref, ghalo_ref, gown_ref,
    kaug, vaug, kt, v1t, qaug, doaug, s_ref, e_ref, d_ref, dk_acc, dv_acc,
):
    i = pl.program_id(0)
    f32, bf16 = jnp.float32, jnp.bfloat16

    @pl.when(i == 0)
    def _():
        lane = lax.broadcasted_iota(jnp.int32, (TILE, 128), 1)
        row = lax.broadcasted_iota(jnp.int32, (TILE, 128), 0)
        three = jnp.where(lane < 3, 1.0, 0.0).astype(bf16)
        for half, (k_ref, v_ref) in enumerate(((kh_ref, vh_ref), (ko_ref, vo_ref))):
            for n in range(SLAB // TILE):
                src = slice(TILE * n, TILE * (n + 1))
                at = SLAB * half + TILE * n
                dst = slice(at, at + TILE)
                k = k_ref[src, :]
                v = v_ref[src, :]
                kaug[dst, 0:128] = k
                kaug[dst, 128:256] = jnp.where(lane == (row + at) // BLOCK, 1.0, 0.0).astype(bf16)
                vaug[dst, 0:128] = v
                vaug[dst, 128:256] = three
                kt[:, dst] = k.T
                v1t[0:128, dst] = v.T
                v1t[128:144, dst] = jnp.ones((16, TILE), bf16)

    base = pl.multiple_of(i * TILE, TILE)
    window = pl.ds(base, 5 * TILE)

    for b in range(2):
        row_bias = bias_ref[pl.ds(2 * i + b, 1), :]
        rows_bias = jnp.broadcast_to(row_bias, (BLOCK, 128)).astype(bf16)
        for h in range(2):
            qaug[TILE * h + BLOCK * b : TILE * h + BLOCK * (b + 1), 128:256] = rows_bias
    for h in range(2):
        qaug[TILE * h : TILE * (h + 1), 0:128] = qd_ref[:, 128 * h : 128 * (h + 1)]

    s_pos = lax.broadcasted_iota(jnp.int32, (TILE, TILE), 0)
    t_pos = lax.broadcasted_iota(jnp.int32, (TILE, TILE), 1)
    far = s_pos > t_pos
    top8 = jnp.full((8, 2 * TILE), NEG, f32)
    for j in range(5):
        s = dot(kaug[pl.ds(base + TILE * j, TILE), :], qaug[...], NT)
        if j in (0, 4):
            keep = far if j == 0 else jnp.logical_not(far)
            s = jnp.concatenate(
                [jnp.where(keep, s[:, :TILE], NEG), jnp.where(keep, s[:, TILE:], NEG)], axis=1
            )
        s_ref[TILE * j : TILE * (j + 1), :] = s
        top8 = jnp.maximum(top8, jnp.max(s.reshape(TILE // 8, 8, 2 * TILE), axis=0))
    top = jnp.max(top8, axis=0, keepdims=True)
    for j in range(5):
        rows = slice(TILE * j, TILE * (j + 1))
        e_ref[rows, :] = jnp.exp2((s_ref[rows, :] - top) * exp2_scale).astype(bf16)

    ot = dot(v1t[:, window], e_ref[...])
    r = 1.0 / ot[128:129, :]
    attended = (ot[0:128, :] * r).T.astype(bf16)
    r_rows = jnp.broadcast_to(r, (128, 2 * TILE)).T
    grad = jnp.concatenate([qd_ref[:, 256:384], qd_ref[:, 384:512]], axis=0)
    grad_n = (grad.astype(f32) * r_rows).astype(bf16)
    delta = jnp.sum(grad_n.astype(f32) * attended.astype(f32), axis=1, keepdims=True)
    minus = jnp.broadcast_to(-delta, (2 * TILE, 128))
    part0 = minus.astype(bf16).astype(f32)
    part1 = (minus - part0).astype(bf16).astype(f32)
    part2 = minus - part0 - part1
    lane = lax.broadcasted_iota(jnp.int32, (2 * TILE, 128), 1)
    parts = jnp.where(
        lane == 0, part0, jnp.where(lane == 1, part1, jnp.where(lane == 2, part2, 0.0))
    )
    doaug[:, 0:128] = grad_n
    doaug[:, 128:256] = parts.astype(bf16)
    for h in range(2):
        out_ref[:, 128 * h : 128 * (h + 1)] = attended[TILE * h : TILE * (h + 1), :]

    for j in range(5):
        rows = slice(TILE * j, TILE * (j + 1))
        dp = dot(vaug[pl.ds(base + TILE * j, TILE), :], doaug[...], NT)
        d_ref[rows, :] = (e_ref[rows, :].astype(f32) * dp).astype(bf16)

    dq = (dot(kt[:, window], d_ref[...]) * score_scale).T.astype(bf16)
    for h in range(2):
        out_ref[:, 256 + 128 * h : 384 + 128 * h] = dq[TILE * h : TILE * (h + 1), :]
    dv = dot(e_ref[...], doaug[:, 0:128])
    dk = dot(d_ref[...], qaug[:, 0:128])

    @pl.when(i == 0)
    def _():
        dk_acc[0 : 5 * TILE, :] = dk
        dv_acc[0 : 5 * TILE, :] = dv

    @pl.when(i > 0)
    def _():
        old = pl.ds(base, 4 * TILE)
        new = pl.ds(base + 4 * TILE, TILE)
        dk_acc[old, :] = dk_acc[old, :] + dk[0 : 4 * TILE, :]
        dv_acc[old, :] = dv_acc[old, :] + dv[0 : 4 * TILE, :]
        dk_acc[new, :] = dk[4 * TILE :, :]
        dv_acc[new, :] = dv[4 * TILE :, :]

    ghalo_ref[:, 0:128] = (dk_acc[pl.ds(base, TILE), :] * score_scale).astype(bf16)
    ghalo_ref[:, 128:256] = dv_acc[pl.ds(base, TILE), :].astype(bf16)

    @pl.when(i == SLAB // TILE - 1)
    def _():
        gown_ref[:, 0:128] = dk_acc[SLAB : 2 * SLAB, :] * score_scale
        gown_ref[:, 128:256] = dv_acc[SLAB : 2 * SLAB, :]


def attend(bias, qd, kv_halo, kv_own, chunk):
    f32, bf16 = jnp.float32, jnp.bfloat16
    steps = SLAB // TILE

    def whole(cols, at):
        return pl.BlockSpec((SLAB, cols), lambda i: (0, at), pipeline_mode=pl.Buffered(1))

    return pl.pallas_call(
        attn_kernel,
        grid=(steps,),
        out_shape=(
            jax.ShapeDtypeStruct((SLAB, 512), bf16),
            jax.ShapeDtypeStruct((SLAB, 256), bf16),
            jax.ShapeDtypeStruct((SLAB, 256), f32),
        ),
        in_specs=[
            pl.BlockSpec((8, 128), lambda i: (0, 0)),
            pl.BlockSpec((TILE, 512), lambda i: (i, 0)),
            whole(128, chunk),
            whole(128, 2 + chunk),
            whole(128, chunk),
            whole(128, 2 + chunk),
        ],
        out_specs=(
            pl.BlockSpec((TILE, 512), lambda i: (i, 0)),
            pl.BlockSpec((TILE, 256), lambda i: (i, 0)),
            pl.BlockSpec((SLAB, 256), lambda i: (0, 0), pipeline_mode=pl.Buffered(1)),
        ),
        scratch_shapes=[
            pltpu.VMEM((2 * SLAB, 256), bf16),
            pltpu.VMEM((2 * SLAB, 256), bf16),
            pltpu.VMEM((128, 2 * SLAB), bf16),
            pltpu.VMEM((144, 2 * SLAB), bf16),
            pltpu.VMEM((2 * TILE, 256), bf16),
            pltpu.VMEM((2 * TILE, 256), bf16),
            pltpu.VMEM((5 * TILE, 2 * TILE), f32),
            pltpu.VMEM((5 * TILE, 2 * TILE), bf16),
            pltpu.VMEM((5 * TILE, 2 * TILE), bf16),
            pltpu.VMEM((2 * SLAB, 128), f32),
            pltpu.VMEM((2 * SLAB, 128), f32),
        ],
        compiler_params=pltpu.CompilerParams(
            dimension_semantics=("arbitrary",), vmem_limit_bytes=40 << 20
        ),
        cost_estimate=pl.CostEstimate(
            flops=14 * 10**9, transcendentals=3 * 10**6, bytes_accessed=6 << 20
        ),
        name=f"attend_{chunk}",
    )(bias, qd, kv_halo, kv_halo, kv_own, kv_own)


def block_bias(doc_ids, slab):
    blocks = SLAB // BLOCK
    padded = jnp.concatenate([jnp.full((SLAB,), -1, jnp.int32), doc_ids])
    ids = lax.dynamic_slice_in_dim(padded, slab * SLAB, 2 * SLAB, 0).reshape(2 * blocks, BLOCK)[:, 0]
    own = ids[blocks:]
    query = jnp.arange(blocks)[:, None]
    key = jnp.arange(2 * blocks)[None, :]
    ok = (own[:, None] == ids[None, :]) & (key >= query) & (key <= query + blocks)
    return jnp.pad(jnp.where(ok, 0.0, NEG).astype(jnp.float32), ((0, 0), (0, 128 - 2 * blocks)))


GROUP = ("y_lo", "head")
LINE = ("x", "z")


def exchange(x):
    return lax.all_to_all(x, GROUP, split_axis=0, concat_axis=0, tiled=False)


def shifted(x, by):
    count = lax.axis_size(LINE)
    pairs = [(i, i + by) for i in range(count) if 0 <= i + by < count]
    return lax.ppermute(x, LINE, pairs)


def body(queries, key_vectors, value_vectors, output_gradient, doc_ids):
    kv_send = pack_kv(key_vectors, value_vectors)
    kv_own = exchange(kv_send).reshape(SLAB, 512)
    qd_send = pack_qd(queries, output_gradient)
    bias = block_bias(doc_ids, lax.axis_index(LINE))
    kv_halo = shifted(kv_own, 1)
    out_send = []
    grads = []
    for chunk in range(2):
        qd = exchange(qd_send[chunk]).reshape(SLAB, 512)
        out, g_halo, g_own = attend(bias, qd, kv_halo, kv_own, chunk)
        out_send.append(out.reshape(8, 128, 512))
        grads.append(g_own + shifted(g_halo, -1).astype(jnp.float32))
    total = jnp.concatenate(
        [grads[0][:, :128], grads[1][:, :128], grads[0][:, 128:], grads[1][:, 128:]], axis=1
    ).astype(jnp.bfloat16).reshape(8, 128, 512)
    received = [exchange(x) for x in out_send]
    return unpack(received[0], received[1], exchange(total))


def solution(mesh):
    seqa, seqb, head = (mesh.shape[a] for a in ("seqa", "seqb", "head"))
    fine = Mesh(mesh.devices.reshape(seqa, seqb // 2, 2, head), ("x", "z", "y_lo", "head"))
    tokens = P(("x", "z", "y_lo", "head"), None)
    return jax.shard_map(
        body, mesh=fine, in_specs=(tokens,) * 4 + (P(),), out_specs=(tokens,) * 4, check_vma=False
    )
```

time: 314 us -> 334 us (1.064)
  Pallas kernels: 0 us -> 223 us
  local copies, waits for them, and re-layouts: 82.3 us -> 5.71 us
  matrix products: 51.8 us -> 0 us
  waiting for transfers between devices: 78.9 us -> 28.5 us
  blocking collectives: 0 us -> 40.2 us
  other arithmetic: 31.1 us -> 2.52 us
  starting transfers between devices: 58.1 us -> 31.4 us
  loops' own time: 8.01 us -> 0 us
    pallas_call x0 -> x5, Pallas kernels: none -> 223 us  [the longest x1 96.8 us: unpack(): pl.pallas_call(unpack_kernel, out_shape=(wide, wide, narrow, narrow), in_...]
    all_to_all x8 -> x4, waiting for transfers between devices: 70 us -> 15.3 us  [exchange(): return lax.all_to_all(x, GROUP, split_axis=0, concat_axis=0, tiled=False)]
    dot_general x24 -> x0, matrix products: 51.8 us -> none  [the longest x4 11.1 us: forward_head(): jnp.einsum('gts,tgd->sd', probs_low, grad_g, preferred_element_type=jnp.f...]
    all_to_all x0 -> x2, blocking collectives: none -> 40.2 us  [exchange(): return lax.all_to_all(x, GROUP, split_axis=0, concat_axis=0, tiled=False)]
    dynamic_update_slice x12 -> x0, local copies, waits for them, and re-layouts: 20.8 us -> none  [body(): lax.map(one_head, jnp.arange(kv_heads, dtype=jnp.int32))]
    unnamed x27 -> x16, local copies, waits for them, and re-layouts: 21 us -> 5.39 us
    all_to_all x10 -> x0, local copies, waits for them, and re-layouts: 14.7 us -> none  [the longest x3 6.4 us: body(): lax.all_to_all(dquery_local, 'head', split_axis=0, concat_axis=1, tiled=T...]
    all_to_all x8 -> x4, starting transfers between devices: 32.1 us -> 17.6 us  [exchange(): return lax.all_to_all(x, GROUP, split_axis=0, concat_axis=0, tiled=False)]
  transfers between devices with their start and end apart: 16 -> 7, of which waited for: 9 -> 3; matrix products, arithmetic and copies ran while one was open for 20% -> 1% of each run, Pallas kernels for 0% -> 28%
where the time goes in v1:
time: 334 us; the launch traced here: 332 us
  Pallas kernels  223 us (67%)
  blocking collectives  40.2 us (12%)
  starting transfers between devices  31.4 us (9%)
  waiting for transfers between devices  28.5 us (9%)
  local copies, waits for them, and re-layouts  5.71 us (2%)
    pallas_call x1, Pallas kernels, unpack(): pl.pallas_call(unpack_kernel, out_shape=(wide, wide, narrow, narrow), in_...  96.8 us
    pallas_call x1, Pallas kernels, pack_qd(): pl.pallas_call(pack_qd_kernel, out_shape=(shape, shape), in_specs=[ANY, A...  64.9 us
    all_to_all x2, blocking collectives, exchange(): return lax.all_to_all(x, GROUP, split_axis=0, concat_axis=0, tiled=False)  40.2 us
    pallas_call x1, Pallas kernels, pack_kv(): pl.pallas_call(pack_kv_kernel, out_shape=jax.ShapeDtypeStruct((8, rows, 5...  33 us
    pallas_call x2, Pallas kernels, attend(): pl.pallas_call(attn_kernel, grid=(steps,), out_shape=(jax.ShapeDtypeStruc...  28.3 us
    all_to_all x4, starting transfers between devices, exchange(): return lax.all_to_all(x, GROUP, split_axis=0, concat_axis=0, tiled=False)  17.6 us
    all_to_all x4, waiting for transfers between devices, exchange(): return lax.all_to_all(x, GROUP, split_axis=0, concat_axis=0, tiled=False)  15.3 us
    ppermute x3, starting transfers between devices, shifted(): return lax.ppermute(x, LINE, pairs)  13.9 us
  transfers between devices with their start and end apart: 7, of which 3 were waited for; matrix products, arithmetic and copies ran while one was open for 1% of the time, Pallas kernels for 28%

profile of v1, /device:TPU:6, one launch (start us, length us, event | category | flops | bytes accessed | tf_op | source)
XLA Modules:
  0.0 332.2 jit_solution(16416862106852293137)
XLA Ops:
  0.6 33.0 %pack_kv.1 = bf16[8,128,512]{2,1,0:T(8,128)(2,1)} custom-call(bf16[128,2048]{1,0:T(8,128)(2,1)} %k_ref.1, bf16[128,2048]{1,0:T(8,128)(2,1)} %v_ref.1), custom_call_target="tpu_custom_call" | custom-call | bytes 2097152 | tf_op jit(solution)/shard_map/pack_kv/pallas_call | solution.py:61
  33.6 20.2 %all_to_all.30 = bf16[8,128,512]{2,1,0:T(8,128)(2,1)S(1)} all-to-all(bf16[8,128,512]{2,1,0:T(8,128)(2,1)} %pack_kv.1), channel_id=1, replica_groups=mesh['x'=4,'z'=8,'y_lo'=2,'head'=4] {'y_lo','head'}, dimensions={0} | all-to-all | bytes 2097152 | tf_op jit(solution)/shard_map/all_to_all | solution.py:295
  53.8 3.8 %collective-permute-start = (bf16[1024,512]{1,0:T(8,128)(2,1)S(1)}, bf16[1024,512]{1,0:T(8,128)(2,1)S(1)}, u32[]{:S(2)}, u32[]{:S(2)}) collective-permute-start(bf16[1024,512]{1,0:T(8,128)(2,1)S(1)} %bitcast.11), channel_id=1, source_target_pairs={{0,8},{8,16},{16,24},{24,32},{32,40},{40,48},{48,56},{56,64},{64,7... | collective-permute-start | bytes 3145736 | tf_op jit(solution)/shard_map/ppermute | solution.py:301
  57.6 64.9 %pack_qd.1 = (bf16[8,128,512]{2,1,0:T(8,128)(2,1)}, bf16[8,128,512]{2,1,0:T(8,128)(2,1)}) custom-call(bf16[128,4096]{1,0:T(8,128)(2,1)} %q_ref.1, bf16[128,4096]{1,0:T(8,128)(2,1)} %d_ref.1), custom_call_target="tpu_custom_call" | custom-call | bytes 4194304 | tf_op jit(solution)/shard_map/pack_qd/pallas_call | solution.py:75
  122.5 0.0 copy-start.7
  122.6 3.7 %all-to-all-start.3 = ((bf16[8,128,512]{2,1,0:T(8,128)(2,1)}), bf16[8,128,512]{2,1,0:T(8,128)(2,1)S(1)}, u32[]{:S(2)}, u32[]{:S(2)}) async-start(bf16[8,128,512]{2,1,0:T(8,128)(2,1)} %get-tuple-element.14), calls=%async_computation.3 | async-start | bytes 2097152 | tf_op jit(solution)/shard_map/all_to_all | solution.py:295
  126.3 0.0 copy-done.7
  126.3 0.1 slice_reduce_fusion.1
  126.4 0.1 slice_reduce_fusion
  126.5 0.1 fusion.3
  126.6 15.2 %all-to-all-done.3 = bf16[8,128,512]{2,1,0:T(8,128)(2,1)S(1)} async-done(((bf16[8,128,512]{2,1,0:T(8,128)(2,1)}), bf16[8,128,512]{2,1,0:T(8,128)(2,1)S(1)}, u32[]{:S(2)}, u32[]{:S(2)}) %all-to-all-start.3) | async-done | bytes 1048608 | tf_op jit(solution)/shard_map/all_to_all | solution.py:295
  141.9 4.2 %all-to-all-start = ((bf16[8,128,512]{2,1,0:T(8,128)(2,1)}), bf16[8,128,512]{2,1,0:T(8,128)(2,1)}, u32[]{:S(2)}, u32[]{:S(2)}) async-start(bf16[8,128,512]{2,1,0:T(8,128)(2,1)} %get-tuple-element.12), calls=%async_computation | async-start | bytes 2097152 | tf_op jit(solution)/shard_map/all_to_all | solution.py:295
  146.1 0.0 collective-permute-done.kh_ref.vh_ref
  146.1 0.0 copy-start.3
  146.2 1.0 copy-done.3
  147.1 0.0 copy-start.4
  147.1 1.2 copy-done.4
  148.3 13.7 %attend_1.1 = (bf16[1024,512]{1,0:T(8,128)(2,1)S(1)}, bf16[1024,256]{1,0:T(8,128)(2,1)}, f32[1024,256]{1,0:T(8,128)S(1)}) custom-call(f32[8,128]{1,0:T(8,128)S(1)} %pad.5.bias_ref, bf16[1024,512]{1,0:T(8,128)(2,1)S(1)} %bitcast.16, bf16[1024,512]{1,0:T(8,128)(2,1)S(1)} %copy-done.4, bf16[1024,512]{1,0:T(8,128)(2,1)S(1)} %copy-done.4, ...), custom_call_target="tpu_custom_call" | custom-call | flops 14000000000 | bytes 6291456 | tf_op jit(solution)/shard_map/attend_1/pallas_call | solution.py:235
  162.1 0.0 copy-start
  162.1 1.0 copy-done
  163.1 0.0 all-to-all-done
  163.1 4.7 %all-to-all-start.4 = ((bf16[8,128,512]{2,1,0:T(8,128)(2,1)}), bf16[8,128,512]{2,1,0:T(8,128)(2,1)}, u32[]{:S(2)}, u32[]{:S(2)}) async-start(bf16[8,128,512]{2,1,0:T(8,128)(2,1)} %bitcast.17), calls=%async_computation.4 | async-start | bytes 2097152 | tf_op jit(solution)/shard_map/all_to_all | solution.py:295
  167.7 0.0 copy-start.5
  167.7 1.2 copy-done.5
  169.0 14.6 %attend_0.1 = (bf16[1024,512]{1,0:T(8,128)(2,1)}, bf16[1024,256]{1,0:T(8,128)(2,1)}, f32[1024,256]{1,0:T(8,128)S(1)}) custom-call(f32[8,128]{1,0:T(8,128)S(1)} %pad.5.bias_ref, bf16[1024,512]{1,0:T(8,128)(2,1)} %bitcast.1.qd_ref, bf16[1024,512]{1,0:T(8,128)(2,1)S(1)} %copy-done.5, bf16[1024,512]{1,0:T(8,128)(2,1)S(1)} %copy-done.5, ...), custom_call_target="tpu_custom_call" | custom-call | flops 14000000000 | bytes 6291456 | tf_op jit(solution)/shard_map/attend_0/pallas_call | solution.py:235
  183.6 0.0 copy-start.1
  183.6 1.0 copy-done.1
  184.5 6.1 %collective-permute-start.1 = (bf16[1024,256]{1,0:T(8,128)(2,1)}, bf16[1024,256]{1,0:T(8,128)(2,1)}, u32[]{:S(2)}, u32[]{:S(2)}) collective-permute-start(bf16[1024,256]{1,0:T(8,128)(2,1)} %get-tuple-element.17), channel_id=1, source_target_pairs={{8,0},{16,8},{24,16},{32,24},{40,32},{48,40},{56,48},{64,56},{72,6... | collective-permute-start | bytes 1572872 | tf_op jit(solution)/shard_map/ppermute | solution.py:301
  190.7 3.9 %collective-permute-start.2 = (bf16[1024,256]{1,0:T(8,128)(2,1)}, bf16[1024,256]{1,0:T(8,128)(2,1)}, u32[]{:S(2)}, u32[]{:S(2)}) collective-permute-start(bf16[1024,256]{1,0:T(8,128)(2,1)} %get-tuple-element.19), channel_id=1, source_target_pairs={{8,0},{16,8},{24,16},{32,24},{40,32},{48,40},{56,48},{64,56},{72,6... | collective-permute-start | bytes 1572872 | tf_op jit(solution)/shard_map/ppermute | solution.py:301
  194.6 0.0 all-to-all-done.4.a1_ref
  194.6 0.0 copy-start.2
  194.6 4.9 %all-to-all-start.2 = ((bf16[8,128,512]{2,1,0:T(8,128)(2,1)}), bf16[8,128,512]{2,1,0:T(8,128)(2,1)S(1)}, u32[]{:S(2)}, u32[]{:S(2)}) async-start(bf16[8,128,512]{2,1,0:T(8,128)(2,1)} %bitcast.3), calls=%async_computation.2 | async-start | bytes 2097152 | tf_op jit(solution)/shard_map/all_to_all | solution.py:295
  199.6 3.6 %collective-permute-done.1 = bf16[1024,256]{1,0:T(8,128)(2,1)} collective-permute-done((bf16[1024,256]{1,0:T(8,128)(2,1)}, bf16[1024,256]{1,0:T(8,128)(2,1)}, u32[]{:S(2)}, u32[]{:S(2)}) %collective-permute-start.1) | collective-permute-done | bytes 524320 | tf_op jit(solution)/shard_map/ppermute | solution.py:301
  203.2 0.0 copy-done.2
  203.2 1.2 add_convert_fusion.1
  204.4 9.6 %collective-permute-done.2 = bf16[1024,256]{1,0:T(8,128)(2,1)} collective-permute-done((bf16[1024,256]{1,0:T(8,128)(2,1)}, bf16[1024,256]{1,0:T(8,128)(2,1)}, u32[]{:S(2)}, u32[]{:S(2)}) %collective-permute-start.2) | collective-permute-done | bytes 524320 | tf_op jit(solution)/shard_map/ppermute | solution.py:301
  214.0 1.2 add_convert_fusion
  215.2 0.1 pad_maximum_fusion
  215.4 0.0 all-to-all-done.2.a0_ref
  215.4 0.0 copy-start.6
  215.4 20.0 %all_to_all.31.kv_ref = bf16[8,128,512]{2,1,0:T(8,128)(2,1)} all-to-all(bf16[8,128,512]{2,1,0:T(8,128)(2,1)S(1)} %pad_maximum_fusion), channel_id=1, replica_groups=mesh['x'=4,'z'=8,'y_lo'=2,'head'=4] {'y_lo','head'}, dimensions={0} | all-to-all | bytes 2097152 | tf_op jit(solution)/shard_map/all_to_all | solution.py:295
  235.4 0.0 copy-done.6
  235.4 96.8 %unpack.1 = (bf16[128,4096]{1,0:T(8,128)(2,1)}, bf16[128,4096]{1,0:T(8,128)(2,1)}, bf16[128,2048]{1,0:T(8,128)(2,1)}, bf16[128,2048]{1,0:T(8,128)(2,1)}) custom-call(bf16[8,128,512]{2,1,0:T(8,128)(2,1)} %copy-done.6, bf16[8,128,512]{2,1,0:T(8,128)(2,1)} %all-to-all-done.4.a1_ref, bf16[8,128,512]{2,1,0:T(8,128)(2,1)} %all_to_all.31.kv_ref), custom_call_target="tpu_custom_call" | custom-call | bytes 6291456 | tf_op jit(solution)/shard_map/unpack/pallas_call | solution.py:106
  (5 shorter events, 0.1 us)
Async XLA Ops:
  53.8 92.3 %collective-permute-start = (bf16[1024,512]{1,0:T(8,128)(2,1)S(1)}, bf16[1024,512]{1,0:T(8,128)(2,1)S(1)}, u32[]{:S(2)}, u32[]{:S(2)}) collective-permute-start(bf16[1024,512]{1,0:T(8,128)(2,1)S(1)} %bitcast.11), channel_id=1, source_target_pairs={{0,8},{8,16},{16,24},{24,32},{32,40},{40,48},{48,56},{56,64},{64,7... | collective-permute-start | bytes 3145736 | tf_op jit(solution)/shard_map/ppermute | solution.py:301
  122.5 3.7 %copy-start.7 = (s32[32768]{0:T(1024)S(1)}, s32[32768]{0:T(1024)}, u32[]{:S(2)}) copy-start(s32[32768]{0:T(1024)} %param.9) | copy-start | bytes 393220
  122.6 19.3 %all-to-all-start.3 = ((bf16[8,128,512]{2,1,0:T(8,128)(2,1)}), bf16[8,128,512]{2,1,0:T(8,128)(2,1)S(1)}, u32[]{:S(2)}, u32[]{:S(2)}) async-start(bf16[8,128,512]{2,1,0:T(8,128)(2,1)} %get-tuple-element.14), calls=%async_computation.3 | async-start | bytes 2097152 | tf_op jit(solution)/shard_map/all_to_all | solution.py:295
  141.9 21.2 %all-to-all-start = ((bf16[8,128,512]{2,1,0:T(8,128)(2,1)}), bf16[8,128,512]{2,1,0:T(8,128)(2,1)}, u32[]{:S(2)}, u32[]{:S(2)}) async-start(bf16[8,128,512]{2,1,0:T(8,128)(2,1)} %get-tuple-element.12), calls=%async_computation | async-start | bytes 2097152 | tf_op jit(solution)/shard_map/all_to_all | solution.py:295
  146.1 1.0 copy-start.3
  147.1 1.2 copy-start.4
  162.1 1.0 copy-start
  163.1 31.5 %all-to-all-start.4 = ((bf16[8,128,512]{2,1,0:T(8,128)(2,1)}), bf16[8,128,512]{2,1,0:T(8,128)(2,1)}, u32[]{:S(2)}, u32[]{:S(2)}) async-start(bf16[8,128,512]{2,1,0:T(8,128)(2,1)} %bitcast.17), calls=%async_computation.4 | async-start | bytes 2097152 | tf_op jit(solution)/shard_map/all_to_all | solution.py:295
  167.7 1.2 copy-start.5
  183.6 1.0 copy-start.1
  184.5 18.7 %collective-permute-start.1 = (bf16[1024,256]{1,0:T(8,128)(2,1)}, bf16[1024,256]{1,0:T(8,128)(2,1)}, u32[]{:S(2)}, u32[]{:S(2)}) collective-permute-start(bf16[1024,256]{1,0:T(8,128)(2,1)} %get-tuple-element.17), channel_id=1, source_target_pairs={{8,0},{16,8},{24,16},{32,24},{40,32},{48,40},{56,48},{64,56},{72,6... | collective-permute-start | bytes 1572872 | tf_op jit(solution)/shard_map/ppermute | solution.py:301
  190.7 23.4 %collective-permute-start.2 = (bf16[1024,256]{1,0:T(8,128)(2,1)}, bf16[1024,256]{1,0:T(8,128)(2,1)}, u32[]{:S(2)}, u32[]{:S(2)}) collective-permute-start(bf16[1024,256]{1,0:T(8,128)(2,1)} %get-tuple-element.19), channel_id=1, source_target_pairs={{8,0},{16,8},{24,16},{32,24},{40,32},{48,40},{56,48},{64,56},{72,6... | collective-permute-start | bytes 1572872 | tf_op jit(solution)/shard_map/ppermute | solution.py:301
  194.6 8.6 %copy-start.2 = (f32[1024,256]{1,0:T(8,128)S(1)}, f32[1024,256]{1,0:T(8,128)}, u32[]{:S(2)}) copy-start(f32[1024,256]{1,0:T(8,128)} %copy-done.1) | copy-start | bytes 3145732
  194.6 20.8 %all-to-all-start.2 = ((bf16[8,128,512]{2,1,0:T(8,128)(2,1)}), bf16[8,128,512]{2,1,0:T(8,128)(2,1)S(1)}, u32[]{:S(2)}, u32[]{:S(2)}) async-start(bf16[8,128,512]{2,1,0:T(8,128)(2,1)} %bitcast.3), calls=%async_computation.2 | async-start | bytes 2097152 | tf_op jit(solution)/shard_map/all_to_all | solution.py:295
  215.4 20.0 %copy-start.6 = (bf16[8,128,512]{2,1,0:T(8,128)(2,1)}, bf16[8,128,512]{2,1,0:T(8,128)(2,1)S(1)}, u32[]{:S(2)}) copy-start(bf16[8,128,512]{2,1,0:T(8,128)(2,1)S(1)} %all-to-all-done.2.a0_ref) | copy-start | bytes 3145732

commit v2 on v1

v2 whole, which is shorter than its diff:
```python
import functools

import jax
import jax.numpy as jnp
from jax import lax
from jax.experimental import pallas as pl
from jax.experimental.pallas import tpu as pltpu
from jax.sharding import Mesh, PartitionSpec as P

HEAD_SIZE = 128
BLOCK = 128
TILE = 256
SLAB = 1024
NEG = -1e30
GRANT = 12
GRANT_ATTEND = 28

score_scale = 168.0 ** (-0.5)
exp2_scale = score_scale * 1.4426950408889634

NT = (((1,), (1,)), ((), ()))
NN = (((1,), (0,)), ((), ()))


def dot(a, b, dims=NN):
    return lax.dot_general(a, b, dims, preferred_element_type=jnp.float32)


SRC, DST, CORE = 0, 4, 8


def scalars():
    y = lax.axis_index("y_hi") * 2 + lax.axis_index("y_lo")
    tiles = []
    for by in (0, -1, -2, -3, 0, 1, 2, 3):
        chip = (y + by) % 4
        tiles.append((chip % 2) * 2 + chip // 2)
    return jnp.stack(tiles + [lax.axis_index("core")]).astype(jnp.int32)


def aligned(start, size):
    return pl.ds(pl.multiple_of(start, 128), size)


def local_call(kernel, out_shape, name, grant, cost, scratch=()):
    def call(tab, *args):
        return pl.pallas_call(
            kernel,
            out_shape=out_shape,
            in_specs=[pl.BlockSpec(memory_space=pltpu.SMEM)]
            + [pl.BlockSpec(memory_space=pltpu.VMEM)] * len(args),
            out_specs=jax.tree.map(lambda _: pl.BlockSpec(memory_space=pltpu.VMEM), out_shape),
            scratch_shapes=list(scratch),
            compiler_params=pltpu.CompilerParams(vmem_limit_bytes=grant << 20),
            cost_estimate=cost,
            name=name,
        )(tab, *args)

    return call


def moves(megabytes):
    return pl.CostEstimate(flops=0, transcendentals=0, bytes_accessed=int(megabytes * 2**20))


def array(*shape, dtype=jnp.bfloat16):
    return jax.ShapeDtypeStruct(shape, dtype)


def pack_kv_kernel(tab, k_ref, v_ref, *out):
    for i in range(4):
        at = tab[DST + i] * 512
        for n, src in enumerate((k_ref, v_ref)):
            for head in range(4):
                col = 256 * head + 128 * n
                out[i][:, col : col + 128] = src[:, aligned(at + 128 * head, 128)]


def pack_qd_kernel(tab, q_ref, d_ref, *out):
    for i in range(4):
        at = tab[DST + i] * 1024
        for n, src in enumerate((q_ref, d_ref)):
            for core in range(2):
                for chunk in range(2):
                    col = 512 * core + 256 * n
                    out[4 * chunk + i][:, col : col + 256] = src[
                        :, aligned(at + 512 * core + 256 * chunk, 256)
                    ]


def to_sibling_in_kernel(tab, p0, p1, p2, p3, out):
    at = (1 - tab[CORE]) * 512
    for i, p in enumerate((p0, p1, p2, p3)):
        out[i] = p[:, aligned(at, 512)]


def to_sibling_out_kernel(tab, p0, p1, p2, p3, out):
    at = (1 - tab[CORE]) * 128
    for i, p in enumerate((p0, p1, p2, p3)):
        out[i] = p[aligned(at, 128), :]


def halo_kernel(tab, p0, p1, p2, p3, sib, out0, out1):
    at = tab[CORE] * 512
    for chunk, out in enumerate((out0, out1)):
        for i, p in enumerate((p0, p1, p2, p3)):
            out[2 * i] = p[:, aligned(at + 256 * chunk, 256)]
            out[2 * i + 1] = sib[i, :, 256 * chunk : 256 * (chunk + 1)]


def merge_kernel(tab, own0, own1, from0, from1, *out):
    for i in range(4):
        rows = aligned(tab[DST + i] * TILE, TILE)
        for chunk, (own, other) in enumerate(((own0, from0), (own1, from1))):
            out[i][:, 256 * chunk : 256 * (chunk + 1)] = (
                own[rows, :] + other[rows, :].astype(jnp.float32)
            ).astype(jnp.bfloat16)


def arrived(tab, direct, sib):
    core = tab[CORE]
    for i in range(4):
        yield 2 * tab[SRC + i] + core, direct[i].at[aligned(core * 128, 128), :]
        yield 2 * tab[SRC + i] + 1 - core, sib.at[i]


def unpack_out_kernel(tab, *refs):
    o_ref, dq_ref = refs[10:]
    for chunk in range(2):
        parts = refs[5 * chunk : 5 * chunk + 5]
        for group, piece in arrived(tab, parts[:4], parts[4]):
            for n, out in enumerate((o_ref, dq_ref)):
                out[:, aligned(group * 512 + 256 * chunk, 256)] = piece[:, 256 * n : 256 * (n + 1)]


def unpack_kv_kernel(tab, p0, p1, p2, p3, sib, dk_ref, dv_ref):
    for group, piece in arrived(tab, (p0, p1, p2, p3), sib):
        for chunk in range(2):
            for n, out in enumerate((dk_ref, dv_ref)):
                at = 256 * chunk + 128 * n
                out[:, aligned(group * 256 + 128 * chunk, 128)] = piece[:, at : at + 128]


def attn_kernel(chunk, tab, bias_ref, *refs):
    q_parts, q_sib, kv_parts, kv_sib, halo = refs[0:4], refs[4], refs[5:9], refs[9], refs[10]
    outs, ghalo_ref, gown_ref = refs[11:15], refs[15], refs[16]
    (
        kaug, vaug, kt, v1t, qd_ref, out_ref, qaug, doaug, s_ref, e_ref, d_ref, dk_acc, dv_acc,
    ) = refs[17:]
    f32, bf16 = jnp.float32, jnp.bfloat16
    core = tab[CORE]

    lane = lax.broadcasted_iota(jnp.int32, (BLOCK, 128), 1)
    three = jnp.where(lane < 3, 1.0, 0.0).astype(bf16)

    def place_kv(at, k, v):
        rows = aligned(at, BLOCK)
        kaug[rows, 0:128] = k
        kaug[rows, 128:256] = jnp.where(lane == at // BLOCK, 1.0, 0.0).astype(bf16)
        vaug[rows, 0:128] = v
        vaug[rows, 128:256] = three
        kt[:, rows] = k.T
        v1t[0:128, rows] = v.T
        v1t[128:144, rows] = jnp.ones((16, BLOCK), bf16)

    for i in range(4):
        for n in range(2):
            at = tab[SRC + i] * TILE + (core if n == 0 else 1 - core) * BLOCK
            place_kv(at, halo[2 * i + n, :, 0:128], halo[2 * i + n, :, 128:256])
            if n == 0:
                col = core * 512 + 256 * chunk
                k = kv_parts[i][:, aligned(col, 128)]
                v = kv_parts[i][:, aligned(col + 128, 128)]
                qd = q_parts[i][:, aligned(core * 512, 512)]
            else:
                k = kv_sib[i, :, 256 * chunk : 256 * chunk + 128]
                v = kv_sib[i, :, 256 * chunk + 128 : 256 * chunk + 256]
                qd = q_sib[i]
            place_kv(SLAB + at, k, v)
            qd_ref[aligned(at, BLOCK), :] = qd
    dk_acc[...] = jnp.zeros_like(dk_acc)
    dv_acc[...] = jnp.zeros_like(dv_acc)

    @pl.loop(0, SLAB // TILE)
    def _(i):
        tile = pl.ds(pl.multiple_of(i * TILE, TILE), TILE)
        attn_tile(
            i, bias_ref, qd_ref.at[tile, :], out_ref.at[tile, :],
            kaug, vaug, kt, v1t, qaug, doaug, s_ref, e_ref, d_ref, dk_acc, dv_acc,
        )

    for i in range(4):
        outs[i][...] = out_ref[aligned(tab[DST + i] * TILE, TILE), :]
    ghalo_ref[:, 0:128] = (dk_acc[0:SLAB, :] * score_scale).astype(bf16)
    ghalo_ref[:, 128:256] = dv_acc[0:SLAB, :].astype(bf16)
    gown_ref[:, 0:128] = dk_acc[SLAB : 2 * SLAB, :] * score_scale
    gown_ref[:, 128:256] = dv_acc[SLAB : 2 * SLAB, :]


def attn_tile(
    i, bias_ref, qd_ref, out_ref,
    kaug, vaug, kt, v1t, qaug, doaug, s_ref, e_ref, d_ref, dk_acc, dv_acc,
):
    f32, bf16 = jnp.float32, jnp.bfloat16
    base = pl.multiple_of(i * TILE, TILE)
    window = pl.ds(base, 5 * TILE)

    for b in range(2):
        row_bias = bias_ref[pl.ds(2 * i + b, 1), :]
        rows_bias = jnp.broadcast_to(row_bias, (BLOCK, 128)).astype(bf16)
        for h in range(2):
            qaug[TILE * h + BLOCK * b : TILE * h + BLOCK * (b + 1), 128:256] = rows_bias
    for h in range(2):
        qaug[TILE * h : TILE * (h + 1), 0:128] = qd_ref[:, 128 * h : 128 * (h + 1)]

    s_pos = lax.broadcasted_iota(jnp.int32, (TILE, TILE), 0)
    t_pos = lax.broadcasted_iota(jnp.int32, (TILE, TILE), 1)
    far = s_pos > t_pos
    top8 = jnp.full((8, 2 * TILE), NEG, f32)
    for j in range(5):
        s = dot(kaug[pl.ds(base + TILE * j, TILE), :], qaug[...], NT)
        if j in (0, 4):
            keep = far if j == 0 else jnp.logical_not(far)
            s = jnp.concatenate(
                [jnp.where(keep, s[:, :TILE], NEG), jnp.where(keep, s[:, TILE:], NEG)], axis=1
            )
        s_ref[TILE * j : TILE * (j + 1), :] = s
        top8 = jnp.maximum(top8, jnp.max(s.reshape(TILE // 8, 8, 2 * TILE), axis=0))
    top = jnp.max(top8, axis=0, keepdims=True)
    for j in range(5):
        rows = slice(TILE * j, TILE * (j + 1))
        e_ref[rows, :] = jnp.exp2((s_ref[rows, :] - top) * exp2_scale).astype(bf16)

    ot = dot(v1t[:, window], e_ref[...])
    r = 1.0 / ot[128:129, :]
    attended = (ot[0:128, :] * r).T.astype(bf16)
    r_rows = jnp.broadcast_to(r, (128, 2 * TILE)).T
    grad = jnp.concatenate([qd_ref[:, 256:384], qd_ref[:, 384:512]], axis=0)
    grad_n = (grad.astype(f32) * r_rows).astype(bf16)
    delta = jnp.sum(grad_n.astype(f32) * attended.astype(f32), axis=1, keepdims=True)
    minus = jnp.broadcast_to(-delta, (2 * TILE, 128))
    part0 = minus.astype(bf16).astype(f32)
    part1 = (minus - part0).astype(bf16).astype(f32)
    part2 = minus - part0 - part1
    lane = lax.broadcasted_iota(jnp.int32, (2 * TILE, 128), 1)
    parts = jnp.where(
        lane == 0, part0, jnp.where(lane == 1, part1, jnp.where(lane == 2, part2, 0.0))
    )
    doaug[:, 0:128] = grad_n
    doaug[:, 128:256] = parts.astype(bf16)
    for h in range(2):
        out_ref[:, 128 * h : 128 * (h + 1)] = attended[TILE * h : TILE * (h + 1), :]

    for j in range(5):
        rows = slice(TILE * j, TILE * (j + 1))
        dp = dot(vaug[pl.ds(base + TILE * j, TILE), :], doaug[...], NT)
        d_ref[rows, :] = (e_ref[rows, :].astype(f32) * dp).astype(bf16)

    dq = (dot(kt[:, window], d_ref[...]) * score_scale).T.astype(bf16)
    for h in range(2):
        out_ref[:, 256 + 128 * h : 384 + 128 * h] = dq[TILE * h : TILE * (h + 1), :]
    dv = dot(e_ref[...], doaug[:, 0:128])
    dk = dot(d_ref[...], qaug[:, 0:128])

    dk_acc[window, :] = dk_acc[window, :] + dk
    dv_acc[window, :] = dv_acc[window, :] + dv


def attend(chunk, tab, bias, q_parts, q_sib, kv_parts, kv_sib, halo):
    f32, bf16 = jnp.float32, jnp.bfloat16
    call = local_call(
        functools.partial(attn_kernel, chunk),
        [array(TILE, 512)] * 4 + [array(SLAB, 256), array(SLAB, 256, dtype=f32)],
        f"attend_{chunk}",
        GRANT_ATTEND,
        pl.CostEstimate(flops=14 * 10**9, transcendentals=0, bytes_accessed=4 << 20),
        scratch=[
            pltpu.VMEM((2 * SLAB, 256), bf16),
            pltpu.VMEM((2 * SLAB, 256), bf16),
            pltpu.VMEM((128, 2 * SLAB), bf16),
            pltpu.VMEM((144, 2 * SLAB), bf16),
            pltpu.VMEM((SLAB, 512), bf16),
            pltpu.VMEM((SLAB, 512), bf16),
            pltpu.VMEM((2 * TILE, 256), bf16),
            pltpu.VMEM((2 * TILE, 256), bf16),
            pltpu.VMEM((5 * TILE, 2 * TILE), f32),
            pltpu.VMEM((5 * TILE, 2 * TILE), bf16),
            pltpu.VMEM((5 * TILE, 2 * TILE), bf16),
            pltpu.VMEM((2 * SLAB, 128), f32),
            pltpu.VMEM((2 * SLAB, 128), f32),
        ],
    )
    out = call(tab, bias, *q_parts, q_sib, *kv_parts, kv_sib, halo)
    return out[:4], out[4], out[5]


def block_bias(doc_ids, slab):
    blocks = SLAB // BLOCK
    padded = jnp.concatenate([jnp.full((SLAB,), -1, jnp.int32), doc_ids])
    ids = lax.dynamic_slice_in_dim(padded, slab * SLAB, 2 * SLAB, 0).reshape(2 * blocks, BLOCK)[:, 0]
    own = ids[blocks:]
    query = jnp.arange(blocks)[:, None]
    key = jnp.arange(2 * blocks)[None, :]
    ok = (own[:, None] == ids[None, :]) & (key >= query) & (key <= query + blocks)
    return jnp.pad(jnp.where(ok, 0.0, NEG).astype(jnp.float32), ((0, 0), (0, 128 - 2 * blocks)))


RING = ("y_lo", "y_hi", "core")
LINE = ("x", "z")


def ring_shift(x, by):
    pairs = []
    for device in range(8):
        y_lo, y_hi, core = device // 4, device // 2 % 2, device % 2
        chip = (2 * y_hi + y_lo + by) % 4
        pairs.append((device, (chip % 2) * 4 + (chip // 2) * 2 + core))
    return lax.ppermute(x, RING, pairs)


def spread(pieces):
    return [pieces[0]] + [ring_shift(pieces[i], i) for i in (1, 3, 2)]


def in_order(received):
    return [received[0], received[1], received[3], received[2]]


def exchange(pieces):
    return in_order(spread(pieces))


def swap_cores(x):
    return lax.ppermute(x, "core", [(0, 1), (1, 0)])


def shifted(x, by):
    count = lax.axis_size(LINE)
    pairs = [(i, i + by) for i in range(count) if 0 <= i + by < count]
    return lax.ppermute(x, LINE, pairs)


def body(queries, key_vectors, value_vectors, output_gradient, doc_ids):
    tab = scalars()
    rows = queries.shape[0]
    sibling_in = local_call(
        to_sibling_in_kernel, array(4, rows, 512), "to_sibling_in", GRANT, moves(1)
    )
    sibling_out = local_call(
        to_sibling_out_kernel, array(4, rows, 512), "to_sibling_out", GRANT, moves(1)
    )
    kv_send = local_call(
        pack_kv_kernel, [array(rows, 1024)] * 4, "pack_kv", GRANT, moves(2)
    )(tab, key_vectors, value_vectors)
    qd_send = local_call(
        pack_qd_kernel, [array(rows, 1024)] * 8, "pack_qd", GRANT, moves(4)
    )(tab, queries, output_gradient)
    bias = block_bias(doc_ids, lax.axis_index(LINE))

    kv = exchange(kv_send)
    kv_sib = swap_cores(sibling_in(tab, *kv))
    halo_send = local_call(
        halo_kernel, [array(8, rows, 256)] * 2, "halo", GRANT, moves(2)
    )(tab, *kv, kv_sib)
    halo = [shifted(x, 1) for x in halo_send]
    out, own, other = [], [], []
    for chunk in range(2):
        qd = exchange(qd_send[4 * chunk : 4 * chunk + 4])
        qd_sib = swap_cores(sibling_in(tab, *qd))
        pieces, g_halo, g_own = attend(chunk, tab, bias, qd, qd_sib, kv, kv_sib, halo[chunk])
        received = exchange(pieces)
        out += [*received, swap_cores(sibling_out(tab, *received))]
        own.append(g_own)
        other.append(shifted(g_halo, -1))
    attn_out, query_grad = local_call(
        unpack_out_kernel, [array(rows, 4096)] * 2, "unpack_out", GRANT, moves(4)
    )(tab, *out)
    pieces = local_call(merge_kernel, [array(TILE, 512)] * 4, "merge", GRANT, moves(4))(
        tab, *own, *other
    )
    received = exchange(pieces)
    key_grad, value_grad = local_call(
        unpack_kv_kernel, [array(rows, 2048)] * 2, "unpack_kv", GRANT, moves(2)
    )(tab, *received, swap_cores(sibling_out(tab, *received)))
    return attn_out, query_grad, key_grad, value_grad


def solution(mesh):
    seqa, seqb, head = (mesh.shape[a] for a in ("seqa", "seqb", "head"))
    axes = ("x", "z", "y_lo", "y_hi", "core")
    fine = Mesh(mesh.devices.reshape(seqa, seqb // 2, 2, head // 2, 2), axes)
    tokens = P(axes, None)
    return jax.shard_map(
        body, mesh=fine, in_specs=(tokens,) * 4 + (P(),), out_specs=(tokens,) * 4, check_vma=False
    )
```

time: 334 us -> 140 us (0.42)
  Pallas kernels: 223 us -> 38.4 us
  blocking collectives: 40.2 us -> 0 us
  waiting for transfers between devices: 28.5 us -> 47.7 us
  starting transfers between devices: 31.4 us -> 47.8 us
    pallas_call x5 -> x14, Pallas kernels: 223 us -> 38.4 us  [call(): pl.pallas_call(kernel, out_shape=out_shape, in_specs=[pl.BlockSpec(memory...]
    all_to_all x2 -> x0, blocking collectives: 40.2 us -> none  [exchange(): return lax.all_to_all(x, GROUP, split_axis=0, concat_axis=0, tiled=False)]
    ppermute x0 -> x24, waiting for transfers between devices: none -> 34.6 us  [the longest x18 34.6 us: ring_shift(): return lax.ppermute(x, RING, pairs)]
    ppermute x0 -> x24, starting transfers between devices: none -> 33.2 us  [the longest x18 32.3 us: ring_shift(): return lax.ppermute(x, RING, pairs)]
    all_to_all x4 -> x0, starting transfers between devices: 17.6 us -> none  [exchange(): return lax.all_to_all(x, GROUP, split_axis=0, concat_axis=0, tiled=False)]
    all_to_all x4 -> x0, waiting for transfers between devices: 15.3 us -> none  [exchange(): return lax.all_to_all(x, GROUP, split_axis=0, concat_axis=0, tiled=False)]
    ppermute x3 -> x4, starting transfers between devices: 13.9 us -> 14.6 us  [shifted(): return lax.ppermute(x, LINE, pairs)]
    ppermute x3 -> x4, waiting for transfers between devices: 13.3 us -> 13.1 us  [shifted(): return lax.ppermute(x, LINE, pairs)]
  transfers between devices with their start and end apart: 7 -> 28, of which waited for: 3 -> 13; matrix products, arithmetic and copies ran while one was open for 1% -> 0% of each run, Pallas kernels for 28% -> 25%
where the time goes in v2:
time: 140 us; the launch traced here: 139 us
  starting transfers between devices  47.8 us (34%)
  waiting for transfers between devices  47.7 us (34%)
  Pallas kernels  38.4 us (27%)
  local copies, waits for them, and re-layouts  3.81 us (3%)
    pallas_call x14, Pallas kernels, call(): pl.pallas_call(kernel, out_shape=out_shape, in_specs=[pl.BlockSpec(memory...  38.4 us
    ppermute x18, waiting for transfers between devices, ring_shift(): return lax.ppermute(x, RING, pairs)  34.6 us
    ppermute x18, starting transfers between devices, ring_shift(): return lax.ppermute(x, RING, pairs)  32.3 us
    ppermute x4, starting transfers between devices, shifted(): return lax.ppermute(x, LINE, pairs)  14.6 us
    ppermute x4, waiting for transfers between devices, shifted(): return lax.ppermute(x, LINE, pairs)  13.1 us
    unnamed x14, local copies, waits for them, and re-layouts  3.48 us
  transfers between devices with their start and end apart: 28, of which 13 were waited for; matrix products, arithmetic and copies ran while one was open for 0% of the time, Pallas kernels for 25%

profile of v2, /device:TPU:6, one launch (start us, length us, event | category | flops | bytes accessed | tf_op | source)
XLA Modules:
  0.0 139.0 jit_solution(17142670898126937819)
XLA Ops:
  1.0 0.1 stack.36.tab
  1.1 1.0 copy-done.2
  2.1 1.0 copy-done.3
  3.1 0.8 pack_kv.1
  4.0 0.0 copy-start
  4.0 1.7 %collective-permute-start.4 = (bf16[128,1024]{1,0:T(8,128)(2,1)S(1)}, bf16[128,1024]{1,0:T(8,128)(2,1)S(1)}, u32[]{:S(2)}, u32[]{:S(2)}) collective-permute-start(bf16[128,1024]{1,0:T(8,128)(2,1)S(1)} %get-tuple-element.43), channel_id=1, source_target_pairs={{0,4},{1,5},{2,6},{3,7},{4,2},{5,3},{6,0},{7,1},{8,12},{9,13},{10,... | collective-permute-start | bytes 786440 | tf_op jit(solution)/shard_map/ppermute | solution.py:318
  5.6 2.9 %collective-permute-start.5 = (bf16[128,1024]{1,0:T(8,128)(2,1)S(1)}, bf16[128,1024]{1,0:T(8,128)(2,1)S(1)}, u32[]{:S(2)}, u32[]{:S(2)}) collective-permute-start(bf16[128,1024]{1,0:T(8,128)(2,1)S(1)} %get-tuple-element.44), channel_id=1, source_target_pairs={{0,2},{1,3},{2,0},{3,1},{4,6},{5,7},{6,4},{7,5},{8,10},{9,11},{10,... | collective-permute-start | bytes 786440 | tf_op jit(solution)/shard_map/ppermute | solution.py:318
  8.5 1.3 collective-permute-start.6
  9.9 3.5 %collective-permute-done.4.p1.refs_6_ = bf16[128,1024]{1,0:T(8,128)(2,1)S(1)} collective-permute-done((bf16[128,1024]{1,0:T(8,128)(2,1)S(1)}, bf16[128,1024]{1,0:T(8,128)(2,1)S(1)}, u32[]{:S(2)}, u32[]{:S(2)}) %collective-permute-start.4) | collective-permute-done | bytes 262176 | tf_op jit(solution)/shard_map/ppermute | solution.py:318
  13.4 6.8 %collective-permute-done.5.p2.refs_7_ = bf16[128,1024]{1,0:T(8,128)(2,1)S(1)} collective-permute-done((bf16[128,1024]{1,0:T(8,128)(2,1)S(1)}, bf16[128,1024]{1,0:T(8,128)(2,1)S(1)}, u32[]{:S(2)}, u32[]{:S(2)}) %collective-permute-start.5) | collective-permute-done | bytes 262176 | tf_op jit(solution)/shard_map/ppermute | solution.py:318
  20.2 0.6 to_sibling_in.4
  20.8 0.0 copy-start.6
  20.8 0.1 collective-permute-start.7
  20.9 1.7 %pack_qd.1 = (bf16[128,1024]{1,0:T(8,128)(2,1)S(1)}, bf16[128,1024]{1,0:T(8,128)(2,1)}, bf16[128,1024]{1,0:T(8,128)(2,1)S(1)}, bf16[128,1024]{1,0:T(8,128)(2,1)S...) custom-call(s32[9]{0:T(128)S(1)} %stack.36.tab, ...), custom_call_target="tpu_custom_call" | custom-call | bytes 4194304 | tf_op jit(solution)/shard_map/pack_qd/pallas_call | solution.py:47
  22.6 0.7 copy-done.4
  23.3 0.7 copy-done.5
  24.0 1.2 collective-permute-start.13
  25.3 2.4 %collective-permute-start.14 = (bf16[128,1024]{1,0:T(8,128)(2,1)}, bf16[128,1024]{1,0:T(8,128)(2,1)S(1)}, u32[]{:S(2)}, u32[]{:S(2)}) collective-permute-start(bf16[128,1024]{1,0:T(8,128)(2,1)} %get-tuple-element.53), channel_id=1, source_target_pairs={{0,2},{1,3},{2,0},{3,1},{4,6},{5,7},{6,4},{7,5},{8,10},{9,11},{10,... | collective-permute-start | bytes 786440 | tf_op jit(solution)/shard_map/ppermute | solution.py:318
  27.6 1.6 %collective-permute-start.15 = (bf16[128,1024]{1,0:T(8,128)(2,1)}, bf16[128,1024]{1,0:T(8,128)(2,1)}, u32[]{:S(2)}, u32[]{:S(2)}) collective-permute-start(bf16[128,1024]{1,0:T(8,128)(2,1)} %get-tuple-element.54), channel_id=1, source_target_pairs={{0,6},{1,7},{2,4},{3,5},{4,0},{5,1},{6,2},{7,3},{8,14},{9,15},{10,... | collective-permute-start | bytes 786440 | tf_op jit(solution)/shard_map/ppermute | solution.py:318
  29.2 0.4 collective-permute-start
  29.7 5.3 %collective-permute-done.13.p1.refs_1_ = bf16[128,1024]{1,0:T(8,128)(2,1)S(1)} collective-permute-done((bf16[128,1024]{1,0:T(8,128)(2,1)}, bf16[128,1024]{1,0:T(8,128)(2,1)S(1)}, u32[]{:S(2)}, u32[]{:S(2)}) %collective-permute-start.13) | collective-permute-done | bytes 262176 | tf_op jit(solution)/shard_map/ppermute | solution.py:318
  35.0 6.3 %collective-permute-start.1 = (bf16[128,1024]{1,0:T(8,128)(2,1)}, bf16[128,1024]{1,0:T(8,128)(2,1)S(1)}, u32[]{:S(2)}, u32[]{:S(2)}) collective-permute-start(bf16[128,1024]{1,0:T(8,128)(2,1)} %copy-done.5), channel_id=1, source_target_pairs={{0,2},{1,3},{2,0},{3,1},{4,6},{5,7},{6,4},{7,5},{8,10},{9,11},{10,... | collective-permute-start | bytes 786440 | tf_op jit(solution)/shard_map/ppermute | solution.py:318
  41.3 1.0 to_sibling_in.5
  42.3 0.1 collective-permute-start.16
  42.4 0.0 collective-permute-done.7.sib.refs_9_
  42.4 0.6 halo.1
  43.1 3.8 %collective-permute-start.17 = (bf16[8,128,256]{2,1,0:T(8,128)(2,1)S(1)}, bf16[8,128,256]{2,1,0:T(8,128)(2,1)S(1)}, u32[]{:S(2)}, u32[]{:S(2)}) collective-permute-start(bf16[8,128,256]{2,1,0:T(8,128)(2,1)S(1)} %get-tuple-element.55), channel_id=1, source_target_pairs={{0,8},{8,16},{16,24},{24,32},{32,40},{40,48},{48,56},{56,64},{64,7... | collective-permute-start | bytes 1572872 | tf_op jit(solution)/shard_map/ppermute | solution.py:340
  46.9 0.1 slice_reduce_fusion.1
  47.0 0.1 slice_reduce_fusion
  47.1 0.1 fusion.3
  47.2 4.2 %collective-permute-done.1.p2.refs_2_ = bf16[128,1024]{1,0:T(8,128)(2,1)S(1)} collective-permute-done((bf16[128,1024]{1,0:T(8,128)(2,1)}, bf16[128,1024]{1,0:T(8,128)(2,1)S(1)}, u32[]{:S(2)}, u32[]{:S(2)}) %collective-permute-start.1) | collective-permute-done | bytes 262176 | tf_op jit(solution)/shard_map/ppermute | solution.py:318
  51.4 0.2 collective-permute-done.2.p3.refs_3_
  51.6 0.6 to_sibling_in.3
  52.2 0.1 collective-permute-start.3
  52.3 4.0 %collective-permute-start.8 = (bf16[8,128,256]{2,1,0:T(8,128)(2,1)S(1)}, bf16[8,128,256]{2,1,0:T(8,128)(2,1)S(1)}, u32[]{:S(2)}, u32[]{:S(2)}) collective-permute-start(bf16[8,128,256]{2,1,0:T(8,128)(2,1)S(1)} %get-tuple-element.46), channel_id=1, source_target_pairs={{0,8},{8,16},{16,24},{24,32},{32,40},{40,48},{48,56},{56,64},{64,7... | collective-permute-start | bytes 1572872 | tf_op jit(solution)/shard_map/ppermute | solution.py:340
  56.4 7.5 %collective-permute-done.17.refs_10_ = bf16[8,128,256]{2,1,0:T(8,128)(2,1)S(1)} collective-permute-done((bf16[8,128,256]{2,1,0:T(8,128)(2,1)S(1)}, bf16[8,128,256]{2,1,0:T(8,128)(2,1)S(1)}, u32[]{:S(2)}, u32[]{:S(2)}) %collective-permute-start.17) | collective-permute-done | bytes 524320 | tf_op jit(solution)/shard_map/ppermute | solution.py:340
  63.9 13.5 %attend_1.1 = (bf16[256,512]{1,0:T(8,128)(2,1)S(1)}, bf16[256,512]{1,0:T(8,128)(2,1)S(1)}, bf16[256,512]{1,0:T(8,128)(2,1)S(1)}, bf16[256,512]{1,0:T(8,128)(2,1)...) custom-call(s32[9]{0:T(128)S(1)} %stack.36.tab, f32[8,128]{1,0:T(8,128)S(1)} %pad.5.bias_ref, ...), custom_call_target="tpu_custom_call" | custom-call | flops 14000000000 | bytes 4194304 | tf_op jit(solution)/shard_map/attend_1/pallas_call | solution.py:47
  77.4 3.8 %collective-permute-start.23 = (bf16[1024,256]{1,0:T(8,128)(2,1)S(1)}, bf16[1024,256]{1,0:T(8,128)(2,1)S(1)}, u32[]{:S(2)}, u32[]{:S(2)}) collective-permute-start(bf16[1024,256]{1,0:T(8,128)(2,1)S(1)} %get-tuple-element.65), channel_id=1, source_target_pairs={{8,0},{16,8},{24,16},{32,24},{40,32},{48,40},{56,48},{64,56},{72,6... | collective-permute-start | bytes 1572872 | tf_op jit(solution)/shard_map/ppermute | solution.py:340
  81.3 13.1 %attend_0.1 = (bf16[256,512]{1,0:T(8,128)(2,1)S(1)}, bf16[256,512]{1,0:T(8,128)(2,1)S(1)}, bf16[256,512]{1,0:T(8,128)(2,1)S(1)}, bf16[256,512]{1,0:T(8,128)(2,1)...) custom-call(s32[9]{0:T(128)S(1)} %stack.36.tab, f32[8,128]{1,0:T(8,128)S(1)} %pad.5.bias_ref, ...), custom_call_target="tpu_custom_call" | custom-call | flops 14000000000 | bytes 4194304 | tf_op jit(solution)/shard_map/attend_0/pallas_call | solution.py:47
  94.4 2.9 %collective-permute-start.22 = (bf16[1024,256]{1,0:T(8,128)(2,1)S(1)}, bf16[1024,256]{1,0:T(8,128)(2,1)S(1)}, u32[]{:S(2)}, u32[]{:S(2)}) collective-permute-start(bf16[1024,256]{1,0:T(8,128)(2,1)S(1)} %get-tuple-element.64), channel_id=1, source_target_pairs={{8,0},{16,8},{24,16},{32,24},{40,32},{48,40},{56,48},{64,56},{72,6... | collective-permute-start | bytes 1572872 | tf_op jit(solution)/shard_map/ppermute | solution.py:340
  97.4 2.1 %collective-permute-start.18 = (bf16[256,512]{1,0:T(8,128)(2,1)S(1)}, bf16[256,512]{1,0:T(8,128)(2,1)S(1)}, u32[]{:S(2)}, u32[]{:S(2)}) collective-permute-start(bf16[256,512]{1,0:T(8,128)(2,1)S(1)} %get-tuple-element.57), channel_id=1, source_target_pairs={{0,4},{1,5},{2,6},{3,7},{4,2},{5,3},{6,0},{7,1},{8,12},{9,13},{10,... | collective-permute-start | bytes 786440 | tf_op jit(solution)/shard_map/ppermute | solution.py:318
  99.5 1.9 %collective-permute-start.19 = (bf16[256,512]{1,0:T(8,128)(2,1)S(1)}, bf16[256,512]{1,0:T(8,128)(2,1)S(1)}, u32[]{:S(2)}, u32[]{:S(2)}) collective-permute-start(bf16[256,512]{1,0:T(8,128)(2,1)S(1)} %get-tuple-element.58), channel_id=1, source_target_pairs={{0,2},{1,3},{2,0},{3,1},{4,6},{5,7},{6,4},{7,5},{8,10},{9,11},{10,... | collective-permute-start | bytes 786440 | tf_op jit(solution)/shard_map/ppermute | solution.py:318
  101.4 1.2 collective-permute-start.20
  102.5 1.1 collective-permute-start.10
  103.6 5.6 %collective-permute-done.22.from0 = bf16[1024,256]{1,0:T(8,128)(2,1)S(1)} collective-permute-done((bf16[1024,256]{1,0:T(8,128)(2,1)S(1)}, bf16[1024,256]{1,0:T(8,128)(2,1)S(1)}, u32[]{:S(2)}, u32[]{:S(2)}) %collective-permute-start.22) | collective-permute-done | bytes 524320 | tf_op jit(solution)/shard_map/ppermute | solution.py:340
  109.2 2.5 %collective-permute-start.11 = (bf16[256,512]{1,0:T(8,128)(2,1)S(1)}, bf16[256,512]{1,0:T(8,128)(2,1)S(1)}, u32[]{:S(2)}, u32[]{:S(2)}) collective-permute-start(bf16[256,512]{1,0:T(8,128)(2,1)S(1)} %get-tuple-element.50), channel_id=1, source_target_pairs={{0,6},{1,7},{2,4},{3,5},{4,0},{5,1},{6,2},{7,3},{8,14},{9,15},{10,... | collective-permute-start | bytes 786440 | tf_op jit(solution)/shard_map/ppermute | solution.py:318
  111.7 0.7 merge.1
  112.4 0.1 collective-permute-start.9
  112.5 1.7 %collective-permute-done.19.p2.refs_7_ = bf16[256,512]{1,0:T(8,128)(2,1)S(1)} collective-permute-done((bf16[256,512]{1,0:T(8,128)(2,1)S(1)}, bf16[256,512]{1,0:T(8,128)(2,1)S(1)}, u32[]{:S(2)}, u32[]{:S(2)}) %collective-permute-start.19) | collective-permute-done | bytes 262176 | tf_op jit(solution)/shard_map/ppermute | solution.py:318
  114.2 0.0 collective-permute-start.24
  114.2 0.3 collective-permute-done.20.p3.refs_8_
  114.5 2.7 %collective-permute-start.25 = (bf16[256,512]{1,0:T(8,128)(2,1)S(1)}, bf16[256,512]{1,0:T(8,128)(2,1)S(1)}, u32[]{:S(2)}, u32[]{:S(2)}) collective-permute-start(bf16[256,512]{1,0:T(8,128)(2,1)S(1)} %get-tuple-element.68), channel_id=1, source_target_pairs={{0,2},{1,3},{2,0},{3,1},{4,6},{5,7},{6,4},{7,5},{8,10},{9,11},{10,... | collective-permute-start | bytes 786440 | tf_op jit(solution)/shard_map/ppermute | solution.py:318
  117.2 2.6 %collective-permute-done.10.p2.refs_2_ = bf16[256,512]{1,0:T(8,128)(2,1)S(1)} collective-permute-done((bf16[256,512]{1,0:T(8,128)(2,1)S(1)}, bf16[256,512]{1,0:T(8,128)(2,1)S(1)}, u32[]{:S(2)}, u32[]{:S(2)}) %collective-permute-start.10) | collective-permute-done | bytes 262176 | tf_op jit(solution)/shard_map/ppermute | solution.py:318
  119.8 2.9 %collective-permute-start.26 = (bf16[256,512]{1,0:T(8,128)(2,1)S(1)}, bf16[256,512]{1,0:T(8,128)(2,1)S(1)}, u32[]{:S(2)}, u32[]{:S(2)}) collective-permute-start(bf16[256,512]{1,0:T(8,128)(2,1)S(1)} %get-tuple-element.69), channel_id=1, source_target_pairs={{0,6},{1,7},{2,4},{3,5},{4,0},{5,1},{6,2},{7,3},{8,14},{9,15},{10,... | collective-permute-start | bytes 786440 | tf_op jit(solution)/shard_map/ppermute | solution.py:318
  122.7 0.6 to_sibling_out.4
  123.3 2.4 %collective-permute-done.11.p3.refs_3_ = bf16[256,512]{1,0:T(8,128)(2,1)S(1)} collective-permute-done((bf16[256,512]{1,0:T(8,128)(2,1)S(1)}, bf16[256,512]{1,0:T(8,128)(2,1)S(1)}, u32[]{:S(2)}, u32[]{:S(2)}) %collective-permute-start.11) | collective-permute-done | bytes 262176 | tf_op jit(solution)/shard_map/ppermute | solution.py:318
  125.7 0.6 to_sibling_out.3
  126.3 0.6 collective-permute-start.12
  126.9 4.2 %collective-permute-done.24.p1 = bf16[256,512]{1,0:T(8,128)(2,1)S(1)} collective-permute-done((bf16[256,512]{1,0:T(8,128)(2,1)S(1)}, bf16[256,512]{1,0:T(8,128)(2,1)S(1)}, u32[]{:S(2)}, u32[]{:S(2)}) %collective-permute-start.24) | collective-permute-done | bytes 262176 | tf_op jit(solution)/shard_map/ppermute | solution.py:318
  131.1 3.3 %collective-permute-done.25.p2 = bf16[256,512]{1,0:T(8,128)(2,1)S(1)} collective-permute-done((bf16[256,512]{1,0:T(8,128)(2,1)S(1)}, bf16[256,512]{1,0:T(8,128)(2,1)S(1)}, u32[]{:S(2)}, u32[]{:S(2)}) %collective-permute-start.25) | collective-permute-done | bytes 262176 | tf_op jit(solution)/shard_map/ppermute | solution.py:318
  134.4 0.6 to_sibling_out.5
  135.0 0.1 collective-permute-start.27
  135.1 2.1 %unpack_out.1 = (bf16[128,4096]{1,0:T(8,128)(2,1)}, bf16[128,4096]{1,0:T(8,128)(2,1)}) custom-call(s32[9]{0:T(128)S(1)} %stack.36.tab, bf16[256,512]{1,0:T(8,128)(2,1)S(1)} %get-tuple-element.47.p0.refs_0_, bf16[256,512]{1,0:T(8,128)(2,1)S(1)} %collective-permute-done.9.p1.refs_1_, bf16[256,512]{1,0:T(8,128)(2,1)S(1)} %collective-permute-done.10.p2.refs_2_, ...), custom_call_target="tpu_custom_call" | custom-call | bytes 4194304 | tf_op jit(solution)/shard_map/unpack_out/pallas_call | solution.py:47
  137.2 1.8 %unpack_kv.1 = (bf16[128,2048]{1,0:T(8,128)(2,1)}, bf16[128,2048]{1,0:T(8,128)(2,1)}) custom-call(s32[9]{0:T(128)S(1)} %stack.36.tab, bf16[256,512]{1,0:T(8,128)(2,1)S(1)} %get-tuple-element.66.p0, bf16[256,512]{1,0:T(8,128)(2,1)S(1)} %collective-permute-done.24.p1, bf16[256,512]{1,0:T(8,128)(2,1)S(1)} %collective-permute-done.25.p2, ...), custom_call_target="tpu_custom_call" | custom-call | bytes 2097152 | tf_op jit(solution)/shard_map/unpack_kv/pallas_call | solution.py:47
  (27 shorter events, 0.1 us)
Async XLA Ops:
  1.1 1.0 copy-start.2
  2.1 1.0 copy-start.3
  3.1 17.7 %copy-start.1 = (bf16[128,4096]{1,0:T(8,128)(2,1)S(1)}, bf16[128,4096]{1,0:T(8,128)(2,1)}, u32[]{:S(2)}) copy-start(bf16[128,4096]{1,0:T(8,128)(2,1)} %d_ref.1) | copy-start | bytes 3145732
  4.0 16.9 %copy-start = (bf16[128,4096]{1,0:T(8,128)(2,1)S(1)}, bf16[128,4096]{1,0:T(8,128)(2,1)}, u32[]{:S(2)}) copy-start(bf16[128,4096]{1,0:T(8,128)(2,1)} %q_ref.1) | copy-start | bytes 3145732
  4.0 9.4 %collective-permute-start.4 = (bf16[128,1024]{1,0:T(8,128)(2,1)S(1)}, bf16[128,1024]{1,0:T(8,128)(2,1)S(1)}, u32[]{:S(2)}, u32[]{:S(2)}) collective-permute-start(bf16[128,1024]{1,0:T(8,128)(2,1)S(1)} %get-tuple-element.43), channel_id=1, source_target_pairs={{0,4},{1,5},{2,6},{3,7},{4,2},{5,3},{6,0},{7,1},{8,12},{9,13},{10,... | collective-permute-start | bytes 786440 | tf_op jit(solution)/shard_map/ppermute | solution.py:318
  5.6 14.5 %collective-permute-start.5 = (bf16[128,1024]{1,0:T(8,128)(2,1)S(1)}, bf16[128,1024]{1,0:T(8,128)(2,1)S(1)}, u32[]{:S(2)}, u32[]{:S(2)}) collective-permute-start(bf16[128,1024]{1,0:T(8,128)(2,1)S(1)} %get-tuple-element.44), channel_id=1, source_target_pairs={{0,2},{1,3},{2,0},{3,1},{4,6},{5,7},{6,4},{7,5},{8,10},{9,11},{10,... | collective-permute-start | bytes 786440 | tf_op jit(solution)/shard_map/ppermute | solution.py:318
  8.5 11.6 %collective-permute-start.6 = (bf16[128,1024]{1,0:T(8,128)(2,1)S(1)}, bf16[128,1024]{1,0:T(8,128)(2,1)S(1)}, u32[]{:S(2)}, u32[]{:S(2)}) collective-permute-start(bf16[128,1024]{1,0:T(8,128)(2,1)S(1)} %get-tuple-element.45), channel_id=1, source_target_pairs={{0,6},{1,7},{2,4},{3,5},{4,0},{5,1},{6,2},{7,3},{8,14},{9,15},{10,... | collective-permute-start | bytes 786440 | tf_op jit(solution)/shard_map/ppermute | solution.py:318
  20.8 8.9 %copy-start.6 = (s32[32768]{0:T(1024)S(1)}, s32[32768]{0:T(1024)}, u32[]{:S(2)}) copy-start(s32[32768]{0:T(1024)} %param.9) | copy-start | bytes 393220
  20.8 21.6 %collective-permute-start.7 = (bf16[4,128,512]{2,1,0:T(8,128)(2,1)S(1)}, bf16[4,128,512]{2,1,0:T(8,128)(2,1)S(1)}, u32[]{:S(2)}, u32[]{:S(2)}) collective-permute-start(bf16[4,128,512]{2,1,0:T(8,128)(2,1)S(1)} %to_sibling_in.4), channel_id=1, source_target_pairs={{0,1},{1,0},{2,3},{3,2},{4,5},{5,4},{6,7},{7,6},{8,9},{9,8},{10,11... | collective-permute-start | bytes 1572872 | tf_op jit(solution)/shard_map/ppermute | solution.py:334
  22.6 0.7 copy-start.4
  23.3 0.7 copy-start.5
  24.0 11.0 %collective-permute-start.13 = (bf16[128,1024]{1,0:T(8,128)(2,1)}, bf16[128,1024]{1,0:T(8,128)(2,1)S(1)}, u32[]{:S(2)}, u32[]{:S(2)}) collective-permute-start(bf16[128,1024]{1,0:T(8,128)(2,1)} %get-tuple-element.52), channel_id=1, source_target_pairs={{0,4},{1,5},{2,6},{3,7},{4,2},{5,3},{6,0},{7,1},{8,12},{9,13},{10,... | collective-permute-start | bytes 786440 | tf_op jit(solution)/shard_map/ppermute | solution.py:318
  25.3 16.1 %collective-permute-start.14 = (bf16[128,1024]{1,0:T(8,128)(2,1)}, bf16[128,1024]{1,0:T(8,128)(2,1)S(1)}, u32[]{:S(2)}, u32[]{:S(2)}) collective-permute-start(bf16[128,1024]{1,0:T(8,128)(2,1)} %get-tuple-element.53), channel_id=1, source_target_pairs={{0,2},{1,3},{2,0},{3,1},{4,6},{5,7},{6,4},{7,5},{8,10},{9,11},{10,... | collective-permute-start | bytes 786440 | tf_op jit(solution)/shard_map/ppermute | solution.py:318
  27.6 13.7 %collective-permute-start.15 = (bf16[128,1024]{1,0:T(8,128)(2,1)}, bf16[128,1024]{1,0:T(8,128)(2,1)}, u32[]{:S(2)}, u32[]{:S(2)}) collective-permute-start(bf16[128,1024]{1,0:T(8,128)(2,1)} %get-tuple-element.54), channel_id=1, source_target_pairs={{0,6},{1,7},{2,4},{3,5},{4,0},{5,1},{6,2},{7,3},{8,14},{9,15},{10,... | collective-permute-start | bytes 786440 | tf_op jit(solution)/shard_map/ppermute | solution.py:318
  29.2 18.0 %collective-permute-start = (bf16[128,1024]{1,0:T(8,128)(2,1)}, bf16[128,1024]{1,0:T(8,128)(2,1)S(1)}, u32[]{:S(2)}, u32[]{:S(2)}) collective-permute-start(bf16[128,1024]{1,0:T(8,128)(2,1)} %get-tuple-element.39), channel_id=1, source_target_pairs={{0,4},{1,5},{2,6},{3,7},{4,2},{5,3},{6,0},{7,1},{8,12},{9,13},{10,... | collective-permute-start | bytes 786440 | tf_op jit(solution)/shard_map/ppermute | solution.py:318
  35.0 16.4 %collective-permute-start.1 = (bf16[128,1024]{1,0:T(8,128)(2,1)}, bf16[128,1024]{1,0:T(8,128)(2,1)S(1)}, u32[]{:S(2)}, u32[]{:S(2)}) collective-permute-start(bf16[128,1024]{1,0:T(8,128)(2,1)} %copy-done.5), channel_id=1, source_target_pairs={{0,2},{1,3},{2,0},{3,1},{4,6},{5,7},{6,4},{7,5},{8,10},{9,11},{10,... | collective-permute-start | bytes 786440 | tf_op jit(solution)/shard_map/ppermute | solution.py:318
  41.3 10.3 %collective-permute-start.2 = (bf16[128,1024]{1,0:T(8,128)(2,1)}, bf16[128,1024]{1,0:T(8,128)(2,1)S(1)}, u32[]{:S(2)}, u32[]{:S(2)}) collective-permute-start(bf16[128,1024]{1,0:T(8,128)(2,1)} %copy-done.4), channel_id=1, source_target_pairs={{0,6},{1,7},{2,4},{3,5},{4,0},{5,1},{6,2},{7,3},{8,14},{9,15},{10,... | collective-permute-start | bytes 786440 | tf_op jit(solution)/shard_map/ppermute | solution.py:318
  42.3 14.0 %collective-permute-start.16 = (bf16[4,128,512]{2,1,0:T(8,128)(2,1)S(1)}, bf16[4,128,512]{2,1,0:T(8,128)(2,1)S(1)}, u32[]{:S(2)}, u32[]{:S(2)}) collective-permute-start(bf16[4,128,512]{2,1,0:T(8,128)(2,1)S(1)} %to_sibling_in.5), channel_id=1, source_target_pairs={{0,1},{1,0},{2,3},{3,2},{4,5},{5,4},{6,7},{7,6},{8,9},{9,8},{10,11... | collective-permute-start | bytes 1572872 | tf_op jit(solution)/shard_map/ppermute | solution.py:334
  43.1 20.8 %collective-permute-start.17 = (bf16[8,128,256]{2,1,0:T(8,128)(2,1)S(1)}, bf16[8,128,256]{2,1,0:T(8,128)(2,1)S(1)}, u32[]{:S(2)}, u32[]{:S(2)}) collective-permute-start(bf16[8,128,256]{2,1,0:T(8,128)(2,1)S(1)} %get-tuple-element.55), channel_id=1, source_target_pairs={{0,8},{8,16},{16,24},{24,32},{32,40},{40,48},{48,56},{56,64},{64,7... | collective-permute-start | bytes 1572872 | tf_op jit(solution)/shard_map/ppermute | solution.py:340
  52.2 29.0 %collective-permute-start.3 = (bf16[4,128,512]{2,1,0:T(8,128)(2,1)S(1)}, bf16[4,128,512]{2,1,0:T(8,128)(2,1)S(1)}, u32[]{:S(2)}, u32[]{:S(2)}) collective-permute-start(bf16[4,128,512]{2,1,0:T(8,128)(2,1)S(1)} %to_sibling_in.3), channel_id=1, source_target_pairs={{0,1},{1,0},{2,3},{3,2},{4,5},{5,4},{6,7},{7,6},{8,9},{9,8},{10,11... | collective-permute-start | bytes 1572872 | tf_op jit(solution)/shard_map/ppermute | solution.py:334
  52.3 29.0 %collective-permute-start.8 = (bf16[8,128,256]{2,1,0:T(8,128)(2,1)S(1)}, bf16[8,128,256]{2,1,0:T(8,128)(2,1)S(1)}, u32[]{:S(2)}, u32[]{:S(2)}) collective-permute-start(bf16[8,128,256]{2,1,0:T(8,128)(2,1)S(1)} %get-tuple-element.46), channel_id=1, source_target_pairs={{0,8},{8,16},{16,24},{24,32},{32,40},{40,48},{48,56},{56,64},{64,7... | collective-permute-start | bytes 1572872 | tf_op jit(solution)/shard_map/ppermute | solution.py:340
  77.4 25.1 %collective-permute-start.23 = (bf16[1024,256]{1,0:T(8,128)(2,1)S(1)}, bf16[1024,256]{1,0:T(8,128)(2,1)S(1)}, u32[]{:S(2)}, u32[]{:S(2)}) collective-permute-start(bf16[1024,256]{1,0:T(8,128)(2,1)S(1)} %get-tuple-element.65), channel_id=1, source_target_pairs={{8,0},{16,8},{24,16},{32,24},{40,32},{48,40},{56,48},{64,56},{72,6... | collective-permute-start | bytes 1572872 | tf_op jit(solution)/shard_map/ppermute | solution.py:340
  94.4 14.8 %collective-permute-start.22 = (bf16[1024,256]{1,0:T(8,128)(2,1)S(1)}, bf16[1024,256]{1,0:T(8,128)(2,1)S(1)}, u32[]{:S(2)}, u32[]{:S(2)}) collective-permute-start(bf16[1024,256]{1,0:T(8,128)(2,1)S(1)} %get-tuple-element.64), channel_id=1, source_target_pairs={{8,0},{16,8},{24,16},{32,24},{40,32},{48,40},{56,48},{64,56},{72,6... | collective-permute-start | bytes 1572872 | tf_op jit(solution)/shard_map/ppermute | solution.py:340
  97.4 15.0 %collective-permute-start.18 = (bf16[256,512]{1,0:T(8,128)(2,1)S(1)}, bf16[256,512]{1,0:T(8,128)(2,1)S(1)}, u32[]{:S(2)}, u32[]{:S(2)}) collective-permute-start(bf16[256,512]{1,0:T(8,128)(2,1)S(1)} %get-tuple-element.57), channel_id=1, source_target_pairs={{0,4},{1,5},{2,6},{3,7},{4,2},{5,3},{6,0},{7,1},{8,12},{9,13},{10,... | collective-permute-start | bytes 786440 | tf_op jit(solution)/shard_map/ppermute | solution.py:318
  99.5 14.7 %collective-permute-start.19 = (bf16[256,512]{1,0:T(8,128)(2,1)S(1)}, bf16[256,512]{1,0:T(8,128)(2,1)S(1)}, u32[]{:S(2)}, u32[]{:S(2)}) collective-permute-start(bf16[256,512]{1,0:T(8,128)(2,1)S(1)} %get-tuple-element.58), channel_id=1, source_target_pairs={{0,2},{1,3},{2,0},{3,1},{4,6},{5,7},{6,4},{7,5},{8,10},{9,11},{10,... | collective-permute-start | bytes 786440 | tf_op jit(solution)/shard_map/ppermute | solution.py:318
  101.4 13.1 %collective-permute-start.20 = (bf16[256,512]{1,0:T(8,128)(2,1)S(1)}, bf16[256,512]{1,0:T(8,128)(2,1)S(1)}, u32[]{:S(2)}, u32[]{:S(2)}) collective-permute-start(bf16[256,512]{1,0:T(8,128)(2,1)S(1)} %get-tuple-element.59), channel_id=1, source_target_pairs={{0,6},{1,7},{2,4},{3,5},{4,0},{5,1},{6,2},{7,3},{8,14},{9,15},{10,... | collective-permute-start | bytes 786440 | tf_op jit(solution)/shard_map/ppermute | solution.py:318
  102.5 17.3 %collective-permute-start.10 = (bf16[256,512]{1,0:T(8,128)(2,1)S(1)}, bf16[256,512]{1,0:T(8,128)(2,1)S(1)}, u32[]{:S(2)}, u32[]{:S(2)}) collective-permute-start(bf16[256,512]{1,0:T(8,128)(2,1)S(1)} %get-tuple-element.49), channel_id=1, source_target_pairs={{0,2},{1,3},{2,0},{3,1},{4,6},{5,7},{6,4},{7,5},{8,10},{9,11},{10,... | collective-permute-start | bytes 786440 | tf_op jit(solution)/shard_map/ppermute | solution.py:318
  109.2 16.5 %collective-permute-start.11 = (bf16[256,512]{1,0:T(8,128)(2,1)S(1)}, bf16[256,512]{1,0:T(8,128)(2,1)S(1)}, u32[]{:S(2)}, u32[]{:S(2)}) collective-permute-start(bf16[256,512]{1,0:T(8,128)(2,1)S(1)} %get-tuple-element.50), channel_id=1, source_target_pairs={{0,6},{1,7},{2,4},{3,5},{4,0},{5,1},{6,2},{7,3},{8,14},{9,15},{10,... | collective-permute-start | bytes 786440 | tf_op jit(solution)/shard_map/ppermute | solution.py:318
  112.4 13.3 %collective-permute-start.9 = (bf16[256,512]{1,0:T(8,128)(2,1)S(1)}, bf16[256,512]{1,0:T(8,128)(2,1)S(1)}, u32[]{:S(2)}, u32[]{:S(2)}) collective-permute-start(bf16[256,512]{1,0:T(8,128)(2,1)S(1)} %get-tuple-element.48), channel_id=1, source_target_pairs={{0,4},{1,5},{2,6},{3,7},{4,2},{5,3},{6,0},{7,1},{8,12},{9,13},{10,... | collective-permute-start | bytes 786440 | tf_op jit(solution)/shard_map/ppermute | solution.py:318
  114.2 16.8 %collective-permute-start.24 = (bf16[256,512]{1,0:T(8,128)(2,1)S(1)}, bf16[256,512]{1,0:T(8,128)(2,1)S(1)}, u32[]{:S(2)}, u32[]{:S(2)}) collective-permute-start(bf16[256,512]{1,0:T(8,128)(2,1)S(1)} %get-tuple-element.67), channel_id=1, source_target_pairs={{0,4},{1,5},{2,6},{3,7},{4,2},{5,3},{6,0},{7,1},{8,12},{9,13},{10,... | collective-permute-start | bytes 786440 | tf_op jit(solution)/shard_map/ppermute | solution.py:318
  114.5 19.9 %collective-permute-start.25 = (bf16[256,512]{1,0:T(8,128)(2,1)S(1)}, bf16[256,512]{1,0:T(8,128)(2,1)S(1)}, u32[]{:S(2)}, u32[]{:S(2)}) collective-permute-start(bf16[256,512]{1,0:T(8,128)(2,1)S(1)} %get-tuple-element.68), channel_id=1, source_target_pairs={{0,2},{1,3},{2,0},{3,1},{4,6},{5,7},{6,4},{7,5},{8,10},{9,11},{10,... | collective-permute-start | bytes 786440 | tf_op jit(solution)/shard_map/ppermute | solution.py:318
  119.8 14.6 %collective-permute-start.26 = (bf16[256,512]{1,0:T(8,128)(2,1)S(1)}, bf16[256,512]{1,0:T(8,128)(2,1)S(1)}, u32[]{:S(2)}, u32[]{:S(2)}) collective-permute-start(bf16[256,512]{1,0:T(8,128)(2,1)S(1)} %get-tuple-element.69), channel_id=1, source_target_pairs={{0,6},{1,7},{2,4},{3,5},{4,0},{5,1},{6,2},{7,3},{8,14},{9,15},{10,... | collective-permute-start | bytes 786440 | tf_op jit(solution)/shard_map/ppermute | solution.py:318
  125.7 9.4 %collective-permute-start.21 = (bf16[4,128,512]{2,1,0:T(8,128)(2,1)S(1)}, bf16[4,128,512]{2,1,0:T(8,128)(2,1)S(1)}, u32[]{:S(2)}, u32[]{:S(2)}) collective-permute-start(bf16[4,128,512]{2,1,0:T(8,128)(2,1)S(1)} %to_sibling_out.4), channel_id=1, source_target_pairs={{0,1},{1,0},{2,3},{3,2},{4,5},{5,4},{6,7},{7,6},{8,9},{9,8},{10,11... | collective-permute-start | bytes 1572872 | tf_op jit(solution)/shard_map/ppermute | solution.py:334
  126.3 8.8 %collective-permute-start.12 = (bf16[4,128,512]{2,1,0:T(8,128)(2,1)S(1)}, bf16[4,128,512]{2,1,0:T(8,128)(2,1)S(1)}, u32[]{:S(2)}, u32[]{:S(2)}) collective-permute-start(bf16[4,128,512]{2,1,0:T(8,128)(2,1)S(1)} %to_sibling_out.3), channel_id=1, source_target_pairs={{0,1},{1,0},{2,3},{3,2},{4,5},{5,4},{6,7},{7,6},{8,9},{9,8},{10,11... | collective-permute-start | bytes 1572872 | tf_op jit(solution)/shard_map/ppermute | solution.py:334
  135.0 2.2 %collective-permute-start.27 = (bf16[4,128,512]{2,1,0:T(8,128)(2,1)S(1)}, bf16[4,128,512]{2,1,0:T(8,128)(2,1)S(1)}, u32[]{:S(2)}, u32[]{:S(2)}) collective-permute-start(bf16[4,128,512]{2,1,0:T(8,128)(2,1)S(1)} %to_sibling_out.5), channel_id=1, source_target_pairs={{0,1},{1,0},{2,3},{3,2},{4,5},{5,4},{6,7},{7,6},{8,9},{9,8},{10,11... | collective-permute-start | bytes 1572872 | tf_op jit(solution)/shard_map/ppermute | solution.py:334

commit v3 on v2

--- a/solution.py
+++ b/solution.py
@@ -352,26 +352,35 @@
     kv_send = local_call(
         pack_kv_kernel, [array(rows, 1024)] * 4, "pack_kv", GRANT, moves(2)
     )(tab, key_vectors, value_vectors)
+    bias = block_bias(doc_ids, lax.axis_index(LINE))
+    kv = exchange(kv_send)
+    queries, _ = lax.optimization_barrier((queries, kv[1]))
     qd_send = local_call(
         pack_qd_kernel, [array(rows, 1024)] * 8, "pack_qd", GRANT, moves(4)
     )(tab, queries, output_gradient)
-    bias = block_bias(doc_ids, lax.axis_index(LINE))
-
-    kv = exchange(kv_send)
+    kv, _, bias = lax.optimization_barrier((kv, qd_send, bias))
     kv_sib = swap_cores(sibling_in(tab, *kv))
     halo_send = local_call(
         halo_kernel, [array(8, rows, 256)] * 2, "halo", GRANT, moves(2)
     )(tab, *kv, kv_sib)
     halo = [shifted(x, 1) for x in halo_send]
-    out, own, other = [], [], []
+    qd_send = [lax.optimization_barrier((qd_send[:4], halo_send))[0], lax.optimization_barrier((qd_send[4:], halo_send))[0]]
+    received, own, other = [], [], []
     for chunk in range(2):
-        qd = exchange(qd_send[4 * chunk : 4 * chunk + 4])
+        qd = exchange(qd_send[chunk])
+        if chunk == 1:
+            qd, own = lax.optimization_barrier((qd, own))
         qd_sib = swap_cores(sibling_in(tab, *qd))
         pieces, g_halo, g_own = attend(chunk, tab, bias, qd, qd_sib, kv, kv_sib, halo[chunk])
-        received = exchange(pieces)
-        out += [*received, swap_cores(sibling_out(tab, *received))]
+        if chunk == 1:
+            received[0], g_own = lax.optimization_barrier((received[0], g_own))
+            sent = sibling_out(tab, *received[0])
+            pieces, g_halo, _ = lax.optimization_barrier((pieces, g_halo, sent))
+        received.append(exchange(pieces))
         own.append(g_own)
         other.append(shifted(g_halo, -1))
+    out = [*received[0], swap_cores(sent), *received[1]]
+    out.append(swap_cores(sibling_out(tab, *received[1])))
     attn_out, query_grad = local_call(
         unpack_out_kernel, [array(rows, 4096)] * 2, "unpack_out", GRANT, moves(4)
     )(tab, *out)

time: 140 us -> 123 us (0.88)
  waiting for transfers between devices: 47.7 us -> 30.4 us
  Pallas kernels: 38.4 us -> 36.7 us
  starting transfers between devices: 47.8 us -> 49.4 us
    ppermute x18, waiting for transfers between devices: 34.6 us -> 22.3 us  [ring_shift(): return lax.ppermute(x, RING, pairs)]
    ppermute x4, waiting for transfers between devices: 13.1 us -> 6.2 us  [shifted(): return lax.ppermute(x, LINE, pairs)]
    ppermute x4, starting transfers between devices: 14.6 us -> 17.2 us  [shifted(): return lax.ppermute(x, LINE, pairs)]
    ppermute x6, waiting for transfers between devices: 0.02 us -> 1.91 us  [swap_cores(): return lax.ppermute(x, 'core', [(0, 1), (1, 0)])]
    pallas_call x14, Pallas kernels: 38.4 us -> 36.7 us  [call(): pl.pallas_call(kernel, out_shape=out_shape, in_specs=[pl.BlockSpec(memory...]
    unnamed x14 -> x10, local copies, waits for them, and re-layouts: 3.48 us -> 3.32 us
  transfers between devices with their start and end apart: 28 -> 28, of which waited for: 13 -> 10; matrix products, arithmetic and copies ran while one was open for 0% -> 0% of each run, Pallas kernels for 25% -> 27%
where the time goes in v3:
time: 123 us; the launch traced here: 121 us
  starting transfers between devices  49.4 us (40%)
  Pallas kernels  36.7 us (30%)
  waiting for transfers between devices  30.4 us (25%)
  local copies, waits for them, and re-layouts  3.65 us (3%)
  between operations  1.23 us (1%)
    pallas_call x14, Pallas kernels, call(): pl.pallas_call(kernel, out_shape=out_shape, in_specs=[pl.BlockSpec(memory...  36.7 us
    ppermute x18, starting transfers between devices, ring_shift(): return lax.ppermute(x, RING, pairs)  31.3 us
    ppermute x18, waiting for transfers between devices, ring_shift(): return lax.ppermute(x, RING, pairs)  22.3 us
    ppermute x4, starting transfers between devices, shifted(): return lax.ppermute(x, LINE, pairs)  17.2 us
    ppermute x4, waiting for transfers between devices, shifted(): return lax.ppermute(x, LINE, pairs)  6.2 us
    unnamed x10, local copies, waits for them, and re-layouts  3.32 us
  transfers between devices with their start and end apart: 28, of which 10 were waited for; matrix products, arithmetic and copies ran while one was open for 0% of the time, Pallas kernels for 27%

profile of v3, /device:TPU:6, one launch (start us, length us, event | category | flops | bytes accessed | tf_op | source)
XLA Modules:
  0.0 121.5 jit_solution(2660101727861937086)
XLA Ops:
  1.0 0.1 stack.36.tab
  1.1 1.0 copy-done.2
  2.1 1.0 copy-done.3
  3.2 0.8 pack_kv.1
  4.0 1.7 %collective-permute-start = (bf16[128,1024]{1,0:T(8,128)(2,1)S(1)}, bf16[128,1024]{1,0:T(8,128)(2,1)S(1)}, u32[]{:S(2)}, u32[]{:S(2)}) collective-permute-start(bf16[128,1024]{1,0:T(8,128)(2,1)S(1)} %get-tuple-element.68), channel_id=1, source_target_pairs={{0,4},{1,5},{2,6},{3,7},{4,2},{5,3},{6,0},{7,1},{8,12},{9,13},{10,... | collective-permute-start | bytes 786440 | tf_op jit(solution)/shard_map/ppermute | solution.py:318
  5.6 2.9 %collective-permute-start.1 = (bf16[128,1024]{1,0:T(8,128)(2,1)S(1)}, bf16[128,1024]{1,0:T(8,128)(2,1)S(1)}, u32[]{:S(2)}, u32[]{:S(2)}) collective-permute-start(bf16[128,1024]{1,0:T(8,128)(2,1)S(1)} %get-tuple-element.69), channel_id=1, source_target_pairs={{0,2},{1,3},{2,0},{3,1},{4,6},{5,7},{6,4},{7,5},{8,10},{9,11},{10,... | collective-permute-start | bytes 786440 | tf_op jit(solution)/shard_map/ppermute | solution.py:318
  8.5 1.4 %collective-permute-start.2 = (bf16[128,1024]{1,0:T(8,128)(2,1)S(1)}, bf16[128,1024]{1,0:T(8,128)(2,1)S(1)}, u32[]{:S(2)}, u32[]{:S(2)}) collective-permute-start(bf16[128,1024]{1,0:T(8,128)(2,1)S(1)} %get-tuple-element.70), channel_id=1, source_target_pairs={{0,6},{1,7},{2,4},{3,5},{4,0},{5,1},{6,2},{7,3},{8,14},{9,15},{10,... | collective-permute-start | bytes 786440 | tf_op jit(solution)/shard_map/ppermute | solution.py:318
  9.9 0.1 slice_reduce_fusion
  10.0 0.1 slice_reduce_fusion.1
  10.1 0.1 fusion.3
  10.2 3.2 %collective-permute-done.p1.refs_6_ = bf16[128,1024]{1,0:T(8,128)(2,1)S(1)} collective-permute-done((bf16[128,1024]{1,0:T(8,128)(2,1)S(1)}, bf16[128,1024]{1,0:T(8,128)(2,1)S(1)}, u32[]{:S(2)}, u32[]{:S(2)}) %collective-permute-start) | collective-permute-done | bytes 262176 | tf_op jit(solution)/shard_map/ppermute | solution.py:318
  13.4 1.2 %copy-done.1 = bf16[128,4096]{1,0:T(8,128)(2,1)S(1)} copy-done((bf16[128,4096]{1,0:T(8,128)(2,1)S(1)}, bf16[128,4096]{1,0:T(8,128)(2,1)}, u32[]{:S(2)}) %copy-start.1) | copy-done | bytes 1048600
  14.6 0.8 pack_qd.1
  15.4 4.7 %collective-permute-done.1.p2.refs_7_ = bf16[128,1024]{1,0:T(8,128)(2,1)S(1)} collective-permute-done((bf16[128,1024]{1,0:T(8,128)(2,1)S(1)}, bf16[128,1024]{1,0:T(8,128)(2,1)S(1)}, u32[]{:S(2)}, u32[]{:S(2)}) %collective-permute-start.1) | collective-permute-done | bytes 262176 | tf_op jit(solution)/shard_map/ppermute | solution.py:318
  20.2 0.6 to_sibling_in.3
  20.8 0.1 collective-permute-start.3
  20.9 1.9 %collective-permute-done.3.sib.refs_9_ = bf16[4,128,512]{2,1,0:T(8,128)(2,1)S(1)} collective-permute-done((bf16[4,128,512]{2,1,0:T(8,128)(2,1)S(1)}, bf16[4,128,512]{2,1,0:T(8,128)(2,1)S(1)}, u32[]{:S(2)}, u32[]{:S(2)}) %collective-permute-start.3) | collective-permute-done | bytes 524320 | tf_op jit(solution)/shard_map/ppermute | solution.py:334
  22.8 0.6 halo.1
  23.4 1.3 %collective-permute-start.4 = (bf16[128,1024]{1,0:T(8,128)(2,1)S(1)}, bf16[128,1024]{1,0:T(8,128)(2,1)S(1)}, u32[]{:S(2)}, u32[]{:S(2)}) collective-permute-start(bf16[128,1024]{1,0:T(8,128)(2,1)S(1)} %get-tuple-element.88), channel_id=1, source_target_pairs={{0,4},{1,5},{2,6},{3,7},{4,2},{5,3},{6,0},{7,1},{8,12},{9,13},{10,... | collective-permute-start | bytes 786440 | tf_op jit(solution)/shard_map/ppermute | solution.py:318
  24.7 2.4 %collective-permute-start.5 = (bf16[128,1024]{1,0:T(8,128)(2,1)S(1)}, bf16[128,1024]{1,0:T(8,128)(2,1)S(1)}, u32[]{:S(2)}, u32[]{:S(2)}) collective-permute-start(bf16[128,1024]{1,0:T(8,128)(2,1)S(1)} %get-tuple-element.89), channel_id=1, source_target_pairs={{0,2},{1,3},{2,0},{3,1},{4,6},{5,7},{6,4},{7,5},{8,10},{9,11},{10,... | collective-permute-start | bytes 786440 | tf_op jit(solution)/shard_map/ppermute | solution.py:318
  27.1 1.8 %collective-permute-start.6 = (bf16[128,1024]{1,0:T(8,128)(2,1)S(1)}, bf16[128,1024]{1,0:T(8,128)(2,1)S(1)}, u32[]{:S(2)}, u32[]{:S(2)}) collective-permute-start(bf16[128,1024]{1,0:T(8,128)(2,1)S(1)} %get-tuple-element.90), channel_id=1, source_target_pairs={{0,6},{1,7},{2,4},{3,5},{4,0},{5,1},{6,2},{7,3},{8,14},{9,15},{10,... | collective-permute-start | bytes 786440 | tf_op jit(solution)/shard_map/ppermute | solution.py:318
  28.9 3.8 %collective-permute-start.8 = (bf16[8,128,256]{2,1,0:T(8,128)(2,1)S(1)}, bf16[8,128,256]{2,1,0:T(8,128)(2,1)S(1)}, u32[]{:S(2)}, u32[]{:S(2)}) collective-permute-start(bf16[8,128,256]{2,1,0:T(8,128)(2,1)S(1)} %get-tuple-element.85), channel_id=1, source_target_pairs={{0,8},{8,16},{16,24},{24,32},{32,40},{40,48},{48,56},{56,64},{64,7... | collective-permute-start | bytes 1572872 | tf_op jit(solution)/shard_map/ppermute | solution.py:340
  32.7 0.7 collective-permute-done.4.p1.refs_1_
  33.4 5.6 %collective-permute-done.5.p2.refs_2_ = bf16[128,1024]{1,0:T(8,128)(2,1)S(1)} collective-permute-done((bf16[128,1024]{1,0:T(8,128)(2,1)S(1)}, bf16[128,1024]{1,0:T(8,128)(2,1)S(1)}, u32[]{:S(2)}, u32[]{:S(2)}) %collective-permute-start.5) | collective-permute-done | bytes 262176 | tf_op jit(solution)/shard_map/ppermute | solution.py:318
  39.0 0.2 collective-permute-done.6.p3.refs_3_
  39.3 0.6 to_sibling_in.4
  39.9 0.1 collective-permute-start.7
  40.0 3.8 %collective-permute-start.16 = (bf16[8,128,256]{2,1,0:T(8,128)(2,1)S(1)}, bf16[8,128,256]{2,1,0:T(8,128)(2,1)S(1)}, u32[]{:S(2)}, u32[]{:S(2)}) collective-permute-start(bf16[8,128,256]{2,1,0:T(8,128)(2,1)S(1)} %get-tuple-element.86), channel_id=1, source_target_pairs={{0,8},{8,16},{16,24},{24,32},{32,40},{40,48},{48,56},{56,64},{64,7... | collective-permute-start | bytes 1572872 | tf_op jit(solution)/shard_map/ppermute | solution.py:340
  43.8 1.8 %collective-permute-start.12 = (bf16[128,1024]{1,0:T(8,128)(2,1)S(1)}, bf16[128,1024]{1,0:T(8,128)(2,1)S(1)}, u32[]{:S(2)}, u32[]{:S(2)}) collective-permute-start(bf16[128,1024]{1,0:T(8,128)(2,1)S(1)} %get-tuple-element.96), channel_id=1, source_target_pairs={{0,4},{1,5},{2,6},{3,7},{4,2},{5,3},{6,0},{7,1},{8,12},{9,13},{10,... | collective-permute-start | bytes 786440 | tf_op jit(solution)/shard_map/ppermute | solution.py:318
  45.6 2.4 %collective-permute-start.13 = (bf16[128,1024]{1,0:T(8,128)(2,1)S(1)}, bf16[128,1024]{1,0:T(8,128)(2,1)S(1)}, u32[]{:S(2)}, u32[]{:S(2)}) collective-permute-start(bf16[128,1024]{1,0:T(8,128)(2,1)S(1)} %get-tuple-element.97), channel_id=1, source_target_pairs={{0,2},{1,3},{2,0},{3,1},{4,6},{5,7},{6,4},{7,5},{8,10},{9,11},{10,... | collective-permute-start | bytes 786440 | tf_op jit(solution)/shard_map/ppermute | solution.py:318
  48.0 0.4 collective-permute-done.8.refs_10_
  48.3 1.0 collective-permute-start.14
  49.3 0.0 collective-permute-done.7.refs_4_
  49.3 13.1 %attend_0.1 = (bf16[256,512]{1,0:T(8,128)(2,1)S(1)}, bf16[256,512]{1,0:T(8,128)(2,1)S(1)}, bf16[256,512]{1,0:T(8,128)(2,1)S(1)}, bf16[256,512]{1,0:T(8,128)(2,1)...) custom-call(s32[9]{0:T(128)S(1)} %stack.36.tab, f32[8,128]{1,0:T(8,128)S(1)} %pad.5.bias_ref, ...), custom_call_target="tpu_custom_call" | custom-call | flops 14000000000 | bytes 4194304 | tf_op jit(solution)/shard_map/attend_0/pallas_call | solution.py:47
  62.4 0.0 collective-permute-done.12.p1.refs_1_
  62.5 0.0 collective-permute-done.14.p3.refs_3_
  62.5 0.6 to_sibling_in.5
  63.1 0.1 collective-permute-start.15
  63.2 1.1 collective-permute-start.9
  64.3 0.8 collective-permute-start.10
  65.1 2.1 %collective-permute-start.11 = (bf16[256,512]{1,0:T(8,128)(2,1)S(1)}, bf16[256,512]{1,0:T(8,128)(2,1)S(1)}, u32[]{:S(2)}, u32[]{:S(2)}) collective-permute-start(bf16[256,512]{1,0:T(8,128)(2,1)S(1)} %get-tuple-element.94), channel_id=1, source_target_pairs={{0,6},{1,7},{2,4},{3,5},{4,0},{5,1},{6,2},{7,3},{8,14},{9,15},{10,... | collective-permute-start | bytes 786440 | tf_op jit(solution)/shard_map/ppermute | solution.py:318
  67.1 0.0 collective-permute-done.16.refs_10_
  67.1 5.7 %collective-permute-start.22 = (bf16[1024,256]{1,0:T(8,128)(2,1)S(1)}, bf16[1024,256]{1,0:T(8,128)(2,1)S(1)}, u32[]{:S(2)}, u32[]{:S(2)}) collective-permute-start(bf16[1024,256]{1,0:T(8,128)(2,1)S(1)} %get-tuple-element.122), channel_id=1, source_target_pairs={{8,0},{16,8},{24,16},{32,24},{40,32},{48,40},{56,48},{64,56},{72,6... | collective-permute-start | bytes 1572872 | tf_op jit(solution)/shard_map/ppermute | solution.py:340
  72.8 13.1 %attend_1.1 = (bf16[256,512]{1,0:T(8,128)(2,1)S(1)}, bf16[256,512]{1,0:T(8,128)(2,1)S(1)}, bf16[256,512]{1,0:T(8,128)(2,1)S(1)}, bf16[256,512]{1,0:T(8,128)(2,1)...) custom-call(s32[9]{0:T(128)S(1)} %stack.36.tab, f32[8,128]{1,0:T(8,128)S(1)} %pad.5.bias_ref, ...), custom_call_target="tpu_custom_call" | custom-call | flops 14000000000 | bytes 4194304 | tf_op jit(solution)/shard_map/attend_1/pallas_call | solution.py:47
  86.0 0.0 collective-permute-done.11.p3.refs_3_
  86.0 0.6 to_sibling_out.3
  86.6 3.9 %collective-permute-start.23 = (bf16[1024,256]{1,0:T(8,128)(2,1)S(1)}, bf16[1024,256]{1,0:T(8,128)(2,1)S(1)}, u32[]{:S(2)}, u32[]{:S(2)}) collective-permute-start(bf16[1024,256]{1,0:T(8,128)(2,1)S(1)} %get-tuple-element.123), channel_id=1, source_target_pairs={{8,0},{16,8},{24,16},{32,24},{40,32},{48,40},{56,48},{64,56},{72,6... | collective-permute-start | bytes 1572872 | tf_op jit(solution)/shard_map/ppermute | solution.py:340
  90.5 0.7 collective-permute-start.18
  91.3 2.2 %collective-permute-start.19 = (bf16[256,512]{1,0:T(8,128)(2,1)S(1)}, bf16[256,512]{1,0:T(8,128)(2,1)S(1)}, u32[]{:S(2)}, u32[]{:S(2)}) collective-permute-start(bf16[256,512]{1,0:T(8,128)(2,1)S(1)} %get-tuple-element.116), channel_id=1, source_target_pairs={{0,2},{1,3},{2,0},{3,1},{4,6},{5,7},{6,4},{7,5},{8,10},{9,11},{10,... | collective-permute-start | bytes 786440 | tf_op jit(solution)/shard_map/ppermute | solution.py:318
  93.4 2.5 %collective-permute-start.20 = (bf16[256,512]{1,0:T(8,128)(2,1)S(1)}, bf16[256,512]{1,0:T(8,128)(2,1)S(1)}, u32[]{:S(2)}, u32[]{:S(2)}) collective-permute-start(bf16[256,512]{1,0:T(8,128)(2,1)S(1)} %get-tuple-element.117), channel_id=1, source_target_pairs={{0,6},{1,7},{2,4},{3,5},{4,0},{5,1},{6,2},{7,3},{8,14},{9,15},{10,... | collective-permute-start | bytes 786440 | tf_op jit(solution)/shard_map/ppermute | solution.py:318
  96.0 5.8 %collective-permute-done.23.from1 = bf16[1024,256]{1,0:T(8,128)(2,1)S(1)} collective-permute-done((bf16[1024,256]{1,0:T(8,128)(2,1)S(1)}, bf16[1024,256]{1,0:T(8,128)(2,1)S(1)}, u32[]{:S(2)}, u32[]{:S(2)}) %collective-permute-start.23) | collective-permute-done | bytes 524320 | tf_op jit(solution)/shard_map/ppermute | solution.py:340
  101.8 0.8 merge.1
  102.6 0.8 collective-permute-start.24
  103.4 1.9 %collective-permute-start.25 = (bf16[256,512]{1,0:T(8,128)(2,1)S(1)}, bf16[256,512]{1,0:T(8,128)(2,1)S(1)}, u32[]{:S(2)}, u32[]{:S(2)}) collective-permute-start(bf16[256,512]{1,0:T(8,128)(2,1)S(1)} %get-tuple-element.126), channel_id=1, source_target_pairs={{0,2},{1,3},{2,0},{3,1},{4,6},{5,7},{6,4},{7,5},{8,10},{9,11},{10,... | collective-permute-start | bytes 786440 | tf_op jit(solution)/shard_map/ppermute | solution.py:318
  105.3 0.0 collective-permute-done.18.p1.refs_6_
  105.3 2.5 %collective-permute-start.26 = (bf16[256,512]{1,0:T(8,128)(2,1)S(1)}, bf16[256,512]{1,0:T(8,128)(2,1)S(1)}, u32[]{:S(2)}, u32[]{:S(2)}) collective-permute-start(bf16[256,512]{1,0:T(8,128)(2,1)S(1)} %get-tuple-element.127), channel_id=1, source_target_pairs={{0,6},{1,7},{2,4},{3,5},{4,0},{5,1},{6,2},{7,3},{8,14},{9,15},{10,... | collective-permute-start | bytes 786440 | tf_op jit(solution)/shard_map/ppermute | solution.py:318
  107.8 0.6 to_sibling_out.4
  108.4 0.6 collective-permute-start.21
  109.0 7.2 %collective-permute-done.24.p1 = bf16[256,512]{1,0:T(8,128)(2,1)S(1)} collective-permute-done((bf16[256,512]{1,0:T(8,128)(2,1)S(1)}, bf16[256,512]{1,0:T(8,128)(2,1)S(1)}, u32[]{:S(2)}, u32[]{:S(2)}) %collective-permute-start.24) | collective-permute-done | bytes 262176 | tf_op jit(solution)/shard_map/ppermute | solution.py:318
  116.2 0.6 collective-permute-done.26.p3
  116.8 0.6 to_sibling_out.5
  117.4 0.1 collective-permute-start.27
  117.6 2.1 %unpack_out.1 = (bf16[128,4096]{1,0:T(8,128)(2,1)}, bf16[128,4096]{1,0:T(8,128)(2,1)}) custom-call(s32[9]{0:T(128)S(1)} %stack.36.tab, bf16[256,512]{1,0:T(8,128)(2,1)S(1)} %get-tuple-element.105.p0.refs_0_, bf16[256,512]{1,0:T(8,128)(2,1)S(1)} %collective-permute-done.9.p1.refs_1_, bf16[256,512]{1,0:T(8,128)(2,1)S(1)} %collective-permute-done.10.p2.refs_2_, ...), custom_call_target="tpu_custom_call" | custom-call | bytes 4194304 | tf_op jit(solution)/shard_map/unpack_out/pallas_call | solution.py:47
  119.7 1.8 %unpack_kv.1 = (bf16[128,2048]{1,0:T(8,128)(2,1)}, bf16[128,2048]{1,0:T(8,128)(2,1)}) custom-call(s32[9]{0:T(128)S(1)} %stack.36.tab, bf16[256,512]{1,0:T(8,128)(2,1)S(1)} %get-tuple-element.124.p0, bf16[256,512]{1,0:T(8,128)(2,1)S(1)} %collective-permute-done.24.p1, bf16[256,512]{1,0:T(8,128)(2,1)S(1)} %collective-permute-done.25.p2, ...), custom_call_target="tpu_custom_call" | custom-call | bytes 2097152 | tf_op jit(solution)/shard_map/unpack_kv/pallas_call | solution.py:47
  (23 shorter events, 0.1 us)
Async XLA Ops:
  0.6 12.7 %copy-start = (bf16[128,4096]{1,0:T(8,128)(2,1)S(1)}, bf16[128,4096]{1,0:T(8,128)(2,1)}, u32[]{:S(2)}) copy-start(bf16[128,4096]{1,0:T(8,128)(2,1)} %q_ref) | copy-start | bytes 3145732
  1.1 1.0 copy-start.2
  2.1 1.0 copy-start.3
  3.2 6.7 %copy-start.4 = (s32[32768]{0:T(1024)S(1)}, s32[32768]{0:T(1024)}, u32[]{:S(2)}) copy-start(s32[32768]{0:T(1024)} %param.9) | copy-start | bytes 393220
  4.0 9.4 %collective-permute-start = (bf16[128,1024]{1,0:T(8,128)(2,1)S(1)}, bf16[128,1024]{1,0:T(8,128)(2,1)S(1)}, u32[]{:S(2)}, u32[]{:S(2)}) collective-permute-start(bf16[128,1024]{1,0:T(8,128)(2,1)S(1)} %get-tuple-element.68), channel_id=1, source_target_pairs={{0,4},{1,5},{2,6},{3,7},{4,2},{5,3},{6,0},{7,1},{8,12},{9,13},{10,... | collective-permute-start | bytes 786440 | tf_op jit(solution)/shard_map/ppermute | solution.py:318
  5.6 14.5 %collective-permute-start.1 = (bf16[128,1024]{1,0:T(8,128)(2,1)S(1)}, bf16[128,1024]{1,0:T(8,128)(2,1)S(1)}, u32[]{:S(2)}, u32[]{:S(2)}) collective-permute-start(bf16[128,1024]{1,0:T(8,128)(2,1)S(1)} %get-tuple-element.69), channel_id=1, source_target_pairs={{0,2},{1,3},{2,0},{3,1},{4,6},{5,7},{6,4},{7,5},{8,10},{9,11},{10,... | collective-permute-start | bytes 786440 | tf_op jit(solution)/shard_map/ppermute | solution.py:318
  8.5 11.6 %collective-permute-start.2 = (bf16[128,1024]{1,0:T(8,128)(2,1)S(1)}, bf16[128,1024]{1,0:T(8,128)(2,1)S(1)}, u32[]{:S(2)}, u32[]{:S(2)}) collective-permute-start(bf16[128,1024]{1,0:T(8,128)(2,1)S(1)} %get-tuple-element.70), channel_id=1, source_target_pairs={{0,6},{1,7},{2,4},{3,5},{4,0},{5,1},{6,2},{7,3},{8,14},{9,15},{10,... | collective-permute-start | bytes 786440 | tf_op jit(solution)/shard_map/ppermute | solution.py:318
  13.4 1.2 %copy-start.1 = (bf16[128,4096]{1,0:T(8,128)(2,1)S(1)}, bf16[128,4096]{1,0:T(8,128)(2,1)}, u32[]{:S(2)}) copy-start(bf16[128,4096]{1,0:T(8,128)(2,1)} %d_ref.1) | copy-start | bytes 3145732
  20.8 2.0 %collective-permute-start.3 = (bf16[4,128,512]{2,1,0:T(8,128)(2,1)S(1)}, bf16[4,128,512]{2,1,0:T(8,128)(2,1)S(1)}, u32[]{:S(2)}, u32[]{:S(2)}) collective-permute-start(bf16[4,128,512]{2,1,0:T(8,128)(2,1)S(1)} %to_sibling_in.3), channel_id=1, source_target_pairs={{0,1},{1,0},{2,3},{3,2},{4,5},{5,4},{6,7},{7,6},{8,9},{9,8},{10,11... | collective-permute-start | bytes 1572872 | tf_op jit(solution)/shard_map/ppermute | solution.py:334
  23.4 10.0 %collective-permute-start.4 = (bf16[128,1024]{1,0:T(8,128)(2,1)S(1)}, bf16[128,1024]{1,0:T(8,128)(2,1)S(1)}, u32[]{:S(2)}, u32[]{:S(2)}) collective-permute-start(bf16[128,1024]{1,0:T(8,128)(2,1)S(1)} %get-tuple-element.88), channel_id=1, source_target_pairs={{0,4},{1,5},{2,6},{3,7},{4,2},{5,3},{6,0},{7,1},{8,12},{9,13},{10,... | collective-permute-start | bytes 786440 | tf_op jit(solution)/shard_map/ppermute | solution.py:318
  24.7 14.3 %collective-permute-start.5 = (bf16[128,1024]{1,0:T(8,128)(2,1)S(1)}, bf16[128,1024]{1,0:T(8,128)(2,1)S(1)}, u32[]{:S(2)}, u32[]{:S(2)}) collective-permute-start(bf16[128,1024]{1,0:T(8,128)(2,1)S(1)} %get-tuple-element.89), channel_id=1, source_target_pairs={{0,2},{1,3},{2,0},{3,1},{4,6},{5,7},{6,4},{7,5},{8,10},{9,11},{10,... | collective-permute-start | bytes 786440 | tf_op jit(solution)/shard_map/ppermute | solution.py:318
  27.1 12.2 %collective-permute-start.6 = (bf16[128,1024]{1,0:T(8,128)(2,1)S(1)}, bf16[128,1024]{1,0:T(8,128)(2,1)S(1)}, u32[]{:S(2)}, u32[]{:S(2)}) collective-permute-start(bf16[128,1024]{1,0:T(8,128)(2,1)S(1)} %get-tuple-element.90), channel_id=1, source_target_pairs={{0,6},{1,7},{2,4},{3,5},{4,0},{5,1},{6,2},{7,3},{8,14},{9,15},{10,... | collective-permute-start | bytes 786440 | tf_op jit(solution)/shard_map/ppermute | solution.py:318
  28.9 19.4 %collective-permute-start.8 = (bf16[8,128,256]{2,1,0:T(8,128)(2,1)S(1)}, bf16[8,128,256]{2,1,0:T(8,128)(2,1)S(1)}, u32[]{:S(2)}, u32[]{:S(2)}) collective-permute-start(bf16[8,128,256]{2,1,0:T(8,128)(2,1)S(1)} %get-tuple-element.85), channel_id=1, source_target_pairs={{0,8},{8,16},{16,24},{24,32},{32,40},{40,48},{48,56},{56,64},{64,7... | collective-permute-start | bytes 1572872 | tf_op jit(solution)/shard_map/ppermute | solution.py:340
  39.9 9.5 %collective-permute-start.7 = (bf16[4,128,512]{2,1,0:T(8,128)(2,1)S(1)}, bf16[4,128,512]{2,1,0:T(8,128)(2,1)S(1)}, u32[]{:S(2)}, u32[]{:S(2)}) collective-permute-start(bf16[4,128,512]{2,1,0:T(8,128)(2,1)S(1)} %to_sibling_in.4), channel_id=1, source_target_pairs={{0,1},{1,0},{2,3},{3,2},{4,5},{5,4},{6,7},{7,6},{8,9},{9,8},{10,11... | collective-permute-start | bytes 1572872 | tf_op jit(solution)/shard_map/ppermute | solution.py:334
  40.0 27.2 %collective-permute-start.16 = (bf16[8,128,256]{2,1,0:T(8,128)(2,1)S(1)}, bf16[8,128,256]{2,1,0:T(8,128)(2,1)S(1)}, u32[]{:S(2)}, u32[]{:S(2)}) collective-permute-start(bf16[8,128,256]{2,1,0:T(8,128)(2,1)S(1)} %get-tuple-element.86), channel_id=1, source_target_pairs={{0,8},{8,16},{16,24},{24,32},{32,40},{40,48},{48,56},{56,64},{64,7... | collective-permute-start | bytes 1572872 | tf_op jit(solution)/shard_map/ppermute | solution.py:340
  43.8 18.7 %collective-permute-start.12 = (bf16[128,1024]{1,0:T(8,128)(2,1)S(1)}, bf16[128,1024]{1,0:T(8,128)(2,1)S(1)}, u32[]{:S(2)}, u32[]{:S(2)}) collective-permute-start(bf16[128,1024]{1,0:T(8,128)(2,1)S(1)} %get-tuple-element.96), channel_id=1, source_target_pairs={{0,4},{1,5},{2,6},{3,7},{4,2},{5,3},{6,0},{7,1},{8,12},{9,13},{10,... | collective-permute-start | bytes 786440 | tf_op jit(solution)/shard_map/ppermute | solution.py:318
  45.6 16.9 %collective-permute-start.13 = (bf16[128,1024]{1,0:T(8,128)(2,1)S(1)}, bf16[128,1024]{1,0:T(8,128)(2,1)S(1)}, u32[]{:S(2)}, u32[]{:S(2)}) collective-permute-start(bf16[128,1024]{1,0:T(8,128)(2,1)S(1)} %get-tuple-element.97), channel_id=1, source_target_pairs={{0,2},{1,3},{2,0},{3,1},{4,6},{5,7},{6,4},{7,5},{8,10},{9,11},{10,... | collective-permute-start | bytes 786440 | tf_op jit(solution)/shard_map/ppermute | solution.py:318
  48.3 14.2 %collective-permute-start.14 = (bf16[128,1024]{1,0:T(8,128)(2,1)S(1)}, bf16[128,1024]{1,0:T(8,128)(2,1)S(1)}, u32[]{:S(2)}, u32[]{:S(2)}) collective-permute-start(bf16[128,1024]{1,0:T(8,128)(2,1)S(1)} %get-tuple-element.98), channel_id=1, source_target_pairs={{0,6},{1,7},{2,4},{3,5},{4,0},{5,1},{6,2},{7,3},{8,14},{9,15},{10,... | collective-permute-start | bytes 786440 | tf_op jit(solution)/shard_map/ppermute | solution.py:318
  63.1 9.7 %collective-permute-start.15 = (bf16[4,128,512]{2,1,0:T(8,128)(2,1)S(1)}, bf16[4,128,512]{2,1,0:T(8,128)(2,1)S(1)}, u32[]{:S(2)}, u32[]{:S(2)}) collective-permute-start(bf16[4,128,512]{2,1,0:T(8,128)(2,1)S(1)} %to_sibling_in.5), channel_id=1, source_target_pairs={{0,1},{1,0},{2,3},{3,2},{4,5},{5,4},{6,7},{7,6},{8,9},{9,8},{10,11... | collective-permute-start | bytes 1572872 | tf_op jit(solution)/shard_map/ppermute | solution.py:334
  63.2 22.8 %collective-permute-start.9 = (bf16[256,512]{1,0:T(8,128)(2,1)S(1)}, bf16[256,512]{1,0:T(8,128)(2,1)S(1)}, u32[]{:S(2)}, u32[]{:S(2)}) collective-permute-start(bf16[256,512]{1,0:T(8,128)(2,1)S(1)} %get-tuple-element.92), channel_id=1, source_target_pairs={{0,4},{1,5},{2,6},{3,7},{4,2},{5,3},{6,0},{7,1},{8,12},{9,13},{10,... | collective-permute-start | bytes 786440 | tf_op jit(solution)/shard_map/ppermute | solution.py:318
  64.3 21.7 %collective-permute-start.10 = (bf16[256,512]{1,0:T(8,128)(2,1)S(1)}, bf16[256,512]{1,0:T(8,128)(2,1)S(1)}, u32[]{:S(2)}, u32[]{:S(2)}) collective-permute-start(bf16[256,512]{1,0:T(8,128)(2,1)S(1)} %get-tuple-element.93), channel_id=1, source_target_pairs={{0,2},{1,3},{2,0},{3,1},{4,6},{5,7},{6,4},{7,5},{8,10},{9,11},{10,... | collective-permute-start | bytes 786440 | tf_op jit(solution)/shard_map/ppermute | solution.py:318
  65.1 20.9 %collective-permute-start.11 = (bf16[256,512]{1,0:T(8,128)(2,1)S(1)}, bf16[256,512]{1,0:T(8,128)(2,1)S(1)}, u32[]{:S(2)}, u32[]{:S(2)}) collective-permute-start(bf16[256,512]{1,0:T(8,128)(2,1)S(1)} %get-tuple-element.94), channel_id=1, source_target_pairs={{0,6},{1,7},{2,4},{3,5},{4,0},{5,1},{6,2},{7,3},{8,14},{9,15},{10,... | collective-permute-start | bytes 786440 | tf_op jit(solution)/shard_map/ppermute | solution.py:318
  67.1 28.8 %collective-permute-start.22 = (bf16[1024,256]{1,0:T(8,128)(2,1)S(1)}, bf16[1024,256]{1,0:T(8,128)(2,1)S(1)}, u32[]{:S(2)}, u32[]{:S(2)}) collective-permute-start(bf16[1024,256]{1,0:T(8,128)(2,1)S(1)} %get-tuple-element.122), channel_id=1, source_target_pairs={{8,0},{16,8},{24,16},{32,24},{40,32},{48,40},{56,48},{64,56},{72,6... | collective-permute-start | bytes 1572872 | tf_op jit(solution)/shard_map/ppermute | solution.py:340
  86.6 15.2 %collective-permute-start.23 = (bf16[1024,256]{1,0:T(8,128)(2,1)S(1)}, bf16[1024,256]{1,0:T(8,128)(2,1)S(1)}, u32[]{:S(2)}, u32[]{:S(2)}) collective-permute-start(bf16[1024,256]{1,0:T(8,128)(2,1)S(1)} %get-tuple-element.123), channel_id=1, source_target_pairs={{8,0},{16,8},{24,16},{32,24},{40,32},{48,40},{56,48},{64,56},{72,6... | collective-permute-start | bytes 1572872 | tf_op jit(solution)/shard_map/ppermute | solution.py:340
  90.5 14.8 %collective-permute-start.18 = (bf16[256,512]{1,0:T(8,128)(2,1)S(1)}, bf16[256,512]{1,0:T(8,128)(2,1)S(1)}, u32[]{:S(2)}, u32[]{:S(2)}) collective-permute-start(bf16[256,512]{1,0:T(8,128)(2,1)S(1)} %get-tuple-element.115), channel_id=1, source_target_pairs={{0,4},{1,5},{2,6},{3,7},{4,2},{5,3},{6,0},{7,1},{8,12},{9,13},{10,... | collective-permute-start | bytes 786440 | tf_op jit(solution)/shard_map/ppermute | solution.py:318
  91.3 16.6 %collective-permute-start.19 = (bf16[256,512]{1,0:T(8,128)(2,1)S(1)}, bf16[256,512]{1,0:T(8,128)(2,1)S(1)}, u32[]{:S(2)}, u32[]{:S(2)}) collective-permute-start(bf16[256,512]{1,0:T(8,128)(2,1)S(1)} %get-tuple-element.116), channel_id=1, source_target_pairs={{0,2},{1,3},{2,0},{3,1},{4,6},{5,7},{6,4},{7,5},{8,10},{9,11},{10,... | collective-permute-start | bytes 786440 | tf_op jit(solution)/shard_map/ppermute | solution.py:318
  93.4 14.4 %collective-permute-start.20 = (bf16[256,512]{1,0:T(8,128)(2,1)S(1)}, bf16[256,512]{1,0:T(8,128)(2,1)S(1)}, u32[]{:S(2)}, u32[]{:S(2)}) collective-permute-start(bf16[256,512]{1,0:T(8,128)(2,1)S(1)} %get-tuple-element.117), channel_id=1, source_target_pairs={{0,6},{1,7},{2,4},{3,5},{4,0},{5,1},{6,2},{7,3},{8,14},{9,15},{10,... | collective-permute-start | bytes 786440 | tf_op jit(solution)/shard_map/ppermute | solution.py:318
  102.6 13.7 %collective-permute-start.24 = (bf16[256,512]{1,0:T(8,128)(2,1)S(1)}, bf16[256,512]{1,0:T(8,128)(2,1)S(1)}, u32[]{:S(2)}, u32[]{:S(2)}) collective-permute-start(bf16[256,512]{1,0:T(8,128)(2,1)S(1)} %get-tuple-element.125), channel_id=1, source_target_pairs={{0,4},{1,5},{2,6},{3,7},{4,2},{5,3},{6,0},{7,1},{8,12},{9,13},{10,... | collective-permute-start | bytes 786440 | tf_op jit(solution)/shard_map/ppermute | solution.py:318
  103.4 12.8 %collective-permute-start.25 = (bf16[256,512]{1,0:T(8,128)(2,1)S(1)}, bf16[256,512]{1,0:T(8,128)(2,1)S(1)}, u32[]{:S(2)}, u32[]{:S(2)}) collective-permute-start(bf16[256,512]{1,0:T(8,128)(2,1)S(1)} %get-tuple-element.126), channel_id=1, source_target_pairs={{0,2},{1,3},{2,0},{3,1},{4,6},{5,7},{6,4},{7,5},{8,10},{9,11},{10,... | collective-permute-start | bytes 786440 | tf_op jit(solution)/shard_map/ppermute | solution.py:318
  105.3 11.6 %collective-permute-start.26 = (bf16[256,512]{1,0:T(8,128)(2,1)S(1)}, bf16[256,512]{1,0:T(8,128)(2,1)S(1)}, u32[]{:S(2)}, u32[]{:S(2)}) collective-permute-start(bf16[256,512]{1,0:T(8,128)(2,1)S(1)} %get-tuple-element.127), channel_id=1, source_target_pairs={{0,6},{1,7},{2,4},{3,5},{4,0},{5,1},{6,2},{7,3},{8,14},{9,15},{10,... | collective-permute-start | bytes 786440 | tf_op jit(solution)/shard_map/ppermute | solution.py:318
  107.8 9.7 %collective-permute-start.17 = (bf16[4,128,512]{2,1,0:T(8,128)(2,1)S(1)}, bf16[4,128,512]{2,1,0:T(8,128)(2,1)S(1)}, u32[]{:S(2)}, u32[]{:S(2)}) collective-permute-start(bf16[4,128,512]{2,1,0:T(8,128)(2,1)S(1)} %to_sibling_out.3), channel_id=1, source_target_pairs={{0,1},{1,0},{2,3},{3,2},{4,5},{5,4},{6,7},{7,6},{8,9},{9,8},{10,11... | collective-permute-start | bytes 1572872 | tf_op jit(solution)/shard_map/ppermute | solution.py:334
  108.4 9.1 %collective-permute-start.21 = (bf16[4,128,512]{2,1,0:T(8,128)(2,1)S(1)}, bf16[4,128,512]{2,1,0:T(8,128)(2,1)S(1)}, u32[]{:S(2)}, u32[]{:S(2)}) collective-permute-start(bf16[4,128,512]{2,1,0:T(8,128)(2,1)S(1)} %to_sibling_out.4), channel_id=1, source_target_pairs={{0,1},{1,0},{2,3},{3,2},{4,5},{5,4},{6,7},{7,6},{8,9},{9,8},{10,11... | collective-permute-start | bytes 1572872 | tf_op jit(solution)/shard_map/ppermute | solution.py:334
  117.4 2.2 %collective-permute-start.27 = (bf16[4,128,512]{2,1,0:T(8,128)(2,1)S(1)}, bf16[4,128,512]{2,1,0:T(8,128)(2,1)S(1)}, u32[]{:S(2)}, u32[]{:S(2)}) collective-permute-start(bf16[4,128,512]{2,1,0:T(8,128)(2,1)S(1)} %to_sibling_out.5), channel_id=1, source_target_pairs={{0,1},{1,0},{2,3},{3,2},{4,5},{5,4},{6,7},{7,6},{8,9},{9,8},{10,11... | collective-permute-start | bytes 1572872 | tf_op jit(solution)/shard_map/ppermute | solution.py:334

commit v4 on v3

--- a/solution.py
+++ b/solution.py
@@ -216,50 +216,73 @@
     s_pos = lax.broadcasted_iota(jnp.int32, (TILE, TILE), 0)
     t_pos = lax.broadcasted_iota(jnp.int32, (TILE, TILE), 1)
     far = s_pos > t_pos
-    top8 = jnp.full((8, 2 * TILE), NEG, f32)
+    heads = [slice(TILE * h, TILE * (h + 1)) for h in range(2)]
+    steps = [slice(TILE * j, TILE * (j + 1)) for j in range(5)]
+
+    def score(h, j, top8):
+        s = dot(kaug[pl.ds(base + TILE * j, TILE), :], qaug[heads[h], :], NT)
+        if j == 0:
+            s = jnp.where(far, s, NEG)
+        if j == 4:
+            s = jnp.where(far, NEG, s)
+        s_ref[steps[j], heads[h]] = s
+        return jnp.maximum(top8, jnp.max(s.reshape(TILE // 8, 8, TILE), axis=0))
+
+    def exponentiate(h, j, top):
+        e_ref[steps[j], heads[h]] = jnp.exp2(
+            (s_ref[steps[j], heads[h]] - top) * exp2_scale
+        ).astype(bf16)
+
+    def normalize(h, ot):
+        r = 1.0 / ot[128:129, :]
+        attended = (ot[0:128, :] * r).T.astype(bf16)
+        out_ref[:, 128 * h : 128 * (h + 1)] = attended
+        r_rows = jnp.broadcast_to(r, (128, TILE)).T
+        grad = qd_ref[:, 256 + 128 * h : 384 + 128 * h]
+        grad_n = (grad.astype(f32) * r_rows).astype(bf16)
+        delta = jnp.sum(grad_n.astype(f32) * attended.astype(f32), axis=1, keepdims=True)
+        minus = jnp.broadcast_to(-delta, (TILE, 128))
+        part0 = minus.astype(bf16).astype(f32)
+        part1 = (minus - part0).astype(bf16).astype(f32)
+        part2 = minus - part0 - part1
+        lane = lax.broadcasted_iota(jnp.int32, (TILE, 128), 1)
+        parts = jnp.where(
+            lane == 0, part0, jnp.where(lane == 1, part1, jnp.where(lane == 2, part2, 0.0))
+        )
+        doaug[heads[h], 0:128] = grad_n
+        doaug[heads[h], 128:256] = parts.astype(bf16)
+
+    def score_gradient(h, j):
+        dp = dot(vaug[pl.ds(base + TILE * j, TILE), :], doaug[heads[h], :], NT)
+        d_ref[steps[j], heads[h]] = (e_ref[steps[j], heads[h]].astype(f32) * dp).astype(bf16)
+
+    def query_gradient(h):
+        dq = (dot(kt[:, window], d_ref[:, heads[h]]) * score_scale).T.astype(bf16)
+        out_ref[:, 256 + 128 * h : 384 + 128 * h] = dq
+
+    lowest = jnp.full((8, TILE), NEG, f32)
+    top8 = lowest
     for j in range(5):
-        s = dot(kaug[pl.ds(base + TILE * j, TILE), :], qaug[...], NT)
-        if j in (0, 4):
-            keep = far if j == 0 else jnp.logical_not(far)
-            s = jnp.concatenate(
-                [jnp.where(keep, s[:, :TILE], NEG), jnp.where(keep, s[:, TILE:], NEG)], axis=1
-            )
-        s_ref[TILE * j : TILE * (j + 1), :] = s
-        top8 = jnp.maximum(top8, jnp.max(s.reshape(TILE // 8, 8, 2 * TILE), axis=0))
-    top = jnp.max(top8, axis=0, keepdims=True)
+        top8 = score(0, j, top8)
+    top0 = jnp.max(top8, axis=0, keepdims=True)
+    top8 = lowest
     for j in range(5):
-        rows = slice(TILE * j, TILE * (j + 1))
-        e_ref[rows, :] = jnp.exp2((s_ref[rows, :] - top) * exp2_scale).astype(bf16)
-
-    ot = dot(v1t[:, window], e_ref[...])
-    r = 1.0 / ot[128:129, :]
-    attended = (ot[0:128, :] * r).T.astype(bf16)
-    r_rows = jnp.broadcast_to(r, (128, 2 * TILE)).T
-    grad = jnp.concatenate([qd_ref[:, 256:384], qd_ref[:, 384:512]], axis=0)
-    grad_n = (grad.astype(f32) * r_rows).astype(bf16)
-    delta = jnp.sum(grad_n.astype(f32) * attended.astype(f32), axis=1, keepdims=True)
-    minus = jnp.broadcast_to(-delta, (2 * TILE, 128))
-    part0 = minus.astype(bf16).astype(f32)
-    part1 = (minus - part0).astype(bf16).astype(f32)
-    part2 = minus - part0 - part1
-    lane = lax.broadcasted_iota(jnp.int32, (2 * TILE, 128), 1)
-    parts = jnp.where(
-        lane == 0, part0, jnp.where(lane == 1, part1, jnp.where(lane == 2, part2, 0.0))
-    )
-    doaug[:, 0:128] = grad_n
-    doaug[:, 128:256] = parts.astype(bf16)
-    for h in range(2):
-        out_ref[:, 128 * h : 128 * (h + 1)] = attended[TILE * h : TILE * (h + 1), :]
-
+        top8 = score(1, j, top8)
+        exponentiate(0, j, top0)
+    top1 = jnp.max(top8, axis=0, keepdims=True)
+    ot0 = dot(v1t[:, window], e_ref[:, heads[0]])
     for j in range(5):
-        rows = slice(TILE * j, TILE * (j + 1))
-        dp = dot(vaug[pl.ds(base + TILE * j, TILE), :], doaug[...], NT)
-        d_ref[rows, :] = (e_ref[rows, :].astype(f32) * dp).astype(bf16)
-
-    dq = (dot(kt[:, window], d_ref[...]) * score_scale).T.astype(bf16)
-    for h in range(2):
-        out_ref[:, 256 + 128 * h : 384 + 128 * h] = dq[TILE * h : TILE * (h + 1), :]
+        exponentiate(1, j, top1)
+    normalize(0, ot0)
+    ot1 = dot(v1t[:, window], e_ref[:, heads[1]])
+    for j in range(5):
+        score_gradient(0, j)
+    normalize(1, ot1)
+    query_gradient(0)
+    for j in range(5):
+        score_gradient(1, j)
     dv = dot(e_ref[...], doaug[:, 0:128])
+    query_gradient(1)
     dk = dot(d_ref[...], qaug[:, 0:128])
 
     dk_acc[window, :] = dk_acc[window, :] + dk

time: 123 us -> 121 us (0.984)
  transfers between devices with their start and end apart: 28 -> 28, of which waited for: 10 -> 10; matrix products, arithmetic and copies ran while one was open for 0% -> 0% of each run, Pallas kernels for 27% -> 26%
where the time goes in v4:
time: 121 us; the launch traced here: 120 us
  starting transfers between devices  49.5 us (41%)
  Pallas kernels  35.5 us (29%)
  waiting for transfers between devices  30.2 us (25%)
  local copies, waits for them, and re-layouts  3.65 us (3%)
  between operations  1.23 us (1%)
    pallas_call x14, Pallas kernels, call(): pl.pallas_call(kernel, out_shape=out_shape, in_specs=[pl.BlockSpec(memory...  35.5 us
    ppermute x18, starting transfers between devices, ring_shift(): return lax.ppermute(x, RING, pairs)  31.3 us
    ppermute x18, waiting for transfers between devices, ring_shift(): return lax.ppermute(x, RING, pairs)  22.1 us
    ppermute x4, starting transfers between devices, shifted(): return lax.ppermute(x, LINE, pairs)  17.2 us
    ppermute x4, waiting for transfers between devices, shifted(): return lax.ppermute(x, LINE, pairs)  6.2 us
    unnamed x10, local copies, waits for them, and re-layouts  3.32 us
  transfers between devices with their start and end apart: 28, of which 10 were waited for; matrix products, arithmetic and copies ran while one was open for 0% of the time, Pallas kernels for 26%

profile of v4, /device:TPU:6, one launch (start us, length us, event | category | flops | bytes accessed | tf_op | source)
XLA Modules:
  0.0 120.2 jit_solution(12873851522116532271)
XLA Ops:
  1.0 0.1 stack.36.tab
  1.1 1.0 copy-done.2
  2.1 1.0 copy-done.3
  3.2 0.8 pack_kv.1
  4.0 1.7 %collective-permute-start = (bf16[128,1024]{1,0:T(8,128)(2,1)S(1)}, bf16[128,1024]{1,0:T(8,128)(2,1)S(1)}, u32[]{:S(2)}, u32[]{:S(2)}) collective-permute-start(bf16[128,1024]{1,0:T(8,128)(2,1)S(1)} %get-tuple-element.68), channel_id=1, source_target_pairs={{0,4},{1,5},{2,6},{3,7},{4,2},{5,3},{6,0},{7,1},{8,12},{9,13},{10,... | collective-permute-start | bytes 786440 | tf_op jit(solution)/shard_map/ppermute | solution.py:341
  5.6 2.9 %collective-permute-start.1 = (bf16[128,1024]{1,0:T(8,128)(2,1)S(1)}, bf16[128,1024]{1,0:T(8,128)(2,1)S(1)}, u32[]{:S(2)}, u32[]{:S(2)}) collective-permute-start(bf16[128,1024]{1,0:T(8,128)(2,1)S(1)} %get-tuple-element.69), channel_id=1, source_target_pairs={{0,2},{1,3},{2,0},{3,1},{4,6},{5,7},{6,4},{7,5},{8,10},{9,11},{10,... | collective-permute-start | bytes 786440 | tf_op jit(solution)/shard_map/ppermute | solution.py:341
  8.5 1.4 %collective-permute-start.2 = (bf16[128,1024]{1,0:T(8,128)(2,1)S(1)}, bf16[128,1024]{1,0:T(8,128)(2,1)S(1)}, u32[]{:S(2)}, u32[]{:S(2)}) collective-permute-start(bf16[128,1024]{1,0:T(8,128)(2,1)S(1)} %get-tuple-element.70), channel_id=1, source_target_pairs={{0,6},{1,7},{2,4},{3,5},{4,0},{5,1},{6,2},{7,3},{8,14},{9,15},{10,... | collective-permute-start | bytes 786440 | tf_op jit(solution)/shard_map/ppermute | solution.py:341
  9.9 0.1 slice_reduce_fusion
  10.0 0.1 slice_reduce_fusion.1
  10.1 0.1 fusion.3
  10.2 3.2 %collective-permute-done.p1.refs_6_ = bf16[128,1024]{1,0:T(8,128)(2,1)S(1)} collective-permute-done((bf16[128,1024]{1,0:T(8,128)(2,1)S(1)}, bf16[128,1024]{1,0:T(8,128)(2,1)S(1)}, u32[]{:S(2)}, u32[]{:S(2)}) %collective-permute-start) | collective-permute-done | bytes 262176 | tf_op jit(solution)/shard_map/ppermute | solution.py:341
  13.4 1.2 %copy-done.1 = bf16[128,4096]{1,0:T(8,128)(2,1)S(1)} copy-done((bf16[128,4096]{1,0:T(8,128)(2,1)S(1)}, bf16[128,4096]{1,0:T(8,128)(2,1)}, u32[]{:S(2)}) %copy-start.1) | copy-done | bytes 1048600
  14.6 0.8 pack_qd.1
  15.4 4.7 %collective-permute-done.1.p2.refs_7_ = bf16[128,1024]{1,0:T(8,128)(2,1)S(1)} collective-permute-done((bf16[128,1024]{1,0:T(8,128)(2,1)S(1)}, bf16[128,1024]{1,0:T(8,128)(2,1)S(1)}, u32[]{:S(2)}, u32[]{:S(2)}) %collective-permute-start.1) | collective-permute-done | bytes 262176 | tf_op jit(solution)/shard_map/ppermute | solution.py:341
  20.2 0.0 collective-permute-done.2.p3.refs_8_
  20.2 0.6 to_sibling_in.3
  20.8 0.1 collective-permute-start.3
  20.9 1.9 %collective-permute-done.3.sib.refs_9_ = bf16[4,128,512]{2,1,0:T(8,128)(2,1)S(1)} collective-permute-done((bf16[4,128,512]{2,1,0:T(8,128)(2,1)S(1)}, bf16[4,128,512]{2,1,0:T(8,128)(2,1)S(1)}, u32[]{:S(2)}, u32[]{:S(2)}) %collective-permute-start.3) | collective-permute-done | bytes 524320 | tf_op jit(solution)/shard_map/ppermute | solution.py:357
  22.8 0.6 halo.1
  23.4 1.3 %collective-permute-start.4 = (bf16[128,1024]{1,0:T(8,128)(2,1)S(1)}, bf16[128,1024]{1,0:T(8,128)(2,1)S(1)}, u32[]{:S(2)}, u32[]{:S(2)}) collective-permute-start(bf16[128,1024]{1,0:T(8,128)(2,1)S(1)} %get-tuple-element.88), channel_id=1, source_target_pairs={{0,4},{1,5},{2,6},{3,7},{4,2},{5,3},{6,0},{7,1},{8,12},{9,13},{10,... | collective-permute-start | bytes 786440 | tf_op jit(solution)/shard_map/ppermute | solution.py:341
  24.7 2.4 %collective-permute-start.5 = (bf16[128,1024]{1,0:T(8,128)(2,1)S(1)}, bf16[128,1024]{1,0:T(8,128)(2,1)S(1)}, u32[]{:S(2)}, u32[]{:S(2)}) collective-permute-start(bf16[128,1024]{1,0:T(8,128)(2,1)S(1)} %get-tuple-element.89), channel_id=1, source_target_pairs={{0,2},{1,3},{2,0},{3,1},{4,6},{5,7},{6,4},{7,5},{8,10},{9,11},{10,... | collective-permute-start | bytes 786440 | tf_op jit(solution)/shard_map/ppermute | solution.py:341
  27.1 1.8 %collective-permute-start.6 = (bf16[128,1024]{1,0:T(8,128)(2,1)S(1)}, bf16[128,1024]{1,0:T(8,128)(2,1)S(1)}, u32[]{:S(2)}, u32[]{:S(2)}) collective-permute-start(bf16[128,1024]{1,0:T(8,128)(2,1)S(1)} %get-tuple-element.90), channel_id=1, source_target_pairs={{0,6},{1,7},{2,4},{3,5},{4,0},{5,1},{6,2},{7,3},{8,14},{9,15},{10,... | collective-permute-start | bytes 786440 | tf_op jit(solution)/shard_map/ppermute | solution.py:341
  28.9 3.8 %collective-permute-start.8 = (bf16[8,128,256]{2,1,0:T(8,128)(2,1)S(1)}, bf16[8,128,256]{2,1,0:T(8,128)(2,1)S(1)}, u32[]{:S(2)}, u32[]{:S(2)}) collective-permute-start(bf16[8,128,256]{2,1,0:T(8,128)(2,1)S(1)} %get-tuple-element.85), channel_id=1, source_target_pairs={{0,8},{8,16},{16,24},{24,32},{32,40},{40,48},{48,56},{56,64},{64,7... | collective-permute-start | bytes 1572872 | tf_op jit(solution)/shard_map/ppermute | solution.py:363
  32.7 0.7 collective-permute-done.4.p1.refs_1_
  33.4 5.6 %collective-permute-done.5.p2.refs_2_ = bf16[128,1024]{1,0:T(8,128)(2,1)S(1)} collective-permute-done((bf16[128,1024]{1,0:T(8,128)(2,1)S(1)}, bf16[128,1024]{1,0:T(8,128)(2,1)S(1)}, u32[]{:S(2)}, u32[]{:S(2)}) %collective-permute-start.5) | collective-permute-done | bytes 262176 | tf_op jit(solution)/shard_map/ppermute | solution.py:341
  39.0 0.2 collective-permute-done.6.p3.refs_3_
  39.3 0.6 to_sibling_in.4
  39.9 0.1 collective-permute-start.7
  40.0 3.8 %collective-permute-start.16 = (bf16[8,128,256]{2,1,0:T(8,128)(2,1)S(1)}, bf16[8,128,256]{2,1,0:T(8,128)(2,1)S(1)}, u32[]{:S(2)}, u32[]{:S(2)}) collective-permute-start(bf16[8,128,256]{2,1,0:T(8,128)(2,1)S(1)} %get-tuple-element.86), channel_id=1, source_target_pairs={{0,8},{8,16},{16,24},{24,32},{32,40},{40,48},{48,56},{56,64},{64,7... | collective-permute-start | bytes 1572872 | tf_op jit(solution)/shard_map/ppermute | solution.py:363
  43.8 1.8 %collective-permute-start.12 = (bf16[128,1024]{1,0:T(8,128)(2,1)S(1)}, bf16[128,1024]{1,0:T(8,128)(2,1)S(1)}, u32[]{:S(2)}, u32[]{:S(2)}) collective-permute-start(bf16[128,1024]{1,0:T(8,128)(2,1)S(1)} %get-tuple-element.96), channel_id=1, source_target_pairs={{0,4},{1,5},{2,6},{3,7},{4,2},{5,3},{6,0},{7,1},{8,12},{9,13},{10,... | collective-permute-start | bytes 786440 | tf_op jit(solution)/shard_map/ppermute | solution.py:341
  45.6 2.4 %collective-permute-start.13 = (bf16[128,1024]{1,0:T(8,128)(2,1)S(1)}, bf16[128,1024]{1,0:T(8,128)(2,1)S(1)}, u32[]{:S(2)}, u32[]{:S(2)}) collective-permute-start(bf16[128,1024]{1,0:T(8,128)(2,1)S(1)} %get-tuple-element.97), channel_id=1, source_target_pairs={{0,2},{1,3},{2,0},{3,1},{4,6},{5,7},{6,4},{7,5},{8,10},{9,11},{10,... | collective-permute-start | bytes 786440 | tf_op jit(solution)/shard_map/ppermute | solution.py:341
  48.0 0.4 collective-permute-done.8.refs_10_
  48.3 1.0 collective-permute-start.14
  49.3 12.5 %attend_0.1 = (bf16[256,512]{1,0:T(8,128)(2,1)S(1)}, bf16[256,512]{1,0:T(8,128)(2,1)S(1)}, bf16[256,512]{1,0:T(8,128)(2,1)S(1)}, bf16[256,512]{1,0:T(8,128)(2,1)...) custom-call(s32[9]{0:T(128)S(1)} %stack.36.tab, f32[8,128]{1,0:T(8,128)S(1)} %pad.5.bias_ref, ...), custom_call_target="tpu_custom_call" | custom-call | flops 14000000000 | bytes 4194304 | tf_op jit(solution)/shard_map/attend_0/pallas_call | solution.py:47
  61.9 0.0 collective-permute-done.12.p1.refs_1_
  61.9 0.0 collective-permute-done.13.p2.refs_2_
  61.9 0.6 to_sibling_in.5
  62.5 0.1 collective-permute-start.15
  62.6 1.1 collective-permute-start.9
  63.7 0.9 collective-permute-start.10
  64.6 2.0 %collective-permute-start.11 = (bf16[256,512]{1,0:T(8,128)(2,1)S(1)}, bf16[256,512]{1,0:T(8,128)(2,1)S(1)}, u32[]{:S(2)}, u32[]{:S(2)}) collective-permute-start(bf16[256,512]{1,0:T(8,128)(2,1)S(1)} %get-tuple-element.94), channel_id=1, source_target_pairs={{0,6},{1,7},{2,4},{3,5},{4,0},{5,1},{6,2},{7,3},{8,14},{9,15},{10,... | collective-permute-start | bytes 786440 | tf_op jit(solution)/shard_map/ppermute | solution.py:341
  66.6 0.0 collective-permute-done.16.refs_10_
  66.6 5.8 %collective-permute-start.22 = (bf16[1024,256]{1,0:T(8,128)(2,1)S(1)}, bf16[1024,256]{1,0:T(8,128)(2,1)S(1)}, u32[]{:S(2)}, u32[]{:S(2)}) collective-permute-start(bf16[1024,256]{1,0:T(8,128)(2,1)S(1)} %get-tuple-element.122), channel_id=1, source_target_pairs={{8,0},{16,8},{24,16},{32,24},{40,32},{48,40},{56,48},{64,56},{72,6... | collective-permute-start | bytes 1572872 | tf_op jit(solution)/shard_map/ppermute | solution.py:363
  72.4 12.6 %attend_1.1 = (bf16[256,512]{1,0:T(8,128)(2,1)S(1)}, bf16[256,512]{1,0:T(8,128)(2,1)S(1)}, bf16[256,512]{1,0:T(8,128)(2,1)S(1)}, bf16[256,512]{1,0:T(8,128)(2,1)...) custom-call(s32[9]{0:T(128)S(1)} %stack.36.tab, f32[8,128]{1,0:T(8,128)S(1)} %pad.5.bias_ref, ...), custom_call_target="tpu_custom_call" | custom-call | flops 14000000000 | bytes 4194304 | tf_op jit(solution)/shard_map/attend_1/pallas_call | solution.py:47
  85.0 0.0 collective-permute-done.10.p2.refs_2_
  85.0 0.0 collective-permute-done.11.p3.refs_3_
  85.0 0.6 to_sibling_out.3
  85.6 3.8 %collective-permute-start.23 = (bf16[1024,256]{1,0:T(8,128)(2,1)S(1)}, bf16[1024,256]{1,0:T(8,128)(2,1)S(1)}, u32[]{:S(2)}, u32[]{:S(2)}) collective-permute-start(bf16[1024,256]{1,0:T(8,128)(2,1)S(1)} %get-tuple-element.123), channel_id=1, source_target_pairs={{8,0},{16,8},{24,16},{32,24},{40,32},{48,40},{56,48},{64,56},{72,6... | collective-permute-start | bytes 1572872 | tf_op jit(solution)/shard_map/ppermute | solution.py:363
  89.4 0.8 collective-permute-start.18
  90.1 2.2 %collective-permute-start.19 = (bf16[256,512]{1,0:T(8,128)(2,1)S(1)}, bf16[256,512]{1,0:T(8,128)(2,1)S(1)}, u32[]{:S(2)}, u32[]{:S(2)}) collective-permute-start(bf16[256,512]{1,0:T(8,128)(2,1)S(1)} %get-tuple-element.116), channel_id=1, source_target_pairs={{0,2},{1,3},{2,0},{3,1},{4,6},{5,7},{6,4},{7,5},{8,10},{9,11},{10,... | collective-permute-start | bytes 786440 | tf_op jit(solution)/shard_map/ppermute | solution.py:341
  92.3 2.5 %collective-permute-start.20 = (bf16[256,512]{1,0:T(8,128)(2,1)S(1)}, bf16[256,512]{1,0:T(8,128)(2,1)S(1)}, u32[]{:S(2)}, u32[]{:S(2)}) collective-permute-start(bf16[256,512]{1,0:T(8,128)(2,1)S(1)} %get-tuple-element.117), channel_id=1, source_target_pairs={{0,6},{1,7},{2,4},{3,5},{4,0},{5,1},{6,2},{7,3},{8,14},{9,15},{10,... | collective-permute-start | bytes 786440 | tf_op jit(solution)/shard_map/ppermute | solution.py:341
  94.8 5.8 %collective-permute-done.23.from1 = bf16[1024,256]{1,0:T(8,128)(2,1)S(1)} collective-permute-done((bf16[1024,256]{1,0:T(8,128)(2,1)S(1)}, bf16[1024,256]{1,0:T(8,128)(2,1)S(1)}, u32[]{:S(2)}, u32[]{:S(2)}) %collective-permute-start.23) | collective-permute-done | bytes 524320 | tf_op jit(solution)/shard_map/ppermute | solution.py:363
  100.6 0.8 merge.1
  101.4 0.8 collective-permute-start.24
  102.3 1.9 %collective-permute-start.25 = (bf16[256,512]{1,0:T(8,128)(2,1)S(1)}, bf16[256,512]{1,0:T(8,128)(2,1)S(1)}, u32[]{:S(2)}, u32[]{:S(2)}) collective-permute-start(bf16[256,512]{1,0:T(8,128)(2,1)S(1)} %get-tuple-element.126), channel_id=1, source_target_pairs={{0,2},{1,3},{2,0},{3,1},{4,6},{5,7},{6,4},{7,5},{8,10},{9,11},{10,... | collective-permute-start | bytes 786440 | tf_op jit(solution)/shard_map/ppermute | solution.py:341
  104.1 2.5 %collective-permute-start.26 = (bf16[256,512]{1,0:T(8,128)(2,1)S(1)}, bf16[256,512]{1,0:T(8,128)(2,1)S(1)}, u32[]{:S(2)}, u32[]{:S(2)}) collective-permute-start(bf16[256,512]{1,0:T(8,128)(2,1)S(1)} %get-tuple-element.127), channel_id=1, source_target_pairs={{0,6},{1,7},{2,4},{3,5},{4,0},{5,1},{6,2},{7,3},{8,14},{9,15},{10,... | collective-permute-start | bytes 786440 | tf_op jit(solution)/shard_map/ppermute | solution.py:341
  106.7 0.6 to_sibling_out.4
  107.3 0.6 collective-permute-start.21
  107.9 7.1 %collective-permute-done.24.p1 = bf16[256,512]{1,0:T(8,128)(2,1)S(1)} collective-permute-done((bf16[256,512]{1,0:T(8,128)(2,1)S(1)}, bf16[256,512]{1,0:T(8,128)(2,1)S(1)}, u32[]{:S(2)}, u32[]{:S(2)}) %collective-permute-start.24) | collective-permute-done | bytes 262176 | tf_op jit(solution)/shard_map/ppermute | solution.py:341
  115.0 0.6 collective-permute-done.26.p3
  115.5 0.6 to_sibling_out.5
  116.1 0.1 collective-permute-start.27
  116.2 2.1 %unpack_out.1 = (bf16[128,4096]{1,0:T(8,128)(2,1)}, bf16[128,4096]{1,0:T(8,128)(2,1)}) custom-call(s32[9]{0:T(128)S(1)} %stack.36.tab, bf16[256,512]{1,0:T(8,128)(2,1)S(1)} %get-tuple-element.105.p0.refs_0_, bf16[256,512]{1,0:T(8,128)(2,1)S(1)} %collective-permute-done.9.p1.refs_1_, bf16[256,512]{1,0:T(8,128)(2,1)S(1)} %collective-permute-done.10.p2.refs_2_, ...), custom_call_target="tpu_custom_call" | custom-call | bytes 4194304 | tf_op jit(solution)/shard_map/unpack_out/pallas_call | solution.py:47
  118.4 1.8 %unpack_kv.1 = (bf16[128,2048]{1,0:T(8,128)(2,1)}, bf16[128,2048]{1,0:T(8,128)(2,1)}) custom-call(s32[9]{0:T(128)S(1)} %stack.36.tab, bf16[256,512]{1,0:T(8,128)(2,1)S(1)} %get-tuple-element.124.p0, bf16[256,512]{1,0:T(8,128)(2,1)S(1)} %collective-permute-done.24.p1, bf16[256,512]{1,0:T(8,128)(2,1)S(1)} %collective-permute-done.25.p2, ...), custom_call_target="tpu_custom_call" | custom-call | bytes 2097152 | tf_op jit(solution)/shard_map/unpack_kv/pallas_call | solution.py:47
  (23 shorter events, 0.1 us)
Async XLA Ops:
  0.6 12.7 %copy-start = (bf16[128,4096]{1,0:T(8,128)(2,1)S(1)}, bf16[128,4096]{1,0:T(8,128)(2,1)}, u32[]{:S(2)}) copy-start(bf16[128,4096]{1,0:T(8,128)(2,1)} %q_ref) | copy-start | bytes 3145732
  1.1 1.0 copy-start.2
  2.1 1.0 copy-start.3
  3.2 6.7 %copy-start.4 = (s32[32768]{0:T(1024)S(1)}, s32[32768]{0:T(1024)}, u32[]{:S(2)}) copy-start(s32[32768]{0:T(1024)} %param.9) | copy-start | bytes 393220
  4.0 9.4 %collective-permute-start = (bf16[128,1024]{1,0:T(8,128)(2,1)S(1)}, bf16[128,1024]{1,0:T(8,128)(2,1)S(1)}, u32[]{:S(2)}, u32[]{:S(2)}) collective-permute-start(bf16[128,1024]{1,0:T(8,128)(2,1)S(1)} %get-tuple-element.68), channel_id=1, source_target_pairs={{0,4},{1,5},{2,6},{3,7},{4,2},{5,3},{6,0},{7,1},{8,12},{9,13},{10,... | collective-permute-start | bytes 786440 | tf_op jit(solution)/shard_map/ppermute | solution.py:341
  5.6 14.5 %collective-permute-start.1 = (bf16[128,1024]{1,0:T(8,128)(2,1)S(1)}, bf16[128,1024]{1,0:T(8,128)(2,1)S(1)}, u32[]{:S(2)}, u32[]{:S(2)}) collective-permute-start(bf16[128,1024]{1,0:T(8,128)(2,1)S(1)} %get-tuple-element.69), channel_id=1, source_target_pairs={{0,2},{1,3},{2,0},{3,1},{4,6},{5,7},{6,4},{7,5},{8,10},{9,11},{10,... | collective-permute-start | bytes 786440 | tf_op jit(solution)/shard_map/ppermute | solution.py:341
  8.5 11.6 %collective-permute-start.2 = (bf16[128,1024]{1,0:T(8,128)(2,1)S(1)}, bf16[128,1024]{1,0:T(8,128)(2,1)S(1)}, u32[]{:S(2)}, u32[]{:S(2)}) collective-permute-start(bf16[128,1024]{1,0:T(8,128)(2,1)S(1)} %get-tuple-element.70), channel_id=1, source_target_pairs={{0,6},{1,7},{2,4},{3,5},{4,0},{5,1},{6,2},{7,3},{8,14},{9,15},{10,... | collective-permute-start | bytes 786440 | tf_op jit(solution)/shard_map/ppermute | solution.py:341
  13.4 1.2 %copy-start.1 = (bf16[128,4096]{1,0:T(8,128)(2,1)S(1)}, bf16[128,4096]{1,0:T(8,128)(2,1)}, u32[]{:S(2)}) copy-start(bf16[128,4096]{1,0:T(8,128)(2,1)} %d_ref.1) | copy-start | bytes 3145732
  20.8 2.0 %collective-permute-start.3 = (bf16[4,128,512]{2,1,0:T(8,128)(2,1)S(1)}, bf16[4,128,512]{2,1,0:T(8,128)(2,1)S(1)}, u32[]{:S(2)}, u32[]{:S(2)}) collective-permute-start(bf16[4,128,512]{2,1,0:T(8,128)(2,1)S(1)} %to_sibling_in.3), channel_id=1, source_target_pairs={{0,1},{1,0},{2,3},{3,2},{4,5},{5,4},{6,7},{7,6},{8,9},{9,8},{10,11... | collective-permute-start | bytes 1572872 | tf_op jit(solution)/shard_map/ppermute | solution.py:357
  23.4 10.0 %collective-permute-start.4 = (bf16[128,1024]{1,0:T(8,128)(2,1)S(1)}, bf16[128,1024]{1,0:T(8,128)(2,1)S(1)}, u32[]{:S(2)}, u32[]{:S(2)}) collective-permute-start(bf16[128,1024]{1,0:T(8,128)(2,1)S(1)} %get-tuple-element.88), channel_id=1, source_target_pairs={{0,4},{1,5},{2,6},{3,7},{4,2},{5,3},{6,0},{7,1},{8,12},{9,13},{10,... | collective-permute-start | bytes 786440 | tf_op jit(solution)/shard_map/ppermute | solution.py:341
  24.7 14.3 %collective-permute-start.5 = (bf16[128,1024]{1,0:T(8,128)(2,1)S(1)}, bf16[128,1024]{1,0:T(8,128)(2,1)S(1)}, u32[]{:S(2)}, u32[]{:S(2)}) collective-permute-start(bf16[128,1024]{1,0:T(8,128)(2,1)S(1)} %get-tuple-element.89), channel_id=1, source_target_pairs={{0,2},{1,3},{2,0},{3,1},{4,6},{5,7},{6,4},{7,5},{8,10},{9,11},{10,... | collective-permute-start | bytes 786440 | tf_op jit(solution)/shard_map/ppermute | solution.py:341
  27.1 12.2 %collective-permute-start.6 = (bf16[128,1024]{1,0:T(8,128)(2,1)S(1)}, bf16[128,1024]{1,0:T(8,128)(2,1)S(1)}, u32[]{:S(2)}, u32[]{:S(2)}) collective-permute-start(bf16[128,1024]{1,0:T(8,128)(2,1)S(1)} %get-tuple-element.90), channel_id=1, source_target_pairs={{0,6},{1,7},{2,4},{3,5},{4,0},{5,1},{6,2},{7,3},{8,14},{9,15},{10,... | collective-permute-start | bytes 786440 | tf_op jit(solution)/shard_map/ppermute | solution.py:341
  28.9 19.4 %collective-permute-start.8 = (bf16[8,128,256]{2,1,0:T(8,128)(2,1)S(1)}, bf16[8,128,256]{2,1,0:T(8,128)(2,1)S(1)}, u32[]{:S(2)}, u32[]{:S(2)}) collective-permute-start(bf16[8,128,256]{2,1,0:T(8,128)(2,1)S(1)} %get-tuple-element.85), channel_id=1, source_target_pairs={{0,8},{8,16},{16,24},{24,32},{32,40},{40,48},{48,56},{56,64},{64,7... | collective-permute-start | bytes 1572872 | tf_op jit(solution)/shard_map/ppermute | solution.py:363
  39.9 9.5 %collective-permute-start.7 = (bf16[4,128,512]{2,1,0:T(8,128)(2,1)S(1)}, bf16[4,128,512]{2,1,0:T(8,128)(2,1)S(1)}, u32[]{:S(2)}, u32[]{:S(2)}) collective-permute-start(bf16[4,128,512]{2,1,0:T(8,128)(2,1)S(1)} %to_sibling_in.4), channel_id=1, source_target_pairs={{0,1},{1,0},{2,3},{3,2},{4,5},{5,4},{6,7},{7,6},{8,9},{9,8},{10,11... | collective-permute-start | bytes 1572872 | tf_op jit(solution)/shard_map/ppermute | solution.py:357
  40.0 26.6 %collective-permute-start.16 = (bf16[8,128,256]{2,1,0:T(8,128)(2,1)S(1)}, bf16[8,128,256]{2,1,0:T(8,128)(2,1)S(1)}, u32[]{:S(2)}, u32[]{:S(2)}) collective-permute-start(bf16[8,128,256]{2,1,0:T(8,128)(2,1)S(1)} %get-tuple-element.86), channel_id=1, source_target_pairs={{0,8},{8,16},{16,24},{24,32},{32,40},{40,48},{48,56},{56,64},{64,7... | collective-permute-start | bytes 1572872 | tf_op jit(solution)/shard_map/ppermute | solution.py:363
  43.8 18.1 %collective-permute-start.12 = (bf16[128,1024]{1,0:T(8,128)(2,1)S(1)}, bf16[128,1024]{1,0:T(8,128)(2,1)S(1)}, u32[]{:S(2)}, u32[]{:S(2)}) collective-permute-start(bf16[128,1024]{1,0:T(8,128)(2,1)S(1)} %get-tuple-element.96), channel_id=1, source_target_pairs={{0,4},{1,5},{2,6},{3,7},{4,2},{5,3},{6,0},{7,1},{8,12},{9,13},{10,... | collective-permute-start | bytes 786440 | tf_op jit(solution)/shard_map/ppermute | solution.py:341
  45.6 16.3 %collective-permute-start.13 = (bf16[128,1024]{1,0:T(8,128)(2,1)S(1)}, bf16[128,1024]{1,0:T(8,128)(2,1)S(1)}, u32[]{:S(2)}, u32[]{:S(2)}) collective-permute-start(bf16[128,1024]{1,0:T(8,128)(2,1)S(1)} %get-tuple-element.97), channel_id=1, source_target_pairs={{0,2},{1,3},{2,0},{3,1},{4,6},{5,7},{6,4},{7,5},{8,10},{9,11},{10,... | collective-permute-start | bytes 786440 | tf_op jit(solution)/shard_map/ppermute | solution.py:341
  48.3 13.6 %collective-permute-start.14 = (bf16[128,1024]{1,0:T(8,128)(2,1)S(1)}, bf16[128,1024]{1,0:T(8,128)(2,1)S(1)}, u32[]{:S(2)}, u32[]{:S(2)}) collective-permute-start(bf16[128,1024]{1,0:T(8,128)(2,1)S(1)} %get-tuple-element.98), channel_id=1, source_target_pairs={{0,6},{1,7},{2,4},{3,5},{4,0},{5,1},{6,2},{7,3},{8,14},{9,15},{10,... | collective-permute-start | bytes 786440 | tf_op jit(solution)/shard_map/ppermute | solution.py:341
  62.5 9.9 %collective-permute-start.15 = (bf16[4,128,512]{2,1,0:T(8,128)(2,1)S(1)}, bf16[4,128,512]{2,1,0:T(8,128)(2,1)S(1)}, u32[]{:S(2)}, u32[]{:S(2)}) collective-permute-start(bf16[4,128,512]{2,1,0:T(8,128)(2,1)S(1)} %to_sibling_in.5), channel_id=1, source_target_pairs={{0,1},{1,0},{2,3},{3,2},{4,5},{5,4},{6,7},{7,6},{8,9},{9,8},{10,11... | collective-permute-start | bytes 1572872 | tf_op jit(solution)/shard_map/ppermute | solution.py:357
  62.6 22.4 %collective-permute-start.9 = (bf16[256,512]{1,0:T(8,128)(2,1)S(1)}, bf16[256,512]{1,0:T(8,128)(2,1)S(1)}, u32[]{:S(2)}, u32[]{:S(2)}) collective-permute-start(bf16[256,512]{1,0:T(8,128)(2,1)S(1)} %get-tuple-element.92), channel_id=1, source_target_pairs={{0,4},{1,5},{2,6},{3,7},{4,2},{5,3},{6,0},{7,1},{8,12},{9,13},{10,... | collective-permute-start | bytes 786440 | tf_op jit(solution)/shard_map/ppermute | solution.py:341
  63.7 21.3 %collective-permute-start.10 = (bf16[256,512]{1,0:T(8,128)(2,1)S(1)}, bf16[256,512]{1,0:T(8,128)(2,1)S(1)}, u32[]{:S(2)}, u32[]{:S(2)}) collective-permute-start(bf16[256,512]{1,0:T(8,128)(2,1)S(1)} %get-tuple-element.93), channel_id=1, source_target_pairs={{0,2},{1,3},{2,0},{3,1},{4,6},{5,7},{6,4},{7,5},{8,10},{9,11},{10,... | collective-permute-start | bytes 786440 | tf_op jit(solution)/shard_map/ppermute | solution.py:341
  64.6 20.4 %collective-permute-start.11 = (bf16[256,512]{1,0:T(8,128)(2,1)S(1)}, bf16[256,512]{1,0:T(8,128)(2,1)S(1)}, u32[]{:S(2)}, u32[]{:S(2)}) collective-permute-start(bf16[256,512]{1,0:T(8,128)(2,1)S(1)} %get-tuple-element.94), channel_id=1, source_target_pairs={{0,6},{1,7},{2,4},{3,5},{4,0},{5,1},{6,2},{7,3},{8,14},{9,15},{10,... | collective-permute-start | bytes 786440 | tf_op jit(solution)/shard_map/ppermute | solution.py:341
  66.6 28.2 %collective-permute-start.22 = (bf16[1024,256]{1,0:T(8,128)(2,1)S(1)}, bf16[1024,256]{1,0:T(8,128)(2,1)S(1)}, u32[]{:S(2)}, u32[]{:S(2)}) collective-permute-start(bf16[1024,256]{1,0:T(8,128)(2,1)S(1)} %get-tuple-element.122), channel_id=1, source_target_pairs={{8,0},{16,8},{24,16},{32,24},{40,32},{48,40},{56,48},{64,56},{72,6... | collective-permute-start | bytes 1572872 | tf_op jit(solution)/shard_map/ppermute | solution.py:363
  85.6 15.1 %collective-permute-start.23 = (bf16[1024,256]{1,0:T(8,128)(2,1)S(1)}, bf16[1024,256]{1,0:T(8,128)(2,1)S(1)}, u32[]{:S(2)}, u32[]{:S(2)}) collective-permute-start(bf16[1024,256]{1,0:T(8,128)(2,1)S(1)} %get-tuple-element.123), channel_id=1, source_target_pairs={{8,0},{16,8},{24,16},{32,24},{40,32},{48,40},{56,48},{64,56},{72,6... | collective-permute-start | bytes 1572872 | tf_op jit(solution)/shard_map/ppermute | solution.py:363
  89.4 14.8 %collective-permute-start.18 = (bf16[256,512]{1,0:T(8,128)(2,1)S(1)}, bf16[256,512]{1,0:T(8,128)(2,1)S(1)}, u32[]{:S(2)}, u32[]{:S(2)}) collective-permute-start(bf16[256,512]{1,0:T(8,128)(2,1)S(1)} %get-tuple-element.115), channel_id=1, source_target_pairs={{0,4},{1,5},{2,6},{3,7},{4,2},{5,3},{6,0},{7,1},{8,12},{9,13},{10,... | collective-permute-start | bytes 786440 | tf_op jit(solution)/shard_map/ppermute | solution.py:341
  90.1 16.6 %collective-permute-start.19 = (bf16[256,512]{1,0:T(8,128)(2,1)S(1)}, bf16[256,512]{1,0:T(8,128)(2,1)S(1)}, u32[]{:S(2)}, u32[]{:S(2)}) collective-permute-start(bf16[256,512]{1,0:T(8,128)(2,1)S(1)} %get-tuple-element.116), channel_id=1, source_target_pairs={{0,2},{1,3},{2,0},{3,1},{4,6},{5,7},{6,4},{7,5},{8,10},{9,11},{10,... | collective-permute-start | bytes 786440 | tf_op jit(solution)/shard_map/ppermute | solution.py:341
  92.3 14.4 %collective-permute-start.20 = (bf16[256,512]{1,0:T(8,128)(2,1)S(1)}, bf16[256,512]{1,0:T(8,128)(2,1)S(1)}, u32[]{:S(2)}, u32[]{:S(2)}) collective-permute-start(bf16[256,512]{1,0:T(8,128)(2,1)S(1)} %get-tuple-element.117), channel_id=1, source_target_pairs={{0,6},{1,7},{2,4},{3,5},{4,0},{5,1},{6,2},{7,3},{8,14},{9,15},{10,... | collective-permute-start | bytes 786440 | tf_op jit(solution)/shard_map/ppermute | solution.py:341
  101.4 13.5 %collective-permute-start.24 = (bf16[256,512]{1,0:T(8,128)(2,1)S(1)}, bf16[256,512]{1,0:T(8,128)(2,1)S(1)}, u32[]{:S(2)}, u32[]{:S(2)}) collective-permute-start(bf16[256,512]{1,0:T(8,128)(2,1)S(1)} %get-tuple-element.125), channel_id=1, source_target_pairs={{0,4},{1,5},{2,6},{3,7},{4,2},{5,3},{6,0},{7,1},{8,12},{9,13},{10,... | collective-permute-start | bytes 786440 | tf_op jit(solution)/shard_map/ppermute | solution.py:341
  102.3 12.7 %collective-permute-start.25 = (bf16[256,512]{1,0:T(8,128)(2,1)S(1)}, bf16[256,512]{1,0:T(8,128)(2,1)S(1)}, u32[]{:S(2)}, u32[]{:S(2)}) collective-permute-start(bf16[256,512]{1,0:T(8,128)(2,1)S(1)} %get-tuple-element.126), channel_id=1, source_target_pairs={{0,2},{1,3},{2,0},{3,1},{4,6},{5,7},{6,4},{7,5},{8,10},{9,11},{10,... | collective-permute-start | bytes 786440 | tf_op jit(solution)/shard_map/ppermute | solution.py:341
  104.1 11.4 %collective-permute-start.26 = (bf16[256,512]{1,0:T(8,128)(2,1)S(1)}, bf16[256,512]{1,0:T(8,128)(2,1)S(1)}, u32[]{:S(2)}, u32[]{:S(2)}) collective-permute-start(bf16[256,512]{1,0:T(8,128)(2,1)S(1)} %get-tuple-element.127), channel_id=1, source_target_pairs={{0,6},{1,7},{2,4},{3,5},{4,0},{5,1},{6,2},{7,3},{8,14},{9,15},{10,... | collective-permute-start | bytes 786440 | tf_op jit(solution)/shard_map/ppermute | solution.py:341
  106.7 9.5 %collective-permute-start.17 = (bf16[4,128,512]{2,1,0:T(8,128)(2,1)S(1)}, bf16[4,128,512]{2,1,0:T(8,128)(2,1)S(1)}, u32[]{:S(2)}, u32[]{:S(2)}) collective-permute-start(bf16[4,128,512]{2,1,0:T(8,128)(2,1)S(1)} %to_sibling_out.3), channel_id=1, source_target_pairs={{0,1},{1,0},{2,3},{3,2},{4,5},{5,4},{6,7},{7,6},{8,9},{9,8},{10,11... | collective-permute-start | bytes 1572872 | tf_op jit(solution)/shard_map/ppermute | solution.py:357
  107.3 9.0 %collective-permute-start.21 = (bf16[4,128,512]{2,1,0:T(8,128)(2,1)S(1)}, bf16[4,128,512]{2,1,0:T(8,128)(2,1)S(1)}, u32[]{:S(2)}, u32[]{:S(2)}) collective-permute-start(bf16[4,128,512]{2,1,0:T(8,128)(2,1)S(1)} %to_sibling_out.4), channel_id=1, source_target_pairs={{0,1},{1,0},{2,3},{3,2},{4,5},{5,4},{6,7},{7,6},{8,9},{9,8},{10,11... | collective-permute-start | bytes 1572872 | tf_op jit(solution)/shard_map/ppermute | solution.py:357
  116.1 2.2 %collective-permute-start.27 = (bf16[4,128,512]{2,1,0:T(8,128)(2,1)S(1)}, bf16[4,128,512]{2,1,0:T(8,128)(2,1)S(1)}, u32[]{:S(2)}, u32[]{:S(2)}) collective-permute-start(bf16[4,128,512]{2,1,0:T(8,128)(2,1)S(1)} %to_sibling_out.5), channel_id=1, source_target_pairs={{0,1},{1,0},{2,3},{3,2},{4,5},{5,4},{6,7},{7,6},{8,9},{9,8},{10,11... | collective-permute-start | bytes 1572872 | tf_op jit(solution)/shard_map/ppermute | solution.py:357

commit v5 on v4

--- a/solution.py
+++ b/solution.py
@@ -398,7 +398,7 @@
         if chunk == 1:
             received[0], g_own = lax.optimization_barrier((received[0], g_own))
             sent = sibling_out(tab, *received[0])
-            pieces, g_halo, _ = lax.optimization_barrier((pieces, g_halo, sent))
+            pieces, _ = lax.optimization_barrier((pieces, sent))
         received.append(exchange(pieces))
         own.append(g_own)
         other.append(shifted(g_halo, -1))

time: 121 us -> 121 us (level)
  transfers between devices with their start and end apart: 28 -> 28, of which waited for: 10 -> 11; matrix products, arithmetic and copies ran while one was open for 0% -> 0% of each run, Pallas kernels for 26% -> 26%
where the time goes in v5:
time: 121 us; the launch traced here: 120 us
  starting transfers between devices  49.4 us (41%)
  Pallas kernels  35.5 us (29%)
  waiting for transfers between devices  30.3 us (25%)
  local copies, waits for them, and re-layouts  3.65 us (3%)
  between operations  1.23 us (1%)
    pallas_call x14, Pallas kernels, call(): pl.pallas_call(kernel, out_shape=out_shape, in_specs=[pl.BlockSpec(memory...  35.5 us
    ppermute x18, starting transfers between devices, ring_shift(): return lax.ppermute(x, RING, pairs)  31.2 us
    ppermute x18, waiting for transfers between devices, ring_shift(): return lax.ppermute(x, RING, pairs)  22.8 us
    ppermute x4, starting transfers between devices, shifted(): return lax.ppermute(x, LINE, pairs)  17.2 us
    ppermute x4, waiting for transfers between devices, shifted(): return lax.ppermute(x, LINE, pairs)  5.57 us
    unnamed x10, local copies, waits for them, and re-layouts  3.32 us
  transfers between devices with their start and end apart: 28, of which 11 were waited for; matrix products, arithmetic and copies ran while one was open for 0% of the time, Pallas kernels for 26%

profile of v5, /device:TPU:6, one launch (start us, length us, event | category | flops | bytes accessed | tf_op | source)
XLA Modules:
  0.0 120.2 jit_solution(8180393977326747786)
XLA Ops:
  1.0 0.1 stack.36.tab
  1.1 1.0 copy-done.2
  2.1 1.0 copy-done.3
  3.2 0.8 pack_kv.1
  4.0 1.7 %collective-permute-start = (bf16[128,1024]{1,0:T(8,128)(2,1)S(1)}, bf16[128,1024]{1,0:T(8,128)(2,1)S(1)}, u32[]{:S(2)}, u32[]{:S(2)}) collective-permute-start(bf16[128,1024]{1,0:T(8,128)(2,1)S(1)} %get-tuple-element.67), channel_id=1, source_target_pairs={{0,4},{1,5},{2,6},{3,7},{4,2},{5,3},{6,0},{7,1},{8,12},{9,13},{10,... | collective-permute-start | bytes 786440 | tf_op jit(solution)/shard_map/ppermute | solution.py:341
  5.6 2.9 %collective-permute-start.1 = (bf16[128,1024]{1,0:T(8,128)(2,1)S(1)}, bf16[128,1024]{1,0:T(8,128)(2,1)S(1)}, u32[]{:S(2)}, u32[]{:S(2)}) collective-permute-start(bf16[128,1024]{1,0:T(8,128)(2,1)S(1)} %get-tuple-element.68), channel_id=1, source_target_pairs={{0,2},{1,3},{2,0},{3,1},{4,6},{5,7},{6,4},{7,5},{8,10},{9,11},{10,... | collective-permute-start | bytes 786440 | tf_op jit(solution)/shard_map/ppermute | solution.py:341
  8.5 1.4 %collective-permute-start.2 = (bf16[128,1024]{1,0:T(8,128)(2,1)S(1)}, bf16[128,1024]{1,0:T(8,128)(2,1)S(1)}, u32[]{:S(2)}, u32[]{:S(2)}) collective-permute-start(bf16[128,1024]{1,0:T(8,128)(2,1)S(1)} %get-tuple-element.69), channel_id=1, source_target_pairs={{0,6},{1,7},{2,4},{3,5},{4,0},{5,1},{6,2},{7,3},{8,14},{9,15},{10,... | collective-permute-start | bytes 786440 | tf_op jit(solution)/shard_map/ppermute | solution.py:341
  9.9 0.1 slice_reduce_fusion
  10.0 0.1 slice_reduce_fusion.1
  10.1 0.1 fusion.3
  10.2 3.2 %collective-permute-done.p1.refs_6_ = bf16[128,1024]{1,0:T(8,128)(2,1)S(1)} collective-permute-done((bf16[128,1024]{1,0:T(8,128)(2,1)S(1)}, bf16[128,1024]{1,0:T(8,128)(2,1)S(1)}, u32[]{:S(2)}, u32[]{:S(2)}) %collective-permute-start) | collective-permute-done | bytes 262176 | tf_op jit(solution)/shard_map/ppermute | solution.py:341
  13.4 1.2 %copy-done.1 = bf16[128,4096]{1,0:T(8,128)(2,1)S(1)} copy-done((bf16[128,4096]{1,0:T(8,128)(2,1)S(1)}, bf16[128,4096]{1,0:T(8,128)(2,1)}, u32[]{:S(2)}) %copy-start.1) | copy-done | bytes 1048600
  14.6 0.8 pack_qd.1
  15.4 4.7 %collective-permute-done.1.p2.refs_7_ = bf16[128,1024]{1,0:T(8,128)(2,1)S(1)} collective-permute-done((bf16[128,1024]{1,0:T(8,128)(2,1)S(1)}, bf16[128,1024]{1,0:T(8,128)(2,1)S(1)}, u32[]{:S(2)}, u32[]{:S(2)}) %collective-permute-start.1) | collective-permute-done | bytes 262176 | tf_op jit(solution)/shard_map/ppermute | solution.py:341
  20.2 0.6 to_sibling_in.3
  20.8 0.1 collective-permute-start.3
  20.9 1.9 %collective-permute-done.3.sib.refs_9_ = bf16[4,128,512]{2,1,0:T(8,128)(2,1)S(1)} collective-permute-done((bf16[4,128,512]{2,1,0:T(8,128)(2,1)S(1)}, bf16[4,128,512]{2,1,0:T(8,128)(2,1)S(1)}, u32[]{:S(2)}, u32[]{:S(2)}) %collective-permute-start.3) | collective-permute-done | bytes 524320 | tf_op jit(solution)/shard_map/ppermute | solution.py:357
  22.8 0.6 halo.1
  23.4 1.3 %collective-permute-start.4 = (bf16[128,1024]{1,0:T(8,128)(2,1)S(1)}, bf16[128,1024]{1,0:T(8,128)(2,1)S(1)}, u32[]{:S(2)}, u32[]{:S(2)}) collective-permute-start(bf16[128,1024]{1,0:T(8,128)(2,1)S(1)} %get-tuple-element.87), channel_id=1, source_target_pairs={{0,4},{1,5},{2,6},{3,7},{4,2},{5,3},{6,0},{7,1},{8,12},{9,13},{10,... | collective-permute-start | bytes 786440 | tf_op jit(solution)/shard_map/ppermute | solution.py:341
  24.7 2.4 %collective-permute-start.5 = (bf16[128,1024]{1,0:T(8,128)(2,1)S(1)}, bf16[128,1024]{1,0:T(8,128)(2,1)S(1)}, u32[]{:S(2)}, u32[]{:S(2)}) collective-permute-start(bf16[128,1024]{1,0:T(8,128)(2,1)S(1)} %get-tuple-element.88), channel_id=1, source_target_pairs={{0,2},{1,3},{2,0},{3,1},{4,6},{5,7},{6,4},{7,5},{8,10},{9,11},{10,... | collective-permute-start | bytes 786440 | tf_op jit(solution)/shard_map/ppermute | solution.py:341
  27.1 1.8 %collective-permute-start.6 = (bf16[128,1024]{1,0:T(8,128)(2,1)S(1)}, bf16[128,1024]{1,0:T(8,128)(2,1)S(1)}, u32[]{:S(2)}, u32[]{:S(2)}) collective-permute-start(bf16[128,1024]{1,0:T(8,128)(2,1)S(1)} %get-tuple-element.89), channel_id=1, source_target_pairs={{0,6},{1,7},{2,4},{3,5},{4,0},{5,1},{6,2},{7,3},{8,14},{9,15},{10,... | collective-permute-start | bytes 786440 | tf_op jit(solution)/shard_map/ppermute | solution.py:341
  28.9 3.8 %collective-permute-start.8 = (bf16[8,128,256]{2,1,0:T(8,128)(2,1)S(1)}, bf16[8,128,256]{2,1,0:T(8,128)(2,1)S(1)}, u32[]{:S(2)}, u32[]{:S(2)}) collective-permute-start(bf16[8,128,256]{2,1,0:T(8,128)(2,1)S(1)} %get-tuple-element.84), channel_id=1, source_target_pairs={{0,8},{8,16},{16,24},{24,32},{32,40},{40,48},{48,56},{56,64},{64,7... | collective-permute-start | bytes 1572872 | tf_op jit(solution)/shard_map/ppermute | solution.py:363
  32.7 0.7 collective-permute-done.4.p1.refs_1_
  33.4 5.6 %collective-permute-done.5.p2.refs_2_ = bf16[128,1024]{1,0:T(8,128)(2,1)S(1)} collective-permute-done((bf16[128,1024]{1,0:T(8,128)(2,1)S(1)}, bf16[128,1024]{1,0:T(8,128)(2,1)S(1)}, u32[]{:S(2)}, u32[]{:S(2)}) %collective-permute-start.5) | collective-permute-done | bytes 262176 | tf_op jit(solution)/shard_map/ppermute | solution.py:341
  39.0 0.2 collective-permute-done.6.p3.refs_3_
  39.3 0.6 to_sibling_in.4
  39.9 0.1 collective-permute-start.7
  40.0 3.8 %collective-permute-start.16 = (bf16[8,128,256]{2,1,0:T(8,128)(2,1)S(1)}, bf16[8,128,256]{2,1,0:T(8,128)(2,1)S(1)}, u32[]{:S(2)}, u32[]{:S(2)}) collective-permute-start(bf16[8,128,256]{2,1,0:T(8,128)(2,1)S(1)} %get-tuple-element.85), channel_id=1, source_target_pairs={{0,8},{8,16},{16,24},{24,32},{32,40},{40,48},{48,56},{56,64},{64,7... | collective-permute-start | bytes 1572872 | tf_op jit(solution)/shard_map/ppermute | solution.py:363
  43.8 1.8 %collective-permute-start.12 = (bf16[128,1024]{1,0:T(8,128)(2,1)S(1)}, bf16[128,1024]{1,0:T(8,128)(2,1)S(1)}, u32[]{:S(2)}, u32[]{:S(2)}) collective-permute-start(bf16[128,1024]{1,0:T(8,128)(2,1)S(1)} %get-tuple-element.95), channel_id=1, source_target_pairs={{0,4},{1,5},{2,6},{3,7},{4,2},{5,3},{6,0},{7,1},{8,12},{9,13},{10,... | collective-permute-start | bytes 786440 | tf_op jit(solution)/shard_map/ppermute | solution.py:341
  45.6 2.4 %collective-permute-start.13 = (bf16[128,1024]{1,0:T(8,128)(2,1)S(1)}, bf16[128,1024]{1,0:T(8,128)(2,1)S(1)}, u32[]{:S(2)}, u32[]{:S(2)}) collective-permute-start(bf16[128,1024]{1,0:T(8,128)(2,1)S(1)} %get-tuple-element.96), channel_id=1, source_target_pairs={{0,2},{1,3},{2,0},{3,1},{4,6},{5,7},{6,4},{7,5},{8,10},{9,11},{10,... | collective-permute-start | bytes 786440 | tf_op jit(solution)/shard_map/ppermute | solution.py:341
  48.0 0.4 collective-permute-done.8.refs_10_
  48.3 1.0 collective-permute-start.14
  49.3 0.0 collective-permute-done.7.refs_4_
  49.3 12.5 %attend_0.1 = (bf16[256,512]{1,0:T(8,128)(2,1)S(1)}, bf16[256,512]{1,0:T(8,128)(2,1)S(1)}, bf16[256,512]{1,0:T(8,128)(2,1)S(1)}, bf16[256,512]{1,0:T(8,128)(2,1)...) custom-call(s32[9]{0:T(128)S(1)} %stack.36.tab, f32[8,128]{1,0:T(8,128)S(1)} %pad.5.bias_ref, ...), custom_call_target="tpu_custom_call" | custom-call | flops 14000000000 | bytes 4194304 | tf_op jit(solution)/shard_map/attend_0/pallas_call | solution.py:47
  61.9 0.0 collective-permute-done.13.p2.refs_2_
  61.9 0.0 collective-permute-done.14.p3.refs_3_
  61.9 0.6 to_sibling_in.5
  62.5 0.1 collective-permute-start.15
  62.6 1.1 collective-permute-start.9
  63.7 0.9 collective-permute-start.10
  64.6 2.0 %collective-permute-start.11 = (bf16[256,512]{1,0:T(8,128)(2,1)S(1)}, bf16[256,512]{1,0:T(8,128)(2,1)S(1)}, u32[]{:S(2)}, u32[]{:S(2)}) collective-permute-start(bf16[256,512]{1,0:T(8,128)(2,1)S(1)} %get-tuple-element.93), channel_id=1, source_target_pairs={{0,6},{1,7},{2,4},{3,5},{4,0},{5,1},{6,2},{7,3},{8,14},{9,15},{10,... | collective-permute-start | bytes 786440 | tf_op jit(solution)/shard_map/ppermute | solution.py:341
  66.6 0.0 collective-permute-done.16.refs_10_
  66.6 5.8 %collective-permute-start.22 = (bf16[1024,256]{1,0:T(8,128)(2,1)S(1)}, bf16[1024,256]{1,0:T(8,128)(2,1)S(1)}, u32[]{:S(2)}, u32[]{:S(2)}) collective-permute-start(bf16[1024,256]{1,0:T(8,128)(2,1)S(1)} %get-tuple-element.120), channel_id=1, source_target_pairs={{8,0},{16,8},{24,16},{32,24},{40,32},{48,40},{56,48},{64,56},{72,6... | collective-permute-start | bytes 1572872 | tf_op jit(solution)/shard_map/ppermute | solution.py:363
  72.4 12.6 %attend_1.1 = (bf16[256,512]{1,0:T(8,128)(2,1)S(1)}, bf16[256,512]{1,0:T(8,128)(2,1)S(1)}, bf16[256,512]{1,0:T(8,128)(2,1)S(1)}, bf16[256,512]{1,0:T(8,128)(2,1)...) custom-call(s32[9]{0:T(128)S(1)} %stack.36.tab, f32[8,128]{1,0:T(8,128)S(1)} %pad.5.bias_ref, ...), custom_call_target="tpu_custom_call" | custom-call | flops 14000000000 | bytes 4194304 | tf_op jit(solution)/shard_map/attend_1/pallas_call | solution.py:47
  84.9 3.8 %collective-permute-start.23 = (bf16[1024,256]{1,0:T(8,128)(2,1)S(1)}, bf16[1024,256]{1,0:T(8,128)(2,1)S(1)}, u32[]{:S(2)}, u32[]{:S(2)}) collective-permute-start(bf16[1024,256]{1,0:T(8,128)(2,1)S(1)} %get-tuple-element.121), channel_id=1, source_target_pairs={{8,0},{16,8},{24,16},{32,24},{40,32},{48,40},{56,48},{64,56},{72,6... | collective-permute-start | bytes 1572872 | tf_op jit(solution)/shard_map/ppermute | solution.py:363
  88.7 0.0 collective-permute-done.9.p1.refs_1_
  88.8 0.6 to_sibling_out.3
  89.4 0.8 collective-permute-start.18
  90.1 2.2 %collective-permute-start.19 = (bf16[256,512]{1,0:T(8,128)(2,1)S(1)}, bf16[256,512]{1,0:T(8,128)(2,1)S(1)}, u32[]{:S(2)}, u32[]{:S(2)}) collective-permute-start(bf16[256,512]{1,0:T(8,128)(2,1)S(1)} %get-tuple-element.114), channel_id=1, source_target_pairs={{0,2},{1,3},{2,0},{3,1},{4,6},{5,7},{6,4},{7,5},{8,10},{9,11},{10,... | collective-permute-start | bytes 786440 | tf_op jit(solution)/shard_map/ppermute | solution.py:341
  92.3 2.5 %collective-permute-start.20 = (bf16[256,512]{1,0:T(8,128)(2,1)S(1)}, bf16[256,512]{1,0:T(8,128)(2,1)S(1)}, u32[]{:S(2)}, u32[]{:S(2)}) collective-permute-start(bf16[256,512]{1,0:T(8,128)(2,1)S(1)} %get-tuple-element.115), channel_id=1, source_target_pairs={{0,6},{1,7},{2,4},{3,5},{4,0},{5,1},{6,2},{7,3},{8,14},{9,15},{10,... | collective-permute-start | bytes 786440 | tf_op jit(solution)/shard_map/ppermute | solution.py:341
  94.8 5.2 %collective-permute-done.23.from1 = bf16[1024,256]{1,0:T(8,128)(2,1)S(1)} collective-permute-done((bf16[1024,256]{1,0:T(8,128)(2,1)S(1)}, bf16[1024,256]{1,0:T(8,128)(2,1)S(1)}, u32[]{:S(2)}, u32[]{:S(2)}) %collective-permute-start.23) | collective-permute-done | bytes 524320 | tf_op jit(solution)/shard_map/ppermute | solution.py:363
  100.0 0.8 merge.1
  100.8 0.8 collective-permute-start.24
  101.6 1.9 %collective-permute-start.25 = (bf16[256,512]{1,0:T(8,128)(2,1)S(1)}, bf16[256,512]{1,0:T(8,128)(2,1)S(1)}, u32[]{:S(2)}, u32[]{:S(2)}) collective-permute-start(bf16[256,512]{1,0:T(8,128)(2,1)S(1)} %get-tuple-element.124), channel_id=1, source_target_pairs={{0,2},{1,3},{2,0},{3,1},{4,6},{5,7},{6,4},{7,5},{8,10},{9,11},{10,... | collective-permute-start | bytes 786440 | tf_op jit(solution)/shard_map/ppermute | solution.py:341
  103.5 0.1 collective-permute-done.18.p1.refs_6_
  103.6 2.5 %collective-permute-start.26 = (bf16[256,512]{1,0:T(8,128)(2,1)S(1)}, bf16[256,512]{1,0:T(8,128)(2,1)S(1)}, u32[]{:S(2)}, u32[]{:S(2)}) collective-permute-start(bf16[256,512]{1,0:T(8,128)(2,1)S(1)} %get-tuple-element.125), channel_id=1, source_target_pairs={{0,6},{1,7},{2,4},{3,5},{4,0},{5,1},{6,2},{7,3},{8,14},{9,15},{10,... | collective-permute-start | bytes 786440 | tf_op jit(solution)/shard_map/ppermute | solution.py:341
  106.1 0.6 to_sibling_out.4
  106.7 0.6 collective-permute-start.21
  107.2 7.7 %collective-permute-done.24.p1 = bf16[256,512]{1,0:T(8,128)(2,1)S(1)} collective-permute-done((bf16[256,512]{1,0:T(8,128)(2,1)S(1)}, bf16[256,512]{1,0:T(8,128)(2,1)S(1)}, u32[]{:S(2)}, u32[]{:S(2)}) %collective-permute-start.24) | collective-permute-done | bytes 262176 | tf_op jit(solution)/shard_map/ppermute | solution.py:341
  114.9 0.7 collective-permute-done.26.p3
  115.6 0.6 to_sibling_out.5
  116.2 0.1 collective-permute-start.27
  116.3 2.1 %unpack_out.1 = (bf16[128,4096]{1,0:T(8,128)(2,1)}, bf16[128,4096]{1,0:T(8,128)(2,1)}) custom-call(s32[9]{0:T(128)S(1)} %stack.36.tab, bf16[256,512]{1,0:T(8,128)(2,1)S(1)} %get-tuple-element.104.p0.refs_0_, bf16[256,512]{1,0:T(8,128)(2,1)S(1)} %collective-permute-done.9.p1.refs_1_, bf16[256,512]{1,0:T(8,128)(2,1)S(1)} %collective-permute-done.10.p2.refs_2_, ...), custom_call_target="tpu_custom_call" | custom-call | bytes 4194304 | tf_op jit(solution)/shard_map/unpack_out/pallas_call | solution.py:47
  118.4 1.8 %unpack_kv.1 = (bf16[128,2048]{1,0:T(8,128)(2,1)}, bf16[128,2048]{1,0:T(8,128)(2,1)}) custom-call(s32[9]{0:T(128)S(1)} %stack.36.tab, bf16[256,512]{1,0:T(8,128)(2,1)S(1)} %get-tuple-element.122.p0, bf16[256,512]{1,0:T(8,128)(2,1)S(1)} %collective-permute-done.24.p1, bf16[256,512]{1,0:T(8,128)(2,1)S(1)} %collective-permute-done.25.p2, ...), custom_call_target="tpu_custom_call" | custom-call | bytes 2097152 | tf_op jit(solution)/shard_map/unpack_kv/pallas_call | solution.py:47
  (23 shorter events, 0.1 us)
Async XLA Ops:
  0.6 12.7 %copy-start = (bf16[128,4096]{1,0:T(8,128)(2,1)S(1)}, bf16[128,4096]{1,0:T(8,128)(2,1)}, u32[]{:S(2)}) copy-start(bf16[128,4096]{1,0:T(8,128)(2,1)} %q_ref) | copy-start | bytes 3145732
  1.1 1.0 copy-start.2
  2.1 1.0 copy-start.3
  3.2 6.7 %copy-start.4 = (s32[32768]{0:T(1024)S(1)}, s32[32768]{0:T(1024)}, u32[]{:S(2)}) copy-start(s32[32768]{0:T(1024)} %param.9) | copy-start | bytes 393220
  4.0 9.4 %collective-permute-start = (bf16[128,1024]{1,0:T(8,128)(2,1)S(1)}, bf16[128,1024]{1,0:T(8,128)(2,1)S(1)}, u32[]{:S(2)}, u32[]{:S(2)}) collective-permute-start(bf16[128,1024]{1,0:T(8,128)(2,1)S(1)} %get-tuple-element.67), channel_id=1, source_target_pairs={{0,4},{1,5},{2,6},{3,7},{4,2},{5,3},{6,0},{7,1},{8,12},{9,13},{10,... | collective-permute-start | bytes 786440 | tf_op jit(solution)/shard_map/ppermute | solution.py:341
  5.6 14.5 %collective-permute-start.1 = (bf16[128,1024]{1,0:T(8,128)(2,1)S(1)}, bf16[128,1024]{1,0:T(8,128)(2,1)S(1)}, u32[]{:S(2)}, u32[]{:S(2)}) collective-permute-start(bf16[128,1024]{1,0:T(8,128)(2,1)S(1)} %get-tuple-element.68), channel_id=1, source_target_pairs={{0,2},{1,3},{2,0},{3,1},{4,6},{5,7},{6,4},{7,5},{8,10},{9,11},{10,... | collective-permute-start | bytes 786440 | tf_op jit(solution)/shard_map/ppermute | solution.py:341
  8.5 11.6 %collective-permute-start.2 = (bf16[128,1024]{1,0:T(8,128)(2,1)S(1)}, bf16[128,1024]{1,0:T(8,128)(2,1)S(1)}, u32[]{:S(2)}, u32[]{:S(2)}) collective-permute-start(bf16[128,1024]{1,0:T(8,128)(2,1)S(1)} %get-tuple-element.69), channel_id=1, source_target_pairs={{0,6},{1,7},{2,4},{3,5},{4,0},{5,1},{6,2},{7,3},{8,14},{9,15},{10,... | collective-permute-start | bytes 786440 | tf_op jit(solution)/shard_map/ppermute | solution.py:341
  13.4 1.2 %copy-start.1 = (bf16[128,4096]{1,0:T(8,128)(2,1)S(1)}, bf16[128,4096]{1,0:T(8,128)(2,1)}, u32[]{:S(2)}) copy-start(bf16[128,4096]{1,0:T(8,128)(2,1)} %d_ref.1) | copy-start | bytes 3145732
  20.8 2.0 %collective-permute-start.3 = (bf16[4,128,512]{2,1,0:T(8,128)(2,1)S(1)}, bf16[4,128,512]{2,1,0:T(8,128)(2,1)S(1)}, u32[]{:S(2)}, u32[]{:S(2)}) collective-permute-start(bf16[4,128,512]{2,1,0:T(8,128)(2,1)S(1)} %to_sibling_in.3), channel_id=1, source_target_pairs={{0,1},{1,0},{2,3},{3,2},{4,5},{5,4},{6,7},{7,6},{8,9},{9,8},{10,11... | collective-permute-start | bytes 1572872 | tf_op jit(solution)/shard_map/ppermute | solution.py:357
  23.4 10.0 %collective-permute-start.4 = (bf16[128,1024]{1,0:T(8,128)(2,1)S(1)}, bf16[128,1024]{1,0:T(8,128)(2,1)S(1)}, u32[]{:S(2)}, u32[]{:S(2)}) collective-permute-start(bf16[128,1024]{1,0:T(8,128)(2,1)S(1)} %get-tuple-element.87), channel_id=1, source_target_pairs={{0,4},{1,5},{2,6},{3,7},{4,2},{5,3},{6,0},{7,1},{8,12},{9,13},{10,... | collective-permute-start | bytes 786440 | tf_op jit(solution)/shard_map/ppermute | solution.py:341
  24.7 14.3 %collective-permute-start.5 = (bf16[128,1024]{1,0:T(8,128)(2,1)S(1)}, bf16[128,1024]{1,0:T(8,128)(2,1)S(1)}, u32[]{:S(2)}, u32[]{:S(2)}) collective-permute-start(bf16[128,1024]{1,0:T(8,128)(2,1)S(1)} %get-tuple-element.88), channel_id=1, source_target_pairs={{0,2},{1,3},{2,0},{3,1},{4,6},{5,7},{6,4},{7,5},{8,10},{9,11},{10,... | collective-permute-start | bytes 786440 | tf_op jit(solution)/shard_map/ppermute | solution.py:341
  27.1 12.2 %collective-permute-start.6 = (bf16[128,1024]{1,0:T(8,128)(2,1)S(1)}, bf16[128,1024]{1,0:T(8,128)(2,1)S(1)}, u32[]{:S(2)}, u32[]{:S(2)}) collective-permute-start(bf16[128,1024]{1,0:T(8,128)(2,1)S(1)} %get-tuple-element.89), channel_id=1, source_target_pairs={{0,6},{1,7},{2,4},{3,5},{4,0},{5,1},{6,2},{7,3},{8,14},{9,15},{10,... | collective-permute-start | bytes 786440 | tf_op jit(solution)/shard_map/ppermute | solution.py:341
  28.9 19.4 %collective-permute-start.8 = (bf16[8,128,256]{2,1,0:T(8,128)(2,1)S(1)}, bf16[8,128,256]{2,1,0:T(8,128)(2,1)S(1)}, u32[]{:S(2)}, u32[]{:S(2)}) collective-permute-start(bf16[8,128,256]{2,1,0:T(8,128)(2,1)S(1)} %get-tuple-element.84), channel_id=1, source_target_pairs={{0,8},{8,16},{16,24},{24,32},{32,40},{40,48},{48,56},{56,64},{64,7... | collective-permute-start | bytes 1572872 | tf_op jit(solution)/shard_map/ppermute | solution.py:363
  39.9 9.5 %collective-permute-start.7 = (bf16[4,128,512]{2,1,0:T(8,128)(2,1)S(1)}, bf16[4,128,512]{2,1,0:T(8,128)(2,1)S(1)}, u32[]{:S(2)}, u32[]{:S(2)}) collective-permute-start(bf16[4,128,512]{2,1,0:T(8,128)(2,1)S(1)} %to_sibling_in.4), channel_id=1, source_target_pairs={{0,1},{1,0},{2,3},{3,2},{4,5},{5,4},{6,7},{7,6},{8,9},{9,8},{10,11... | collective-permute-start | bytes 1572872 | tf_op jit(solution)/shard_map/ppermute | solution.py:357
  40.0 26.6 %collective-permute-start.16 = (bf16[8,128,256]{2,1,0:T(8,128)(2,1)S(1)}, bf16[8,128,256]{2,1,0:T(8,128)(2,1)S(1)}, u32[]{:S(2)}, u32[]{:S(2)}) collective-permute-start(bf16[8,128,256]{2,1,0:T(8,128)(2,1)S(1)} %get-tuple-element.85), channel_id=1, source_target_pairs={{0,8},{8,16},{16,24},{24,32},{32,40},{40,48},{48,56},{56,64},{64,7... | collective-permute-start | bytes 1572872 | tf_op jit(solution)/shard_map/ppermute | solution.py:363
  43.8 18.1 %collective-permute-start.12 = (bf16[128,1024]{1,0:T(8,128)(2,1)S(1)}, bf16[128,1024]{1,0:T(8,128)(2,1)S(1)}, u32[]{:S(2)}, u32[]{:S(2)}) collective-permute-start(bf16[128,1024]{1,0:T(8,128)(2,1)S(1)} %get-tuple-element.95), channel_id=1, source_target_pairs={{0,4},{1,5},{2,6},{3,7},{4,2},{5,3},{6,0},{7,1},{8,12},{9,13},{10,... | collective-permute-start | bytes 786440 | tf_op jit(solution)/shard_map/ppermute | solution.py:341
  45.6 16.3 %collective-permute-start.13 = (bf16[128,1024]{1,0:T(8,128)(2,1)S(1)}, bf16[128,1024]{1,0:T(8,128)(2,1)S(1)}, u32[]{:S(2)}, u32[]{:S(2)}) collective-permute-start(bf16[128,1024]{1,0:T(8,128)(2,1)S(1)} %get-tuple-element.96), channel_id=1, source_target_pairs={{0,2},{1,3},{2,0},{3,1},{4,6},{5,7},{6,4},{7,5},{8,10},{9,11},{10,... | collective-permute-start | bytes 786440 | tf_op jit(solution)/shard_map/ppermute | solution.py:341
  48.3 13.6 %collective-permute-start.14 = (bf16[128,1024]{1,0:T(8,128)(2,1)S(1)}, bf16[128,1024]{1,0:T(8,128)(2,1)S(1)}, u32[]{:S(2)}, u32[]{:S(2)}) collective-permute-start(bf16[128,1024]{1,0:T(8,128)(2,1)S(1)} %get-tuple-element.97), channel_id=1, source_target_pairs={{0,6},{1,7},{2,4},{3,5},{4,0},{5,1},{6,2},{7,3},{8,14},{9,15},{10,... | collective-permute-start | bytes 786440 | tf_op jit(solution)/shard_map/ppermute | solution.py:341
  62.5 9.9 %collective-permute-start.15 = (bf16[4,128,512]{2,1,0:T(8,128)(2,1)S(1)}, bf16[4,128,512]{2,1,0:T(8,128)(2,1)S(1)}, u32[]{:S(2)}, u32[]{:S(2)}) collective-permute-start(bf16[4,128,512]{2,1,0:T(8,128)(2,1)S(1)} %to_sibling_in.5), channel_id=1, source_target_pairs={{0,1},{1,0},{2,3},{3,2},{4,5},{5,4},{6,7},{7,6},{8,9},{9,8},{10,11... | collective-permute-start | bytes 1572872 | tf_op jit(solution)/shard_map/ppermute | solution.py:357
  62.6 26.2 %collective-permute-start.9 = (bf16[256,512]{1,0:T(8,128)(2,1)S(1)}, bf16[256,512]{1,0:T(8,128)(2,1)S(1)}, u32[]{:S(2)}, u32[]{:S(2)}) collective-permute-start(bf16[256,512]{1,0:T(8,128)(2,1)S(1)} %get-tuple-element.91), channel_id=1, source_target_pairs={{0,4},{1,5},{2,6},{3,7},{4,2},{5,3},{6,0},{7,1},{8,12},{9,13},{10,... | collective-permute-start | bytes 786440 | tf_op jit(solution)/shard_map/ppermute | solution.py:341
  63.7 25.1 %collective-permute-start.10 = (bf16[256,512]{1,0:T(8,128)(2,1)S(1)}, bf16[256,512]{1,0:T(8,128)(2,1)S(1)}, u32[]{:S(2)}, u32[]{:S(2)}) collective-permute-start(bf16[256,512]{1,0:T(8,128)(2,1)S(1)} %get-tuple-element.92), channel_id=1, source_target_pairs={{0,2},{1,3},{2,0},{3,1},{4,6},{5,7},{6,4},{7,5},{8,10},{9,11},{10,... | collective-permute-start | bytes 786440 | tf_op jit(solution)/shard_map/ppermute | solution.py:341
  64.6 24.2 %collective-permute-start.11 = (bf16[256,512]{1,0:T(8,128)(2,1)S(1)}, bf16[256,512]{1,0:T(8,128)(2,1)S(1)}, u32[]{:S(2)}, u32[]{:S(2)}) collective-permute-start(bf16[256,512]{1,0:T(8,128)(2,1)S(1)} %get-tuple-element.93), channel_id=1, source_target_pairs={{0,6},{1,7},{2,4},{3,5},{4,0},{5,1},{6,2},{7,3},{8,14},{9,15},{10,... | collective-permute-start | bytes 786440 | tf_op jit(solution)/shard_map/ppermute | solution.py:341
  66.6 28.2 %collective-permute-start.22 = (bf16[1024,256]{1,0:T(8,128)(2,1)S(1)}, bf16[1024,256]{1,0:T(8,128)(2,1)S(1)}, u32[]{:S(2)}, u32[]{:S(2)}) collective-permute-start(bf16[1024,256]{1,0:T(8,128)(2,1)S(1)} %get-tuple-element.120), channel_id=1, source_target_pairs={{8,0},{16,8},{24,16},{32,24},{40,32},{48,40},{56,48},{64,56},{72,6... | collective-permute-start | bytes 1572872 | tf_op jit(solution)/shard_map/ppermute | solution.py:363
  84.9 15.1 %collective-permute-start.23 = (bf16[1024,256]{1,0:T(8,128)(2,1)S(1)}, bf16[1024,256]{1,0:T(8,128)(2,1)S(1)}, u32[]{:S(2)}, u32[]{:S(2)}) collective-permute-start(bf16[1024,256]{1,0:T(8,128)(2,1)S(1)} %get-tuple-element.121), channel_id=1, source_target_pairs={{8,0},{16,8},{24,16},{32,24},{40,32},{48,40},{56,48},{64,56},{72,6... | collective-permute-start | bytes 1572872 | tf_op jit(solution)/shard_map/ppermute | solution.py:363
  89.4 14.2 %collective-permute-start.18 = (bf16[256,512]{1,0:T(8,128)(2,1)S(1)}, bf16[256,512]{1,0:T(8,128)(2,1)S(1)}, u32[]{:S(2)}, u32[]{:S(2)}) collective-permute-start(bf16[256,512]{1,0:T(8,128)(2,1)S(1)} %get-tuple-element.113), channel_id=1, source_target_pairs={{0,4},{1,5},{2,6},{3,7},{4,2},{5,3},{6,0},{7,1},{8,12},{9,13},{10,... | collective-permute-start | bytes 786440 | tf_op jit(solution)/shard_map/ppermute | solution.py:341
  90.1 15.9 %collective-permute-start.19 = (bf16[256,512]{1,0:T(8,128)(2,1)S(1)}, bf16[256,512]{1,0:T(8,128)(2,1)S(1)}, u32[]{:S(2)}, u32[]{:S(2)}) collective-permute-start(bf16[256,512]{1,0:T(8,128)(2,1)S(1)} %get-tuple-element.114), channel_id=1, source_target_pairs={{0,2},{1,3},{2,0},{3,1},{4,6},{5,7},{6,4},{7,5},{8,10},{9,11},{10,... | collective-permute-start | bytes 786440 | tf_op jit(solution)/shard_map/ppermute | solution.py:341
  92.3 13.8 %collective-permute-start.20 = (bf16[256,512]{1,0:T(8,128)(2,1)S(1)}, bf16[256,512]{1,0:T(8,128)(2,1)S(1)}, u32[]{:S(2)}, u32[]{:S(2)}) collective-permute-start(bf16[256,512]{1,0:T(8,128)(2,1)S(1)} %get-tuple-element.115), channel_id=1, source_target_pairs={{0,6},{1,7},{2,4},{3,5},{4,0},{5,1},{6,2},{7,3},{8,14},{9,15},{10,... | collective-permute-start | bytes 786440 | tf_op jit(solution)/shard_map/ppermute | solution.py:341
  100.8 14.1 %collective-permute-start.24 = (bf16[256,512]{1,0:T(8,128)(2,1)S(1)}, bf16[256,512]{1,0:T(8,128)(2,1)S(1)}, u32[]{:S(2)}, u32[]{:S(2)}) collective-permute-start(bf16[256,512]{1,0:T(8,128)(2,1)S(1)} %get-tuple-element.123), channel_id=1, source_target_pairs={{0,4},{1,5},{2,6},{3,7},{4,2},{5,3},{6,0},{7,1},{8,12},{9,13},{10,... | collective-permute-start | bytes 786440 | tf_op jit(solution)/shard_map/ppermute | solution.py:341
  101.6 13.3 %collective-permute-start.25 = (bf16[256,512]{1,0:T(8,128)(2,1)S(1)}, bf16[256,512]{1,0:T(8,128)(2,1)S(1)}, u32[]{:S(2)}, u32[]{:S(2)}) collective-permute-start(bf16[256,512]{1,0:T(8,128)(2,1)S(1)} %get-tuple-element.124), channel_id=1, source_target_pairs={{0,2},{1,3},{2,0},{3,1},{4,6},{5,7},{6,4},{7,5},{8,10},{9,11},{10,... | collective-permute-start | bytes 786440 | tf_op jit(solution)/shard_map/ppermute | solution.py:341
  103.6 12.0 %collective-permute-start.26 = (bf16[256,512]{1,0:T(8,128)(2,1)S(1)}, bf16[256,512]{1,0:T(8,128)(2,1)S(1)}, u32[]{:S(2)}, u32[]{:S(2)}) collective-permute-start(bf16[256,512]{1,0:T(8,128)(2,1)S(1)} %get-tuple-element.125), channel_id=1, source_target_pairs={{0,6},{1,7},{2,4},{3,5},{4,0},{5,1},{6,2},{7,3},{8,14},{9,15},{10,... | collective-permute-start | bytes 786440 | tf_op jit(solution)/shard_map/ppermute | solution.py:341
  106.1 10.2 %collective-permute-start.17 = (bf16[4,128,512]{2,1,0:T(8,128)(2,1)S(1)}, bf16[4,128,512]{2,1,0:T(8,128)(2,1)S(1)}, u32[]{:S(2)}, u32[]{:S(2)}) collective-permute-start(bf16[4,128,512]{2,1,0:T(8,128)(2,1)S(1)} %to_sibling_out.3), channel_id=1, source_target_pairs={{0,1},{1,0},{2,3},{3,2},{4,5},{5,4},{6,7},{7,6},{8,9},{9,8},{10,11... | collective-permute-start | bytes 1572872 | tf_op jit(solution)/shard_map/ppermute | solution.py:357
  106.7 9.6 %collective-permute-start.21 = (bf16[4,128,512]{2,1,0:T(8,128)(2,1)S(1)}, bf16[4,128,512]{2,1,0:T(8,128)(2,1)S(1)}, u32[]{:S(2)}, u32[]{:S(2)}) collective-permute-start(bf16[4,128,512]{2,1,0:T(8,128)(2,1)S(1)} %to_sibling_out.4), channel_id=1, source_target_pairs={{0,1},{1,0},{2,3},{3,2},{4,5},{5,4},{6,7},{7,6},{8,9},{9,8},{10,11... | collective-permute-start | bytes 1572872 | tf_op jit(solution)/shard_map/ppermute | solution.py:357
  116.2 2.2 %collective-permute-start.27 = (bf16[4,128,512]{2,1,0:T(8,128)(2,1)S(1)}, bf16[4,128,512]{2,1,0:T(8,128)(2,1)S(1)}, u32[]{:S(2)}, u32[]{:S(2)}) collective-permute-start(bf16[4,128,512]{2,1,0:T(8,128)(2,1)S(1)} %to_sibling_out.5), channel_id=1, source_target_pairs={{0,1},{1,0},{2,3},{3,2},{4,5},{5,4},{6,7},{7,6},{8,9},{9,8},{10,11... | collective-permute-start | bytes 1572872 | tf_op jit(solution)/shard_map/ppermute | solution.py:357
